TPU v7x, 32 devices: a whole 2x2x4 slice. The times are simulated.
32 devices in a mesh: dp: 4 (over z), seq: 8 (over y, x, core).
Axes of the slice: x: 2, y: 2, z: 4, core: 2. Of those that a mesh axis runs over, the one named last changes fastest.
Arguments:
- tokens: bfloat16 [4, 4096, 256], P('dp', 'seq'), may hold values from -6 to 6
- cotangent: bfloat16 [4, 4096, 256], P('dp', 'seq'), may hold values from -6 to 6
- w_in: bfloat16 [256, 768], replicated, may hold values from -0.375 to 0.375
- w_out: bfloat16 [256, 256], replicated, may hold values from -0.375 to 0.375
- filter_taps: float32 [4096, 256], P('seq'), may hold values from -0.09375 to 0.09375
- skip: float32 [256], replicated, may hold values from -4 to 4
Outputs:
- output: bfloat16 [4, 4096, 256], P('dp', 'seq')
- dinput: bfloat16 [4, 4096, 256], P('dp', 'seq')
- grad_in_proj: float32 [256, 768], P('dp')
- grad_out_proj: float32 [256, 256], P('dp')
- grad_filter: float32 [4096, 256], P('seq', 'dp')
- grad_skip: float32 [256], P('dp')
All inputs are finite; a program needn't handle non-finite values.
Results may differ from a plain program's by a relative error of at most 0.0049.
Values sent between devices are 32-bit elements; how exact they have to be, the bound alone decides.
No kernel may reach another device: no remote copies, remote signals or barrier semaphores. Data moves between devices by JAX's collectives and lax.ppermute only.
A program may use at most 128 MiB of HBM per device.

v0:
```python
import math

import jax
import jax.numpy as jnp
from jax import lax
from jax.sharding import PartitionSpec as P

HIGHEST = lax.Precision.HIGHEST


def regroup_real(signal):
    return lax.all_to_all(signal, "seq", split_axis=1, concat_axis=0, tiled=True)


def regroup_spectral(signal):
    return lax.all_to_all(signal, "seq", split_axis=1, concat_axis=0, tiled=True)


def angles(first_index, second_index, modulus):
    product = first_index[:, None] * second_index[None, :] % modulus
    return 2.0 * math.pi / modulus * product.astype(jnp.float32)


def forward_spectrum(signal):
    tok_rows, chan_count = signal.shape
    seq_parts = lax.axis_size("seq")
    block_rows = tok_rows // seq_parts
    full_length = 2 * seq_parts * tok_rows
    seq_index = lax.axis_index("seq")
    regrouped = regroup_real(signal[None])
    freq_index = jnp.arange(2 * seq_parts, dtype=jnp.int32)
    slot_index = jnp.arange(seq_parts, dtype=jnp.int32)
    outer_angle = angles(freq_index, slot_index, 2 * seq_parts)
    first_re = jnp.einsum("ks,scf->ckf", jnp.cos(outer_angle), regrouped, precision=HIGHEST)
    first_im = jnp.einsum("ks,scf->ckf", -jnp.sin(outer_angle), regrouped, precision=HIGHEST)
    local_pos = seq_index * block_rows + jnp.arange(block_rows, dtype=jnp.int32)
    twiddle = angles(local_pos, freq_index, full_length)[:, :, None]
    tw_cos = jnp.cos(twiddle)
    tw_sin = -jnp.sin(twiddle)
    packed = jnp.concatenate(
        [first_re * tw_cos - first_im * tw_sin, first_re * tw_sin + first_im * tw_cos], axis=2
    )
    spread = regroup_spectral(packed)
    row_index = jnp.arange(tok_rows, dtype=jnp.int32)
    inner_angle = angles(row_index, row_index, tok_rows)
    cos_part = jnp.einsum("kc,cjf->kjf", jnp.cos(inner_angle), spread, precision=HIGHEST)
    sin_part = jnp.einsum("kc,cjf->kjf", -jnp.sin(inner_angle), spread, precision=HIGHEST)
    spectrum = jnp.concatenate(
        [
            cos_part[..., :chan_count] - sin_part[..., chan_count:],
            sin_part[..., :chan_count] + cos_part[..., chan_count:],
        ],
        axis=2,
    )
    return spectrum


def inverse_field(spectrum):
    tok_rows = spectrum.shape[0]
    chan_count = spectrum.shape[2] // 2
    seq_parts = lax.axis_size("seq")
    block_rows = tok_rows // seq_parts
    full_length = 2 * seq_parts * tok_rows
    seq_index = lax.axis_index("seq")
    row_index = jnp.arange(tok_rows, dtype=jnp.int32)
    inner_angle = angles(row_index, row_index, tok_rows)
    cos_part = jnp.einsum("kc,kjf->jcf", jnp.cos(inner_angle), spectrum, precision=HIGHEST)
    sin_part = jnp.einsum("kc,kjf->jcf", jnp.sin(inner_angle), spectrum, precision=HIGHEST)
    packed = jnp.concatenate(
        [
            cos_part[..., :chan_count] - sin_part[..., chan_count:],
            sin_part[..., :chan_count] + cos_part[..., chan_count:],
        ],
        axis=2,
    )
    regrouped = regroup_spectral(packed)
    freq_index = jnp.arange(2 * seq_parts, dtype=jnp.int32)
    slot_index = jnp.arange(seq_parts, dtype=jnp.int32)
    local_pos = seq_index * block_rows + jnp.arange(block_rows, dtype=jnp.int32)
    twiddle = angles(freq_index, local_pos, full_length)[:, :, None]
    tw_cos = jnp.cos(twiddle)
    tw_sin = jnp.sin(twiddle)
    moved_re = regrouped[..., :chan_count]
    moved_im = regrouped[..., chan_count:]
    turned_re = moved_re * tw_cos - moved_im * tw_sin
    turned_im = moved_re * tw_sin + moved_im * tw_cos
    outer_angle = angles(slot_index, freq_index, 2 * seq_parts)
    outer_cos = jnp.cos(outer_angle)
    outer_sin = jnp.sin(outer_angle)
    signal = jnp.einsum("sk,kcf->csf", outer_cos, turned_re, precision=HIGHEST) - jnp.einsum(
        "sk,kcf->csf", outer_sin, turned_im, precision=HIGHEST
    )
    signal = signal * (1.0 / full_length)
    return regroup_real(signal)[:, 0, :]


def invert_real(real_part, imag_part):
    return inverse_field(jnp.concatenate([real_part, imag_part], axis=2))


def shards(tokens, cotangent, w_in, w_out, filter_taps, skip):
    model_width = w_out.shape[0]
    seq_in = tokens[0]
    grad_out = cotangent[0]
    projected = jnp.dot(seq_in, w_in, preferred_element_type=jnp.float32)
    gate_out = projected[:, :model_width]
    gate_in = projected[:, model_width : 2 * model_width]
    values = projected[:, 2 * model_width :]
    gated = values * gate_in
    joint_spec = forward_spectrum(jnp.concatenate([gated, filter_taps], axis=1))
    gated_re = joint_spec[..., :model_width]
    taps_re = joint_spec[..., model_width : 2 * model_width]
    gated_im = joint_spec[..., 2 * model_width : 3 * model_width]
    taps_im = joint_spec[..., 3 * model_width :]
    prod_re = taps_re * gated_re - taps_im * gated_im
    prod_im = taps_re * gated_im + taps_im * gated_re
    conv = invert_real(prod_re, prod_im) + skip * gated
    mixed = (conv * gate_out).astype(jnp.bfloat16)
    output = jnp.dot(mixed, w_out, preferred_element_type=jnp.float32).astype(jnp.bfloat16)
    dmixed = lax.dot_general(
        grad_out, w_out, (((1,), (1,)), ((), ())), preferred_element_type=jnp.float32
    )
    dconv = dmixed * gate_out
    dconv_spec = forward_spectrum(dconv)
    dconv_re = dconv_spec[..., :model_width]
    dconv_im = dconv_spec[..., model_width:]
    taps_corr_re = taps_re * dconv_re + taps_im * dconv_im
    taps_corr_im = taps_re * dconv_im - taps_im * dconv_re
    gated_corr_re = gated_re * dconv_re + gated_im * dconv_im
    gated_corr_im = gated_re * dconv_im - gated_im * dconv_re
    back_field = invert_real(
        jnp.concatenate([taps_corr_re, gated_corr_re], axis=2),
        jnp.concatenate([taps_corr_im, gated_corr_im], axis=2),
    )
    dgated = back_field[:, :model_width] + skip * dconv
    taps_term = back_field[:, model_width:]
    dproj = jnp.concatenate([dmixed * conv, dgated * values, dgated * gate_in], axis=1).astype(
        jnp.bfloat16
    )
    dinput = lax.dot_general(
        dproj, w_in, (((1,), (1,)), ((), ())), preferred_element_type=jnp.float32
    ).astype(jnp.bfloat16)
    token_total = lax.axis_size("dp") * tokens.shape[0] * lax.axis_size("seq") * tokens.shape[1]
    grad_scale = 1.0 / math.sqrt(token_total)
    in_term = (
        lax.dot_general(seq_in, dproj, (((0,), (0,)), ((), ())), preferred_element_type=jnp.float32)
        * grad_scale
    )
    out_term = (
        lax.dot_general(
            mixed, grad_out, (((0,), (0,)), ((), ())), preferred_element_type=jnp.float32
        )
        * grad_scale
    )
    skip_term = jnp.sum(dconv * gated, axis=0) * grad_scale
    taps_term = taps_term * grad_scale
    in_sum, out_sum, skip_sum = lax.psum((in_term, out_term, skip_term), "seq")
    in_part, out_part, skip_part, taps_part = (
        lax.psum_scatter(in_sum, "dp", scatter_dimension=0, tiled=True),
        lax.psum_scatter(out_sum, "dp", scatter_dimension=0, tiled=True),
        lax.psum_scatter(skip_sum, "dp", scatter_dimension=0, tiled=True),
        lax.psum_scatter(taps_term, "dp", scatter_dimension=1, tiled=True),
    )
    return (output[None], dinput[None], in_part, out_part, taps_part, skip_part)


def solution(mesh):
    return jax.shard_map(
        shards,
        mesh=mesh,
        in_specs=(P("dp", "seq", None), P("dp", "seq", None), P(), P(), P("seq", None), P()),
        out_specs=(
            P("dp", "seq", None),
            P("dp", "seq", None),
            P("dp", None),
            P("dp", None),
            P("seq", "dp"),
            P("dp"),
        ),
        check_vma=False,
    )
```

profile of v0, /device:TPU:0, one launch (start us, length us, event | category | flops | bytes accessed | tf_op | source)
XLA Modules:
  0.0 450.9 jit_solution(3059098929109072439)
XLA Ops:
  12.5 5.2 %all-to-all-start.4 = ((f32[1,512,256]{2,0,1:T(1,128)}), f32[1,512,256]{2,0,1:T(1,128)S(1)}, u32[]{:S(2)}, u32[]{:S(2)}) async-start(f32[1,512,256]{2,0,1:T(1,128)} %copy.124), calls=%async_computation.4 | async-start | bytes 1048576 | tf_op jit(solution)/shard_map/all_to_all | solution.py:12
  21.0 6.5 %all-to-all-done.4 = f32[1,512,256]{2,0,1:T(1,128)S(1)} async-done(((f32[1,512,256]{2,0,1:T(1,128)}), f32[1,512,256]{2,0,1:T(1,128)S(1)}, u32[]{:S(2)}, u32[]{:S(2)}) %all-to-all-start.4) | async-done | bytes 524320 | tf_op jit(solution)/shard_map/all_to_all | solution.py:12
  27.4 4.3 all-to-all-start
  37.8 9.3 %all-to-all-done = f32[1,512,512]{2,0,1:T(1,128)} async-done(((f32[1,512,512]{2,0,1:T(1,128)}), f32[1,512,512]{2,0,1:T(1,128)}, u32[]{:S(2)}, u32[]{:S(2)}) %all-to-all-start) | async-done | bytes 1048608 | tf_op jit(solution)/shard_map/all_to_all | solution.py:12
  47.1 4.5 %all-to-all-start.5 = ((f32[64,16,512]{2,0,1:T(8,128)}), f32[64,16,512]{2,0,1:T(8,128)}, u32[]{:S(2)}, u32[]{:S(2)}) async-start(f32[64,16,512]{2,0,1:T(8,128)} %copy.127), calls=%async_computation.5 | async-start | bytes 4194304 | tf_op jit(solution)/shard_map/all_to_all | solution.py:16
  55.4 3.1 subtract_bitcast_fusion
  59.0 4.4 copy.114
  63.4 14.8 %all-to-all-done.5 = f32[64,16,512]{2,0,1:T(8,128)} async-done(((f32[64,16,512]{2,0,1:T(8,128)}), f32[64,16,512]{2,0,1:T(8,128)}, u32[]{:S(2)}, u32[]{:S(2)}) %all-to-all-start.5) | async-done | bytes 2097184 | tf_op jit(solution)/shard_map/all_to_all | solution.py:16
  78.3 4.8 %all-to-all-start.1 = ((f32[64,16,1024]{2,0,1:T(8,128)}), f32[64,16,1024]{2,0,1:T(8,128)}, u32[]{:S(2)}, u32[]{:S(2)}) async-start(f32[64,16,1024]{2,0,1:T(8,128)} %copy.114), calls=%async_computation.1 | async-start | bytes 8388608 | tf_op jit(solution)/shard_map/all_to_all | solution.py:16
  84.9 9.2 %fusion.31 = f32[512,2,512]{2,0,1:T(8,128)} fusion(f32[512,2,512]{2,0,1:T(8,128)S(1)} %bitcast.143), kind=kOutput, calls=%fused_computation.52 | convolution fusion | flops 3225157632 | bytes 4194304 | tf_op jit(solution)/shard_map/kc,cjf->kjf/dot_general | solution.py:47
  94.1 9.5 %fusion.36 = f32[512,2,512]{2,0,1:T(8,128)} fusion(f32[512,2,512]{2,0,1:T(8,128)S(1)} %bitcast.144), kind=kOutput, calls=%fused_computation.57 | convolution fusion | flops 3224895488 | bytes 4194304 | tf_op jit(solution)/shard_map/kc,cjf->kjf/dot_general | solution.py:46
  103.5 28.6 %all-to-all-done.1 = f32[64,16,1024]{2,0,1:T(8,128)} async-done(((f32[64,16,1024]{2,0,1:T(8,128)}), f32[64,16,1024]{2,0,1:T(8,128)}, u32[]{:S(2)}, u32[]{:S(2)}) %all-to-all-start.1) | async-done | bytes 4194336 | tf_op jit(solution)/shard_map/all_to_all | solution.py:16
  134.6 10.9 %fusion.33 = f32[512,2,1024]{2,0,1:T(8,128)S(1)} fusion(f32[512,2,1024]{2,0,1:T(8,128)S(1)} %bitcast.131), kind=kOutput, calls=%fused_computation.54 | convolution fusion | flops 6446383104 | bytes 8388608 | tf_op jit(solution)/shard_map/kc,cjf->kjf/dot_general | solution.py:47
  145.5 11.0 %fusion.39 = f32[512,2,1024]{2,0,1:T(8,128)S(1)} fusion(f32[512,2,1024]{2,0,1:T(8,128)S(1)} %bitcast.132), kind=kOutput, calls=%fused_computation.60 | convolution fusion | flops 6446120960 | bytes 8388608 | tf_op jit(solution)/shard_map/kc,cjf->kjf/dot_general | solution.py:46
  162.5 7.7 %fusion.10 = f32[2,512,512]{1,2,0:T(8,128)S(1)} fusion(f32[512,2,256]{2,0,1:T(8,128)S(1)} %get-tuple-element.55, f32[512,2,256]{2,0,1:T(8,128)S(1)} %get-tuple-element.56), kind=kOutput, calls=%fused_computation.24 | convolution fusion | flops 3225419776 | bytes 4194304 | tf_op jit(solution)/shard_map/kc,kjf->jcf/dot_general | solution.py:67
  170.2 7.6 %fusion.11 = f32[2,512,512]{1,2,0:T(8,128)S(1)} fusion(f32[512,2,256]{2,0,1:T(8,128)S(1)} %get-tuple-element.55, f32[512,2,256]{2,0,1:T(8,128)S(1)} %get-tuple-element.56), kind=kOutput, calls=%fused_computation.25 | convolution fusion | flops 3225419776 | bytes 4194304 | tf_op jit(solution)/shard_map/kc,kjf->jcf/dot_general | solution.py:68
  179.8 4.2 copy.118
  184.0 4.4 all-to-all-start.2
  188.4 13.5 %fusion.2 = f32[2,512,1024]{1,2,0:T(8,128)S(1)} fusion(f32[512,2,256]{2,0,1:T(8,128)} %get-tuple-element.50, f32[512,2,256]{2,0,1:T(8,128)} %get-tuple-element.49, f32[512,2,256]{2,0,1:T(8,128)} %get-tuple-element.48, f32[512,2,256]{2,0,1:T(8,128)} %get-tuple-element.41), kind=kOutput, calls=%fused_computation.5 | convolution fusion | flops 6449266688 | bytes 8388608 | tf_op jit(solution)/shard_map/kc,kjf->jcf/dot_general | solution.py:67
  201.9 11.7 %fusion.3 = f32[2,512,1024]{1,2,0:T(8,128)S(1)} fusion(f32[512,2,256]{2,0,1:T(8,128)S(1)} %copy-done.11, f32[512,2,256]{2,0,1:T(8,128)S(1)} %copy-done.10, f32[512,2,256]{2,0,1:T(8,128)S(1)} %copy-done.9, f32[512,2,256]{2,0,1:T(8,128)S(1)} %copy-done.6), kind=kOutput, calls=%fused_computation.6 | convolution fusion | flops 6449266688 | bytes 8388608 | tf_op jit(solution)/shard_map/kc,kjf->jcf/dot_general | solution.py:68
  217.1 7.4 %copy.137 = f32[2,512,1024]{2,0,1:T(2,128)} copy(f32[2,512,1024]{1,2,0:T(8,128)} %pad_maximum_fusion.2) | data formatting | bytes 8388608 | tf_op jit(solution)/shard_map/concatenate | solution.py:69
  224.4 4.9 %all-to-all-start.6 = ((f32[2,512,1024]{2,0,1:T(2,128)}), f32[2,512,1024]{2,0,1:T(2,128)}, u32[]{:S(2)}, u32[]{:S(2)}) async-start(f32[2,512,1024]{2,0,1:T(2,128)} %copy.137), calls=%async_computation.6 | async-start | bytes 8388608 | tf_op jit(solution)/shard_map/all_to_all | solution.py:16
  235.5 42.9 %all-to-all-done.6 = f32[2,512,1024]{2,0,1:T(2,128)} async-done(((f32[2,512,1024]{2,0,1:T(2,128)}), f32[2,512,1024]{2,0,1:T(2,128)}, u32[]{:S(2)}, u32[]{:S(2)}) %all-to-all-start.6) | async-done | bytes 4194336 | tf_op jit(solution)/shard_map/all_to_all | solution.py:16
  278.4 3.5 all-to-all-start.3
  282.0 3.5 copy.138
  293.2 19.5 %all_to_all.126 = f32[64,8,512]{2,0,1:T(8,128)S(1)} all-to-all(f32[64,8,512]{2,0,1:T(8,128)} %copy.142), channel_id=1, replica_groups=mesh['dp'=4,'seq'=8] {'seq'}, dimensions={1} | all-to-all | bytes 2097152 | tf_op jit(solution)/shard_map/all_to_all | solution.py:12
  318.7 21.6 %reduce-scatter.12.cloned.1.call-done = f32[64,768]{1,0:T(8,128)} async-done(((f32[256,768]{1,0:T(8,128)}), f32[64,768]{1,0:T(8,128)}) %reduce-scatter.12.cloned.1.call-update) | async-done | bytes 196624
  342.1 20.5 %reduce-scatter.8.cloned.1.call-done = f32[64,256]{1,0:T(8,128)} async-done(((f32[256,256]{1,0:T(8,128)}), f32[64,256]{1,0:T(8,128)}) %reduce-scatter.8.cloned.1.call-update) | async-done | bytes 65552 | tf_op jit(solution)/shard_map/reduce_scatter | solution.py:160
  365.0 8.8 %all-reduce = f32[256]{0:T(256)S(1)} all-reduce(f32[256]{0:T(256)S(1)} %broadcast_multiply_fusion), channel_id=5, replica_groups=mesh['dp'=4,'seq'=8] {'dp'}, use_global_device_ids=true, to_apply=%region_7.8.clone | all-reduce | flops 256 | bytes 2048
  373.9 12.3 %psum.26 = f32[64]{0:T(128)} all-reduce(f32[64]{0:T(128)S(1)} %dynamic-slice.1), channel_id=1, replica_groups=mesh['dp'=4,'seq'=8] {'seq'}, use_global_device_ids=true, to_apply=%region_6.7 | all-reduce | flops 64 | bytes 512 | tf_op jit(solution)/shard_map/psum | solution.py:157
  388.2 30.5 %all-reduce.4.cloned.1.call-done = (f32[64,768]{0,1:T(8,128)}, f32[64,256]{1,0:T(8,128)}) async-done(((f32[64,768]{0,1:T(8,128)}, f32[64,256]{1,0:T(8,128)}), (f32[64,768]{0,1:T(8,128)}, f32[64,256]{1,0:T(8,128)})) %all-reduce.4.cloned.1.call-update) | async-done | bytes 262160 | tf_op jit(solution)/shard_map/psum | solution.py:157
  420.6 22.1 %reduce-scatter.10.cloned.1.call-done = f32[64,512]{1,0:T(8,128)} async-done(((f32[256,512]{1,0:T(8,128)}), f32[64,512]{1,0:T(8,128)}) %reduce-scatter.10.cloned.1.call-update) | async-done | bytes 131088
  (115 shorter events, 63.2 us)
Async XLA Ops:
  7.2 2.3 copy-start.7
  12.5 14.9 %all-to-all-start.4 = ((f32[1,512,256]{2,0,1:T(1,128)}), f32[1,512,256]{2,0,1:T(1,128)S(1)}, u32[]{:S(2)}, u32[]{:S(2)}) async-start(f32[1,512,256]{2,0,1:T(1,128)} %copy.124), calls=%async_computation.4 | async-start | bytes 1048576 | tf_op jit(solution)/shard_map/all_to_all | solution.py:12
  21.0 12.3 %copy-start.24 = (s32[64]{0:T(128)}, s32[64]{0:T(128)S(1)}, u32[]{:S(2)}) copy-start(s32[64]{0:T(128)S(1)} %iota_add_fusion) | copy-start | bytes 772
  27.4 19.6 %all-to-all-start = ((f32[1,512,512]{2,0,1:T(1,128)}), f32[1,512,512]{2,0,1:T(1,128)}, u32[]{:S(2)}, u32[]{:S(2)}) async-start(f32[1,512,512]{2,0,1:T(1,128)} %copy.111), calls=%async_computation | async-start | bytes 2097152 | tf_op jit(solution)/shard_map/all_to_all | solution.py:12
  31.9 3.0 copy-start.14
  31.9 3.0 copy-start.16
  47.1 31.2 %all-to-all-start.5 = ((f32[64,16,512]{2,0,1:T(8,128)}), f32[64,16,512]{2,0,1:T(8,128)}, u32[]{:S(2)}, u32[]{:S(2)}) async-start(f32[64,16,512]{2,0,1:T(8,128)} %copy.127), calls=%async_computation.5 | async-start | bytes 4194304 | tf_op jit(solution)/shard_map/all_to_all | solution.py:16
  52.9 2.5 copy-start.15
  52.9 2.5 copy-start.17
  78.3 53.9 %all-to-all-start.1 = ((f32[64,16,1024]{2,0,1:T(8,128)}), f32[64,16,1024]{2,0,1:T(8,128)}, u32[]{:S(2)}, u32[]{:S(2)}) async-start(f32[64,16,1024]{2,0,1:T(8,128)} %copy.114), calls=%async_computation.1 | async-start | bytes 8388608 | tf_op jit(solution)/shard_map/all_to_all | solution.py:16
  184.0 40.5 %all-to-all-start.2 = ((f32[2,512,512]{2,0,1:T(2,128)}), f32[2,512,512]{2,0,1:T(2,128)}, u32[]{:S(2)}, u32[]{:S(2)}) async-start(f32[2,512,512]{2,0,1:T(2,128)} %copy.118), calls=%async_computation.2 | async-start | bytes 4194304 | tf_op jit(solution)/shard_map/all_to_all | solution.py:16
  188.4 13.5 %copy-start.6 = (f32[512,2,256]{2,0,1:T(8,128)S(1)}, f32[512,2,256]{2,0,1:T(8,128)}, u32[]{:S(2)}) copy-start(f32[512,2,256]{2,0,1:T(8,128)} %get-tuple-element.41) | copy-start | bytes 3145732
  188.4 13.5 %copy-start.9 = (f32[512,2,256]{2,0,1:T(8,128)S(1)}, f32[512,2,256]{2,0,1:T(8,128)}, u32[]{:S(2)}) copy-start(f32[512,2,256]{2,0,1:T(8,128)} %get-tuple-element.48) | copy-start | bytes 3145732
  188.4 13.5 %copy-start.10 = (f32[512,2,256]{2,0,1:T(8,128)S(1)}, f32[512,2,256]{2,0,1:T(8,128)}, u32[]{:S(2)}) copy-start(f32[512,2,256]{2,0,1:T(8,128)} %get-tuple-element.49) | copy-start | bytes 3145732
  188.4 13.5 %copy-start.11 = (f32[512,2,256]{2,0,1:T(8,128)S(1)}, f32[512,2,256]{2,0,1:T(8,128)}, u32[]{:S(2)}) copy-start(f32[512,2,256]{2,0,1:T(8,128)} %get-tuple-element.50) | copy-start | bytes 3145732
  224.4 4.9 %copy-start.25 = (s32[64]{0:T(128)S(1)}, s32[64]{0:T(128)}, u32[]{:S(2)}) copy-start(s32[64]{0:T(128)} %copy-done.24) | copy-start | bytes 772
  224.4 54.0 %all-to-all-start.6 = ((f32[2,512,1024]{2,0,1:T(2,128)}), f32[2,512,1024]{2,0,1:T(2,128)}, u32[]{:S(2)}, u32[]{:S(2)}) async-start(f32[2,512,1024]{2,0,1:T(2,128)} %copy.137), calls=%async_computation.6 | async-start | bytes 8388608 | tf_op jit(solution)/shard_map/all_to_all | solution.py:16
  278.4 14.8 %all-to-all-start.3 = ((f32[64,8,256]{2,0,1:T(8,128)}), f32[64,8,256]{2,0,1:T(8,128)S(1)}, u32[]{:S(2)}, u32[]{:S(2)}) async-start(f32[64,8,256]{2,0,1:T(8,128)} %copy.123), calls=%async_computation.3 | async-start | bytes 1048576 | tf_op jit(solution)/shard_map/all_to_all | solution.py:12
  281.9 58.3 %reduce-scatter.12.cloned.1.call-start = ((), (), s32[]{:S(2)}) async-start(), calls=%async_computation.13 | async-start | bytes 983040
  291.5 21.2 %copy-start.26 = (f32[256]{0:T(256)S(1)}, f32[256]{0:T(256)}, u32[]{:S(2)}) copy-start(f32[256]{0:T(256)} %param.11) | copy-start | bytes 3076
  293.2 19.5 %copy-start.4 = (f32[64,8,256]{2,0,1:T(8,128)}, f32[64,8,256]{2,0,1:T(8,128)S(1)}, u32[]{:S(2)}) copy-start(f32[64,8,256]{2,0,1:T(8,128)S(1)} %all-to-all-done.3) | copy-start | bytes 1572868
  293.2 19.5 %copy-start.5 = (f32[512,256]{1,0:T(8,128)S(1)}, f32[512,256]{1,0:T(8,128)}, u32[]{:S(2)}) copy-start(f32[512,256]{1,0:T(8,128)} %get-tuple-element.72) | copy-start | bytes 1572868
  312.7 3.2 copy-start.18
  316.4 46.4 %copy-start.3 = (f32[512,256]{1,0:T(8,128)S(1)}, f32[512,256]{1,0:T(8,128)}, u32[]{:S(2)}) copy-start(f32[512,256]{1,0:T(8,128)} %get-tuple-element.67) | copy-start | bytes 1572868
  317.5 46.2 %copy-start.27 = (u32[32]{0:T(128)S(1)}, u32[32]{0:T(128)}, u32[]{:S(2)}) copy-start(u32[32]{0:T(128)} %constant.108) | copy-start | bytes 388
  317.5 47.5 %copy-start.23 = (f32[256]{0:T(256)S(1)}, f32[256]{0:T(256)}, u32[]{:S(2)}) copy-start(f32[256]{0:T(256)} %get-tuple-element.38) | copy-start | bytes 3076
  317.5 68.7 %copy-start.13 = (bf16[256,256]{1,0:T(8,128)(2,1)S(1)}, bf16[256,256]{1,0:T(8,128)(2,1)}, u32[]{:S(2)}) copy-start(bf16[256,256]{1,0:T(8,128)(2,1)} %param.9) | copy-start | bytes 393220
  317.6 45.1 %reduce-scatter.8.cloned.1.call-start = ((), (), s32[]{:S(2)}) async-start(), calls=%async_computation.11 | async-start | bytes 327680 | tf_op jit(solution)/shard_map/reduce_scatter | solution.py:160
  317.6 69.5 %copy-start.20 = (bf16[512,256]{1,0:T(8,128)(2,1)S(1)}, bf16[512,256]{1,0:T(8,128)(2,1)}, u32[]{:S(2)}) copy-start(bf16[512,256]{1,0:T(8,128)(2,1)} %copy-done.19) | copy-start | bytes 786436
  317.6 69.5 %copy-start.22 = (bf16[512,256]{1,0:T(8,128)(2,1)S(1)}, bf16[512,256]{1,0:T(8,128)(2,1)}, u32[]{:S(2)}) copy-start(bf16[512,256]{1,0:T(8,128)(2,1)} %copy-done.21) | copy-start | bytes 786436
  318.6 100.1 %all-reduce.4.cloned.1.call-start = ((), (), s32[]{:S(2)}) async-start(), calls=%async_computation.14 | async-start | bytes 917504 | tf_op jit(solution)/shard_map/psum | solution.py:157
  362.7 80.0 %reduce-scatter.10.cloned.1.call-start = ((), (), s32[]{:S(2)}) async-start(), calls=%async_computation.12 | async-start | bytes 655360
  (7 other events, 10.3 us)
Sparse Core Ops, SparseCore 0:
  317.7 22.5 reduce-scatter.11
  343.1 19.4 reduce-scatter.7
  365.8 52.9 all-reduce.3
  421.5 21.1 reduce-scatter.9
where the time goes:
time: 458 us; the launch traced here: 451 us
  waiting for transfers between devices  197 us (43%)
  matrix products  103 us (22%)
  local copies, waits for them, and re-layouts  47.5 us (10%)
  blocking collectives  40.6 us (9%)
  starting transfers between devices  31.7 us (7%)
  other arithmetic  15.7 us (3%)
  between operations  15.2 us (3%)
    all_to_all x4, waiting for transfers between devices, regroup_spectral(): lax.all_to_all(signal, 'seq', split_axis=1, concat_axis=0, tiled=True)  86.4 us
    unnamed x6, waiting for transfers between devices  43.7 us
    psum x1, waiting for transfers between devices, shards(): in_sum, out_sum, skip_sum = lax.psum((in_term, out_term, skip_term), 'seq')  30.5 us
    dot_general x2, matrix products, inverse_field(): jnp.einsum('kc,kjf->jcf', jnp.cos(inner_angle), spectrum, precision=HIGHEST)  21.2 us
    reduce_scatter x1, waiting for transfers between devices, shards(): lax.psum_scatter(out_sum, 'dp', scatter_dimension=0, tiled=True)  20.5 us
    dot_general x2, matrix products, forward_spectrum(): jnp.einsum('kc,cjf->kjf', jnp.cos(inner_angle), spread, precision=HIGHEST)  20.4 us
    dot_general x2, matrix products, forward_spectrum(): jnp.einsum('kc,cjf->kjf', -jnp.sin(inner_angle), spread, precision=HIGHEST)  20.1 us
    all_to_all x1, blocking collectives, regroup_real(): lax.all_to_all(signal, 'seq', split_axis=1, concat_axis=0, tiled=True)  19.5 us
  transfers between devices with their start and end apart: 11, of which 9 were waited for; matrix products, arithmetic and copies ran while one was open for 23% of the time, Pallas kernels for 0%

commit v1 on v0

v1 whole, which is shorter than its diff:
```python
import math

import jax
import jax.numpy as jnp
import numpy as np
from jax import lax
from jax.experimental import pallas as pl
from jax.experimental.pallas import tpu as pltpu
from jax.sharding import PartitionSpec as P

LANES = 128
F32 = jnp.float32
BF16 = jnp.bfloat16
SHIFT = 0.25


def split_const(table):
    high = table.astype(BF16)
    low = (table - high.astype(np.float64)).astype(BF16)
    return high, low


def tables(seq_parts, tiles):
    outer = seq_parts * tiles
    length = outer * LANES
    row = np.arange(outer)
    row_pos = (row % seq_parts) * tiles + row // seq_parts
    freq = np.arange(outer) + SHIFT
    lane = np.arange(LANES)
    angle = 2.0 * np.pi * np.outer(freq, row_pos) / outer
    fwd_high, fwd_low = split_const(np.concatenate([np.cos(angle), -np.sin(angle)], axis=0))
    first = np.concatenate([fwd_high, fwd_high, fwd_low], axis=1)
    inv_high, inv_low = split_const(
        np.concatenate([np.cos(angle.T), -np.sin(angle.T)], axis=1) / length
    )
    last = np.concatenate([inv_high, inv_high, inv_low], axis=1)
    turn = 2.0 * np.pi * np.outer(freq, lane) / length
    twiddle = np.stack([np.cos(turn), -np.sin(turn)]).astype(np.float32)
    inner = 2.0 * np.pi * np.outer(lane, lane) / LANES
    cos, sin = np.cos(inner), np.sin(inner)
    wide_fwd = np.stack(split_const(np.block([[cos, -sin], [sin, cos]])))
    wide_inv = np.stack(split_const(np.block([[cos, sin], [-sin, cos]])))
    return [jnp.asarray(t) for t in (first, last, twiddle, wide_fwd, wide_inv)]


def dot(a, b, contract=((1,), (0,))):
    return lax.dot_general(a, b, (contract, ((), ())), preferred_element_type=F32)


def split(x):
    high = x.astype(BF16)
    return high, (x - high.astype(F32)).astype(BF16)


def projections(tok_ref, cot_ref, win_ref, wout_ref):
    width = wout_ref.shape[0]
    projected = dot(win_ref[...], tok_ref[...], ((0,), (1,)))
    dmixed = dot(wout_ref[...], cot_ref[...], ((1,), (1,)))
    return projected[:width], projected[width : 2 * width], projected[2 * width :], dmixed


def prep_kernel(tok_ref, cot_ref, win_ref, wout_ref, taps_ref, send_ref):
    parts, _, tiles, chans, _ = send_ref.shape
    gate_out, gate_in, values, dmixed = projections(tok_ref, cot_ref, win_ref, wout_ref)
    signals = (values * gate_in, dmixed * gate_out, taps_ref[...].T)
    for sig, signal in enumerate(signals):
        for dest in range(parts):
            for tile in range(tiles):
                send_ref[dest, sig, tile] = signal[
                    dest * chans : (dest + 1) * chans, tile * LANES : (tile + 1) * LANES
                ]


def conv_kernel(parts, tiles, chans, chunk, recv_ref, first_ref, last_ref, tw_ref, fwd_ref, inv_ref, out_ref, zh_ref, zl_ref):
    outer = parts * tiles
    stride = 3 * tiles * chans
    tw_re, tw_im = tw_ref[0], tw_ref[1]

    def rows(sig, tile, chan):
        return pl.ds(sig * tiles * chans + tile * chans + chan, parts, stride=stride)

    def wide(high, low, ref):
        return dot(high, ref[0]) + dot(low, ref[0]) + dot(high, ref[1])

    def load(sig, chan):
        return jnp.concatenate([recv_ref[rows(sig, t, chan), :] for t in range(tiles)], axis=0)

    def step(index, _):
        base = index * chunk
        spectra = []
        for sig in range(3):
            for pair in range(chunk // 2):
                chan = base + 2 * pair
                x = jnp.concatenate([load(sig, chan), load(sig, chan + 1)], axis=1)
                high, low = split(x)
                a = dot(first_ref[...], jnp.concatenate([high, low, high], axis=0))
                for side in range(2):
                    lanes = slice(side * LANES, (side + 1) * LANES)
                    re, im = a[:outer, lanes], a[outer:, lanes]
                    z = jnp.concatenate(
                        [re * tw_re - im * tw_im, re * tw_im + im * tw_re], axis=1
                    )
                    high, low = split(z)
                    place = pl.ds((2 * pair + side) * outer, outer)
                    zh_ref[sig, place, :] = high
                    zl_ref[sig, place, :] = low
            f = wide(zh_ref[sig], zl_ref[sig], fwd_ref)
            spectra.append((f[:, :LANES], f[:, LANES:]))
        (g_re, g_im), (d_re, d_im), (h_re, h_im) = spectra
        products = (
            (h_re * g_re - h_im * g_im, h_re * g_im + h_im * g_re),
            (h_re * d_re + h_im * d_im, h_re * d_im - h_im * d_re),
            (g_re * d_re + g_im * d_im, g_re * d_im - g_im * d_re),
        )
        for sig, (re, im) in enumerate(products):
            high, low = split(jnp.concatenate([re, im], axis=1))
            u = wide(high, low, inv_ref)
            for pair in range(chunk // 2):
                sides = []
                for side in range(2):
                    start = (2 * pair + side) * outer
                    u_re, u_im = u[start : start + outer, :LANES], u[start : start + outer, LANES:]
                    sides.append(
                        jnp.concatenate(
                            [u_re * tw_re + u_im * tw_im, u_im * tw_re - u_re * tw_im], axis=0
                        )
                    )
                high, low = split(jnp.concatenate(sides, axis=1))
                y = dot(last_ref[...], jnp.concatenate([high, low, high], axis=0))
                for side in range(2):
                    chan = base + 2 * pair + side
                    for t in range(tiles):
                        out_ref[rows(sig, t, chan), :] = y[
                            t * parts : (t + 1) * parts, side * LANES : (side + 1) * LANES
                        ]
        return 0

    lax.fori_loop(0, chans // chunk, step, 0)


def final_kernel(scale, tok_ref, cot_ref, win_ref, wout_ref, skip_ref, back_ref, out_ref, din_ref, part_ref):
    parts, _, tiles, chans, _ = back_ref.shape
    width = wout_ref.shape[0]
    gate_out, gate_in, values, dmixed = projections(tok_ref, cot_ref, win_ref, wout_ref)
    gated = values * gate_in
    dconv = dmixed * gate_out

    def gather(sig):
        return jnp.concatenate(
            [
                jnp.concatenate([back_ref[src, sig, t] for t in range(tiles)], axis=1)
                for src in range(parts)
            ],
            axis=0,
        )

    skip = skip_ref[...]
    conv = gather(0) + skip * gated
    dgated = gather(1) + skip * dconv
    mixed = (conv * gate_out).astype(BF16)
    dproj = jnp.concatenate(
        [(dmixed * conv).astype(BF16), (dgated * values).astype(BF16), (dgated * gate_in).astype(BF16)],
        axis=0,
    )
    out_ref[...] = dot(mixed, wout_ref[...], ((0,), (0,))).astype(BF16)
    din_ref[...] = dot(dproj, win_ref[...], ((0,), (1,))).astype(BF16)
    part_ref[:, : 3 * width] = dot(tok_ref[...], dproj, ((0,), (1,))) * scale
    part_ref[:, 3 * width : 4 * width] = dot(mixed, cot_ref[...]) * scale
    product = dconv * gated * scale
    total = product[:, :LANES]
    for t in range(1, tiles):
        total = total + product[:, t * LANES : (t + 1) * LANES]
    part_ref[:, 4 * width :] = total


def exchange(x, axis):
    return lax.all_to_all(x, axis, split_axis=0, concat_axis=0, tiled=True)


def shards(tokens, cotangent, w_in, w_out, filter_taps, skip):
    width = w_out.shape[0]
    tok, cot = tokens[0], cotangent[0]
    rows = tok.shape[0]
    tiles = rows // LANES
    parts = lax.axis_size("seq")
    groups = lax.axis_size("dp")
    chans = width // parts
    outer = parts * tiles
    chunk = min(chans, 8)
    scale = 1.0 / math.sqrt(groups * parts * rows)
    first, last, twiddle, fwd, inv = tables(parts, tiles)
    shape = (parts, 3, tiles, chans, LANES)

    send = pl.pallas_call(
        prep_kernel,
        out_shape=jax.ShapeDtypeStruct(shape, F32),
        name="prep",
    )(tok, cot, w_in, w_out, filter_taps)
    recv = exchange(send, "seq")
    flat = (parts * 3 * tiles * chans, LANES)

    def body(*refs):
        conv_kernel(parts, tiles, chans, chunk, *refs)

    fields = pl.pallas_call(
        body,
        out_shape=jax.ShapeDtypeStruct(flat, F32),
        scratch_shapes=[pltpu.VMEM((3, chunk * outer, 2 * LANES), BF16)] * 2,
        name="convolve",
    )(recv.reshape(flat), first, last, twiddle, fwd, inv)
    back = exchange(fields.reshape(shape), "seq")

    def tail(*refs):
        final_kernel(scale, *refs)

    output, dinput, part = pl.pallas_call(
        tail,
        out_shape=(
            jax.ShapeDtypeStruct((rows, width), BF16),
            jax.ShapeDtypeStruct((rows, width), BF16),
            jax.ShapeDtypeStruct((width, 4 * width + LANES), F32),
        ),
        name="finish",
    )(tok, cot, w_in, w_out, skip[:, None], back)

    share = parts // groups
    taps = exchange(back[:, 2], "dp").reshape(groups, share, tiles, chans, LANES)
    taps = jnp.sum(taps, axis=0) * scale
    taps_part = taps.transpose(1, 3, 0, 2).reshape(rows, share * chans)

    cols = part.shape[1]
    piece = width // (groups * parts)
    part = part.reshape(groups, parts, piece, cols).transpose(1, 0, 2, 3)
    part = jnp.sum(exchange(part, "seq").reshape(parts, groups, piece, cols), axis=0)
    part = jnp.sum(exchange(part, "dp").reshape(groups, piece, cols), axis=0)
    spread = jnp.broadcast_to(part[None], (parts, piece, cols))
    total = exchange(spread, "seq").reshape(parts * piece, cols)
    return (
        output[None],
        dinput[None],
        total[:, : 3 * width],
        total[:, 3 * width : 4 * width],
        taps_part,
        jnp.sum(total[:, 4 * width :], axis=1),
    )


def solution(mesh):
    return jax.shard_map(
        shards,
        mesh=mesh,
        in_specs=(P("dp", "seq", None), P("dp", "seq", None), P(), P(), P("seq", None), P()),
        out_specs=(
            P("dp", "seq", None),
            P("dp", "seq", None),
            P("dp", None),
            P("dp", None),
            P("seq", "dp"),
            P("dp"),
        ),
        check_vma=False,
    )
```

time: 458 us -> 134 us (0.29); the launches traced: 451 us -> 134 us
  waiting for transfers between devices: 197 us -> 43.7 us
  matrix products: 103 us -> 0 us
  local copies, waits for them, and re-layouts: 47.5 us -> 8 us
  Pallas kernels: 0 us -> 18.4 us
  starting transfers between devices: 31.7 us -> 15.9 us
  between operations: 15.2 us -> 0.71 us
  other arithmetic: 15.7 us -> 1.41 us
  blocking collectives: 40.6 us -> 45.4 us
    dot_general x22 -> x0, matrix products: 103 us -> none  [the longest x2 21.2 us: inverse_field(): jnp.einsum('kc,kjf->jcf', jnp.cos(inner_angle), spectrum, precision=HIGHEST)]
    all_to_all x7 -> x4, waiting for transfers between devices: 102 us -> 43.7 us  [exchange(): return lax.all_to_all(x, axis, split_axis=0, concat_axis=0, tiled=True)]
    unnamed x6 -> x0, waiting for transfers between devices: 43.7 us -> none
    psum x1 -> x0, waiting for transfers between devices: 30.5 us -> none  [shards(): in_sum, out_sum, skip_sum = lax.psum((in_term, out_term, skip_term), 'seq')]
    all_to_all x1 -> x2, blocking collectives: 19.5 us -> 45.4 us  [exchange(): return lax.all_to_all(x, axis, split_axis=0, concat_axis=0, tiled=True)]
    reduce_scatter x1 -> x0, waiting for transfers between devices: 20.5 us -> none  [shards(): lax.psum_scatter(out_sum, 'dp', scatter_dimension=0, tiled=True)]
    concatenate x4 -> x0, local copies, waits for them, and re-layouts: 18.5 us -> none  [the longest x2 11.5 us: inverse_field(): jnp.concatenate([cos_part[..., :chan_count] - sin_part[..., chan_count:],...]
    pallas_call x0 -> x3, Pallas kernels: none -> 18.4 us  [the longest x1 11.2 us: shards(): pl.pallas_call(body, out_shape=jax.ShapeDtypeStruct(flat, F32), scratch_s...]
  transfers between devices with their start and end apart: 11 -> 4, of which waited for: 9 -> 4; matrix products, arithmetic and copies ran while one was open for 23% -> 3% of each run, Pallas kernels for 0% -> 0%
where the time goes in v1:
time: 134 us
  blocking collectives  45.4 us (34%)
  waiting for transfers between devices  43.7 us (33%)
  Pallas kernels  18.4 us (14%)
  starting transfers between devices  15.9 us (12%)
  local copies, waits for them, and re-layouts  8 us (6%)
  other arithmetic  1.41 us (1%)
    all_to_all x2, blocking collectives, exchange(): return lax.all_to_all(x, axis, split_axis=0, concat_axis=0, tiled=True)  45.4 us
    all_to_all x4, waiting for transfers between devices, exchange(): return lax.all_to_all(x, axis, split_axis=0, concat_axis=0, tiled=True)  43.7 us
    all_to_all x4, starting transfers between devices, exchange(): return lax.all_to_all(x, axis, split_axis=0, concat_axis=0, tiled=True)  15.9 us
    pallas_call x1, Pallas kernels, shards(): pl.pallas_call(body, out_shape=jax.ShapeDtypeStruct(flat, F32), scratch_s...  11.2 us
    pallas_call x1, Pallas kernels, shards(): pl.pallas_call(tail, out_shape=(jax.ShapeDtypeStruct((rows, width), BF16)...  4.22 us
    pallas_call x1, Pallas kernels, shards(): pl.pallas_call(prep_kernel, out_shape=jax.ShapeDtypeStruct(shape, F32), n...  3.01 us
  transfers between devices with their start and end apart: 4, of which 4 were waited for; matrix products, arithmetic and copies ran while one was open for 3% of the time, Pallas kernels for 0%

profile of v1, /device:TPU:0, one launch (start us, length us, event | category | flops | bytes accessed | tf_op | source)
XLA Modules:
  0.0 133.5 jit_solution(4490896198627448071)
XLA Ops:
  0.6 3.0 %prep.1 = f32[8,3,4,32,128]{4,3,2,1,0:T(8,128)} custom-call(bf16[512,256]{1,0:T(8,128)(2,1)} %bitcast.32, bf16[512,256]{1,0:T(8,128)(2,1)} %bitcast.34, bf16[256,768]{1,0:T(8,128)(2,1)} %refs_2_.2, bf16[256,256]{1,0:T(8,128)(2,1)} %refs_3_.2, f32[512,256]{1,0:T(8,128)} %taps_ref.1), custom_call_target="tpu_custom_call" | custom-call | tf_op jit(solution)/shard_map/prep/pallas_call | solution.py:194
  3.6 26.2 %all_to_all.30 = f32[8,3,4,32,128]{4,3,2,1,0:T(8,128)} all-to-all(f32[8,3,4,32,128]{4,3,2,1,0:T(8,128)} %prep.1), channel_id=1, replica_groups=mesh['dp'=4,'seq'=8] {'seq'}, dimensions={0} | all-to-all | bytes 3145728 | tf_op jit(solution)/shard_map/all_to_all | solution.py:177
  29.9 11.2 %convolve.1 = f32[3072,128]{1,0:T(8,128)} custom-call(f32[3072,128]{1,0:T(8,128)} %bitcast.25, bf16[64,96]{1,0:T(8,128)(2,1)} %constant.14.clone.refs_1_, bf16[32,192]{1,0:T(8,128)(2,1)} %constant.15.clone.refs_2_, f32[2,32,128]{2,1,0:T(8,128)} %constant.16.clone.refs_3_, bf16[2,256,256]{2,1,0:T(8,128)(2,1)} %constant.17.clone.refs_4_, ...), custom_call_target="tpu_custom_call" | custom-call | tf_op jit(solution)/shard_map/convolve/pallas_call | solution.py:205
  41.1 0.0 copy-start.1
  41.1 3.7 %all-to-all-start.1 = ((f32[8,3,4,32,128]{4,3,2,1,0:T(8,128)}), f32[8,3,4,32,128]{4,3,2,1,0:T(8,128)S(1)}, u32[]{:S(2)}, u32[]{:S(2)}) async-start(f32[8,3,4,32,128]{4,3,2,1,0:T(8,128)} %bitcast.24), calls=%async_computation.1 | async-start | bytes 3145728 | tf_op jit(solution)/shard_map/all_to_all | solution.py:177
  44.8 0.0 copy-done.1
  44.8 0.8 copy.23.refs_4_
  45.6 20.1 %all-to-all-done.1.refs_5_ = f32[8,3,4,32,128]{4,3,2,1,0:T(8,128)S(1)} async-done(((f32[8,3,4,32,128]{4,3,2,1,0:T(8,128)}), f32[8,3,4,32,128]{4,3,2,1,0:T(8,128)S(1)}, u32[]{:S(2)}, u32[]{:S(2)}) %all-to-all-start.1) | async-done | bytes 1572896 | tf_op jit(solution)/shard_map/all_to_all | solution.py:177
  65.7 0.0 copy-start
  65.7 1.2 copy-done
  66.9 4.2 %finish.1 = (bf16[512,256]{1,0:T(8,128)(2,1)}, bf16[512,256]{1,0:T(8,128)(2,1)}, f32[256,1152]{1,0:T(8,128)}) custom-call(bf16[512,256]{1,0:T(8,128)(2,1)} %bitcast.33, bf16[512,256]{1,0:T(8,128)(2,1)} %bitcast.35, bf16[256,768]{1,0:T(8,128)(2,1)} %refs_2_.2, bf16[256,256]{1,0:T(8,128)(2,1)} %refs_3_.2, f32[256,1]{1,0:T(8,128)} %copy.23.refs_4_, ...), custom_call_target="tpu_custom_call" | custom-call | tf_op jit(solution)/shard_map/finish/pallas_call | solution.py:216
  71.1 1.4 %copy.29 = f32[4,8,8,1152]{3,2,0,1:T(8,128)S(1)} copy(f32[4,8,8,1152]{3,2,1,0:T(8,128)} %bitcast.28) | data formatting | bytes 2359296 | tf_op jit(solution)/shard_map/reshape | solution.py:233
  72.5 19.1 %all_to_all.31 = f32[8,4,8,1152]{3,2,1,0:T(8,128)S(1)} all-to-all(f32[8,4,8,1152]{3,2,1,0:T(8,128)S(1)} %bitcast.26), channel_id=1, replica_groups=mesh['dp'=4,'seq'=8] {'seq'}, dimensions={0} | all-to-all | bytes 2359296 | tf_op jit(solution)/shard_map/all_to_all | solution.py:177
  91.6 0.7 reduce_sum.36
  92.3 5.3 %all-to-all-start.3 = ((f32[4,8,1152]{2,1,0:T(8,128)}), f32[4,8,1152]{2,1,0:T(8,128)S(1)}, u32[]{:S(2)}, u32[]{:S(2)}) async-start(f32[4,8,1152]{2,1,0:T(8,128)} %reduce_sum.36), calls=%async_computation.3 | async-start | bytes 294912 | tf_op jit(solution)/shard_map/all_to_all | solution.py:177
  97.7 1.9 %slice_bitcast_fusion = f32[8,4,32,128]{3,2,1,0:T(8,128)} fusion(f32[8,3,4,32,128]{4,3,2,1,0:T(8,128)} %copy-done), kind=kLoop, calls=%fused_computation.1 | loop fusion | bytes 1048576 | tf_op jit(solution)/shard_map/squeeze | solution.py:227
  99.5 4.3 %all-to-all-done.3 = f32[4,8,1152]{2,1,0:T(8,128)S(1)} async-done(((f32[4,8,1152]{2,1,0:T(8,128)}), f32[4,8,1152]{2,1,0:T(8,128)S(1)}, u32[]{:S(2)}, u32[]{:S(2)}) %all-to-all-start.3) | async-done | bytes 147488 | tf_op jit(solution)/shard_map/all_to_all | solution.py:177
  103.9 3.5 %all-to-all-start.5 = ((f32[8,4,32,128]{3,2,1,0:T(8,128)}), f32[8,4,32,128]{3,2,1,0:T(8,128)S(1)}, u32[]{:S(2)}, u32[]{:S(2)}) async-start(f32[8,4,32,128]{3,2,1,0:T(8,128)} %slice_bitcast_fusion), calls=%async_computation.5 | async-start | bytes 1048576 | tf_op jit(solution)/shard_map/all_to_all | solution.py:177
  107.4 12.8 %all-to-all-done.5 = f32[8,4,32,128]{3,2,1,0:T(8,128)S(1)} async-done(((f32[8,4,32,128]{3,2,1,0:T(8,128)}), f32[8,4,32,128]{3,2,1,0:T(8,128)S(1)}, u32[]{:S(2)}, u32[]{:S(2)}) %all-to-all-start.5) | async-done | bytes 524320 | tf_op jit(solution)/shard_map/all_to_all | solution.py:177
  120.2 0.7 broadcast_in_dim.18
  120.9 3.4 %all-to-all-start.4 = ((f32[8,8,1152]{2,1,0:T(8,128)}), f32[8,8,1152]{2,1,0:T(8,128)S(1)}, u32[]{:S(2)}, u32[]{:S(2)}) async-start(f32[8,8,1152]{2,1,0:T(8,128)} %broadcast_in_dim.18), calls=%async_computation.4 | async-start | bytes 589824 | tf_op jit(solution)/shard_map/all_to_all | solution.py:177
  124.4 0.1 copy.25
  124.5 0.7 copy.30
  125.2 6.4 %all-to-all-done.4 = f32[8,8,1152]{2,1,0:T(8,128)S(1)} async-done(((f32[8,8,1152]{2,1,0:T(8,128)}), f32[8,8,1152]{2,1,0:T(8,128)S(1)}, u32[]{:S(2)}, u32[]{:S(2)}) %all-to-all-start.4) | async-done | bytes 294944 | tf_op jit(solution)/shard_map/all_to_all | solution.py:177
  131.6 0.6 slice_reduce_fusion
  132.2 0.6 slice.17
  132.8 0.7 slice.16
  (3 shorter events, 0.1 us)
Async XLA Ops:
  41.1 3.7 %copy-start.1 = (f32[256]{0:T(256)S(1)}, f32[256]{0:T(256)}, u32[]{:S(2)}) copy-start(f32[256]{0:T(256)} %param.16) | copy-start | bytes 3076
  41.1 24.6 %all-to-all-start.1 = ((f32[8,3,4,32,128]{4,3,2,1,0:T(8,128)}), f32[8,3,4,32,128]{4,3,2,1,0:T(8,128)S(1)}, u32[]{:S(2)}, u32[]{:S(2)}) async-start(f32[8,3,4,32,128]{4,3,2,1,0:T(8,128)} %bitcast.24), calls=%async_computation.1 | async-start | bytes 3145728 | tf_op jit(solution)/shard_map/all_to_all | solution.py:177
  65.7 1.2 copy-start
  92.3 11.6 %all-to-all-start.3 = ((f32[4,8,1152]{2,1,0:T(8,128)}), f32[4,8,1152]{2,1,0:T(8,128)S(1)}, u32[]{:S(2)}, u32[]{:S(2)}) async-start(f32[4,8,1152]{2,1,0:T(8,128)} %reduce_sum.36), calls=%async_computation.3 | async-start | bytes 294912 | tf_op jit(solution)/shard_map/all_to_all | solution.py:177
  103.9 16.3 %all-to-all-start.5 = ((f32[8,4,32,128]{3,2,1,0:T(8,128)}), f32[8,4,32,128]{3,2,1,0:T(8,128)S(1)}, u32[]{:S(2)}, u32[]{:S(2)}) async-start(f32[8,4,32,128]{3,2,1,0:T(8,128)} %slice_bitcast_fusion), calls=%async_computation.5 | async-start | bytes 1048576 | tf_op jit(solution)/shard_map/all_to_all | solution.py:177
  120.9 10.6 %all-to-all-start.4 = ((f32[8,8,1152]{2,1,0:T(8,128)}), f32[8,8,1152]{2,1,0:T(8,128)S(1)}, u32[]{:S(2)}, u32[]{:S(2)}) async-start(f32[8,8,1152]{2,1,0:T(8,128)} %broadcast_in_dim.18), calls=%async_computation.4 | async-start | bytes 589824 | tf_op jit(solution)/shard_map/all_to_all | solution.py:177

commit v2 on v1

v2 whole, which is shorter than its diff:
```python
import math

import jax
import jax.numpy as jnp
import numpy as np
from jax import lax
from jax.experimental import pallas as pl
from jax.experimental.pallas import tpu as pltpu
from jax.sharding import PartitionSpec as P


LANES = 128
F32 = jnp.float32
BF16 = jnp.bfloat16
SHIFT = 0.25
VMEM_GRANT = 8 * 2**20
PREP_GRANT = 54984704


def split_const(table):
    high = table.astype(BF16)
    low = (table - high.astype(np.float64)).astype(BF16)
    return high, low


def tables(outer):
    length = outer * LANES
    place = np.arange(outer)
    freq = place + SHIFT
    lane = np.arange(LANES)
    angle = 2.0 * np.pi * np.outer(freq, place) / outer
    high, low = split_const(np.concatenate([np.cos(angle), -np.sin(angle)], axis=0))
    first = np.concatenate([high, high, low], axis=1)
    back = np.concatenate([np.cos(angle.T), -np.sin(angle.T)], axis=1) / length
    high, low = split_const(back)
    last = np.concatenate([high, high, low], axis=1)
    turn = 2.0 * np.pi * np.outer(freq, lane) / length
    twiddle = np.stack([np.cos(turn), -np.sin(turn)]).astype(np.float32)
    inner = 2.0 * np.pi * np.outer(lane, lane) / LANES
    cos, sin = np.cos(inner), np.sin(inner)
    fwd = np.stack(split_const(np.block([[cos, -sin], [sin, cos]])))
    inv = np.stack(split_const(np.block([[cos, sin], [-sin, cos]])))
    return [jnp.asarray(t) for t in (first, last, twiddle, fwd, inv)]


def dot(a, b, contract=((1,), (0,))):
    return lax.dot_general(a, b, (contract, ((), ())), preferred_element_type=F32)


def split(x):
    high = x.astype(BF16)
    return high, (x - high.astype(F32)).astype(BF16)


def wide(high, low, ref):
    return dot(high, ref[0]) + dot(low, ref[0]) + dot(high, ref[1])


def multiply(a, b):
    return a[0] * b[0] - a[1] * b[1], a[0] * b[1] + a[1] * b[0]


def correlate(a, b):
    return a[0] * b[0] + a[1] * b[1], a[0] * b[1] - a[1] * b[0]


def halves(x):
    return x[:, :LANES], x[:, LANES:]


def projections(tok_ref, cot_ref, win_ref, wout_ref):
    width = wout_ref.shape[0]
    projected = dot(win_ref[...], tok_ref[...], ((0,), (1,)))
    dmixed = dot(wout_ref[...], cot_ref[...], ((1,), (1,)))
    return projected[:width], projected[width : 2 * width], projected[2 * width :], dmixed


def skip_column(skip_ref, tiles):
    column = jnp.broadcast_to(skip_ref[...], (LANES, skip_ref.shape[1])).T
    return jnp.concatenate([column] * tiles, axis=1)


def deal(me, signal_ref, keep_ref, give_ref):
    count, size, _ = keep_ref.shape
    tiles = signal_ref.shape[1] // LANES
    chans = size // tiles
    for k in range(count):
        for flip, ref in enumerate((keep_ref, give_ref)):
            dest = me ^ (2 * k + flip)
            start = pl.multiple_of(dest * chans, chans)
            for t in range(tiles):
                ref[k, t * chans : (t + 1) * chans, :] = signal_ref[
                    pl.ds(start, chans), t * LANES : (t + 1) * LANES
                ]


def blocks_of(me, keep_ref, got_ref, recv_refs):
    yield me, keep_ref.at[0]
    yield me ^ 1, got_ref.at[0]
    for k, ref in enumerate(recv_refs):
        for flip in range(2):
            yield me ^ (2 * (k + 1) + flip), ref.at[flip]


def collect(me, field_ref, blocks):
    for source, ref in blocks_of(me, *blocks):
        size = ref.shape[0]
        field_ref[pl.ds(pl.multiple_of(source * size, size), size), :] = ref[...]


def collect_signal(me, signal_ref, blocks):
    tiles = signal_ref.shape[1] // LANES
    for source, ref in blocks_of(me, *blocks):
        chans = ref.shape[0] // tiles
        start = pl.multiple_of(source * chans, chans)
        for t in range(tiles):
            signal_ref[pl.ds(start, chans), t * LANES : (t + 1) * LANES] = ref[
                t * chans : (t + 1) * chans, :
            ]


def deal_field(me, field_ref, keep_ref, give_ref):
    count, size, _ = keep_ref.shape
    for k in range(count):
        for flip, ref in enumerate((keep_ref, give_ref)):
            dest = me ^ (2 * k + flip)
            ref[k] = field_ref[pl.ds(pl.multiple_of(dest * size, size), size), :]


def forward(field_ref, base, chunk, chans, first_ref, tw_ref, fwd_ref, zh_ref, zl_ref):
    outer = tw_ref.shape[1]
    tw_re, tw_im = tw_ref[0], tw_ref[1]
    for pair in range(chunk // 2):
        chan = base + 2 * pair
        x = jnp.concatenate(
            [field_ref[pl.ds(chan + side, outer, stride=chans), :] for side in range(2)], axis=1
        )
        high, low = split(x)
        a = dot(first_ref[...], jnp.concatenate([high, low, high], axis=0))
        for side in range(2):
            lanes = slice(side * LANES, (side + 1) * LANES)
            re, im = a[:outer, lanes], a[outer:, lanes]
            z = jnp.concatenate([re * tw_re - im * tw_im, re * tw_im + im * tw_re], axis=1)
            place = slice((2 * pair + side) * outer, (2 * pair + side + 1) * outer)
            zh_ref[place, :], zl_ref[place, :] = split(z)
    return wide(zh_ref[...], zl_ref[...], fwd_ref)


def inverse(pair_of, field_ref, base, chunk, chans, last_ref, tw_ref, inv_ref):
    outer = tw_ref.shape[1]
    tw_re, tw_im = tw_ref[0], tw_ref[1]
    high, low = split(jnp.concatenate(pair_of, axis=1))
    u = wide(high, low, inv_ref)
    for pair in range(chunk // 2):
        sides = []
        for side in range(2):
            start = (2 * pair + side) * outer
            re, im = halves(u[start : start + outer])
            sides.append(jnp.concatenate([re * tw_re + im * tw_im, im * tw_re - re * tw_im], axis=0))
        high, low = split(jnp.concatenate(sides, axis=1))
        y = dot(last_ref[...], jnp.concatenate([high, low, high], axis=0))
        for side in range(2):
            chan = base + 2 * pair + side
            field_ref[pl.ds(chan, outer, stride=chans), :] = y[:, side * LANES : (side + 1) * LANES]


def call(body, operands, outs, scratch=(), flops=0, space=pltpu.VMEM, grant=VMEM_GRANT):
    size = sum(x.size * x.dtype.itemsize for x in list(operands) + list(outs))
    specs = [pl.BlockSpec(memory_space=pltpu.SMEM)]
    specs += [pl.BlockSpec(memory_space=space)] * (len(operands) - 1)
    return pl.pallas_call(
        body,
        out_shape=tuple(outs),
        in_specs=specs,
        out_specs=tuple(pl.BlockSpec(memory_space=pltpu.VMEM) for _ in outs),
        scratch_shapes=list(scratch),
        cost_estimate=pl.CostEstimate(flops=flops, bytes_accessed=size, transcendentals=0),
        compiler_params=pltpu.CompilerParams(vmem_limit_bytes=grant),
    )(*operands)


def mirror(x, axis, mask):
    count = lax.axis_size(axis)
    return lax.ppermute(x, axis, [(i, i ^ mask) for i in range(count)])


def exchange(keep, give):
    got = mirror(give, "seq", 1)
    recv = []
    for k in range(1, keep.shape[0]):
        both = jnp.stack([keep[k], got[k]])
        recv.append(mirror(both, "seq", 2 * k))
    return [keep, got] + recv


def tree_sum(terms):
    while len(terms) > 1:
        terms = [a + b for a, b in zip(terms[::2], terms[1::2])]
    return terms[0]


def reversed_bits(slot, count):
    value = 0
    while count > 1:
        value = 2 * value + slot % 2
        slot //= 2
        count //= 2
    return value


def halve(x):
    mask = 1
    while x.shape[0] > 1:
        middle = x.shape[0] // 2
        x = x[:middle] + mirror(x[middle:], "dp", mask)
        mask *= 2
    return x[0]


def reduce_rows(keep, give):
    return halve(keep + mirror(give, "seq", 1))


def spread_rows(held):
    whole = [held]
    for k in range(1, lax.axis_size("seq") // 2):
        whole.append(mirror(held, "seq", 2 * k))
    whole = tree_sum(whole)
    return whole, mirror(whole, "seq", 1)


def shards(tokens, cotangent, w_in, w_out, filter_taps, skip):
    width = w_out.shape[0]
    tok, cot = tokens[0], cotangent[0]
    rows = tok.shape[0]
    tiles = rows // LANES
    parts = lax.axis_size("seq")
    groups = lax.axis_size("dp")
    chans = width // parts
    share = parts // groups
    outer = parts * tiles
    chunk = min(chans, 8)
    size = tiles * chans
    half = width // groups // 2
    scale = 1.0 / math.sqrt(groups * parts * rows)
    first, last, twiddle, fwd, inv = tables(outer)
    place = jnp.stack([lax.axis_index("seq"), lax.axis_index("dp")]).astype(jnp.int32)
    block = jax.ShapeDtypeStruct((parts // 2, size, LANES), F32)
    spectrum = jax.ShapeDtypeStruct((chans * outer, 2 * LANES), F32)
    signal = pltpu.VMEM((width, rows), F32)
    field = pltpu.VMEM((outer * chans, LANES), F32)
    split_rows = pltpu.VMEM((chunk * outer, 2 * LANES), BF16)
    n_blocks = parts // 2 + 1

    inputs = (filter_taps, tok, cot, w_in, w_out)

    def prep_kernel(at_ref, *refs):
        signal_ref, sems = refs[-2:]
        held = refs[-7:-2]
        copies = [
            pltpu.make_async_copy(source, target, sems.at[n])
            for n, (source, target) in enumerate(zip(refs[:5], held))
        ]
        for copy in copies:
            copy.start()
        refs = refs[5:-7]
        copies[0].wait()
        signal_ref[...] = held[0][...].T
        deal(at_ref[0], signal_ref, *refs[:2])
        for copy in copies[1:]:
            copy.wait()
        gate_out, gate_in, values, dmixed = projections(*held[1:])
        signal_ref[...] = values * gate_in
        deal(at_ref[0], signal_ref, *refs[2:4])
        signal_ref[...] = dmixed * gate_out
        deal(at_ref[0], signal_ref, *refs[4:6])

    dealt = call(
        prep_kernel, (place, *inputs), (block,) * 6,
        [pltpu.VMEM(x.shape, x.dtype) for x in inputs] + [signal, pltpu.SemaphoreType.DMA((5,))],
        flops=8 * rows * width * width, space=pltpu.MemorySpace.HBM, grant=PREP_GRANT,
    )
    taps_blocks = exchange(*dealt[:2])
    gated_blocks = exchange(*dealt[2:4])
    dconv_blocks = exchange(*dealt[4:])

    work = chans * outer * LANES * 4 * (3 * 2 * LANES + 6 * outer)

    def split_blocks(refs):
        return refs[0], refs[1], refs[2:n_blocks]

    def loop(step):
        def body(index, carry):
            step(index * chunk, pl.ds(pl.multiple_of(index * chunk * outer, chunk * outer), chunk * outer))
            return carry

        lax.fori_loop(0, chans // chunk, body, 0)

    def taps_spectrum_kernel(at_ref, first_ref, tw_ref, fwd_ref, *refs):
        blocks, (h_ref, x_ref, zh_ref, zl_ref) = split_blocks(refs[:n_blocks]), refs[n_blocks:]
        collect(at_ref[0], x_ref, blocks)

        def step(base, span):
            h_ref[span, :] = forward(x_ref, base, chunk, chans, first_ref, tw_ref, fwd_ref, zh_ref, zl_ref)

        loop(step)

    (taps_spec,) = call(
        taps_spectrum_kernel, (place, first, twiddle, fwd, *taps_blocks), (spectrum,),
        [field, split_rows, split_rows], flops=work,
    )

    def conv_kernel(at_ref, first_ref, last_ref, tw_ref, fwd_ref, inv_ref, h_ref, *refs):
        blocks = split_blocks(refs[:n_blocks])
        g_ref, keep_ref, give_ref, x_ref, y_ref, zh_ref, zl_ref = refs[n_blocks:]
        collect(at_ref[0], x_ref, blocks)

        def step(base, span):
            g = forward(x_ref, base, chunk, chans, first_ref, tw_ref, fwd_ref, zh_ref, zl_ref)
            g_ref[span, :] = g
            product = multiply(halves(h_ref[span, :]), halves(g))
            inverse(product, y_ref, base, chunk, chans, last_ref, tw_ref, inv_ref)

        loop(step)
        deal_field(at_ref[0], y_ref, keep_ref, give_ref)

    gated_spec, conv_keep, conv_give = call(
        conv_kernel, (place, first, last, twiddle, fwd, inv, taps_spec, *gated_blocks),
        (spectrum, block, block), [field, field, split_rows, split_rows], flops=2 * work,
    )
    conv_blocks = exchange(conv_keep, conv_give)
    term = jax.ShapeDtypeStruct((groups, share * size, LANES), F32)

    def corr_kernel(at_ref, first_ref, last_ref, tw_ref, fwd_ref, inv_ref, h_ref, g_ref, *refs):
        blocks = split_blocks(refs[:n_blocks])
        keep_ref, give_ref, term_ref, x_ref, y_ref, k_ref, zh_ref, zl_ref = refs[n_blocks:]
        collect(at_ref[0], x_ref, blocks)

        def step(base, span):
            d = halves(forward(x_ref, base, chunk, chans, first_ref, tw_ref, fwd_ref, zh_ref, zl_ref))
            for spec_ref, field_ref in ((h_ref, y_ref), (g_ref, k_ref)):
                product = correlate(halves(spec_ref[span, :]), d)
                inverse(product, field_ref, base, chunk, chans, last_ref, tw_ref, inv_ref)

        loop(step)
        deal_field(at_ref[0], y_ref, keep_ref, give_ref)
        for k in range(groups):
            for v in range(share):
                dest = at_ref[1] ^ reversed_bits(k, groups)
                row = (dest * share + ((at_ref[0] % share) ^ v)) * size
                term_ref[k, v * size : (v + 1) * size, :] = (
                    k_ref[pl.ds(pl.multiple_of(row, size), size), :] * scale
                )

    dgated_keep, dgated_give, term_parts = call(
        corr_kernel, (place, first, last, twiddle, fwd, inv, taps_spec, gated_spec, *dconv_blocks),
        (block, block, term), [field, field, field, split_rows, split_rows], flops=3 * work,
    )
    dgated_blocks = exchange(dgated_keep, dgated_give)

    def deal_part(at_ref, part_ref, keep_ref, give_ref):
        for k in range(groups):
            for flip, ref in enumerate((keep_ref, give_ref)):
                dest = at_ref[1] ^ reversed_bits(k, groups)
                start = (dest * 2 + ((at_ref[0] & 1) ^ flip)) * half
                ref[k] = part_ref[pl.ds(pl.multiple_of(start, half), half), :]

    def mix_kernel(at_ref, tok_ref, cot_ref, win_ref, wout_ref, skip_ref, *refs):
        blocks = split_blocks(refs[:n_blocks])
        out_ref, dproj_ref, keep_ref, give_ref, c_ref, part_ref = refs[n_blocks:]
        gate_out, gate_in, values, dmixed = projections(tok_ref, cot_ref, win_ref, wout_ref)
        gated = values * gate_in
        collect_signal(at_ref[0], c_ref, blocks)
        conv = c_ref[...] + skip_column(skip_ref, tiles) * gated
        mixed = (conv * gate_out).astype(BF16)
        dproj = (dmixed * conv).astype(BF16)
        dproj_ref[...] = dproj
        out_ref[...] = dot(mixed, wout_ref[...], ((0,), (0,))).astype(BF16)
        part_ref[:, :width] = dot(tok_ref[...], dproj, ((0,), (1,))) * scale
        part_ref[:, width : 2 * width] = dot(mixed, cot_ref[...]) * scale
        product = dmixed * gate_out * gated * scale
        total = product[:, :LANES]
        for t in range(1, tiles):
            total = total + product[:, t * LANES : (t + 1) * LANES]
        part_ref[:, 2 * width :] = total
        deal_part(at_ref, part_ref, keep_ref, give_ref)

    early = 2 * width + LANES
    piece = jax.ShapeDtypeStruct((groups, half, early), F32)
    output, dproj_first, early_keep, early_give = call(
        mix_kernel, (place, tok, cot, w_in, w_out, skip[None, :], *conv_blocks),
        (jax.ShapeDtypeStruct((rows, width), BF16), jax.ShapeDtypeStruct((width, rows), BF16), piece, piece),
        [signal, pltpu.VMEM((width, early), F32)], flops=14 * rows * width * width,
    )
    early_sum = reduce_rows(early_keep, early_give)

    def last_kernel(at_ref, tok_ref, cot_ref, win_ref, wout_ref, skip_ref, dproj_ref, *refs):
        blocks = split_blocks(refs[:n_blocks])
        din_ref, keep_ref, give_ref, c_ref, part_ref = refs[n_blocks:]
        gate_out, gate_in, values, dmixed = projections(tok_ref, cot_ref, win_ref, wout_ref)
        collect_signal(at_ref[0], c_ref, blocks)
        dgated = c_ref[...] + skip_column(skip_ref, tiles) * (dmixed * gate_out)
        dproj = jnp.concatenate([(dgated * values).astype(BF16), (dgated * gate_in).astype(BF16)], axis=0)
        part_ref[...] = dot(tok_ref[...], dproj, ((0,), (1,))) * scale
        deal_part(at_ref, part_ref, keep_ref, give_ref)
        dproj = jnp.concatenate([dproj_ref[...], dproj], axis=0)
        din_ref[...] = dot(dproj, win_ref[...], ((0,), (1,))).astype(BF16)

    piece = jax.ShapeDtypeStruct((groups, half, 2 * width), F32)
    dinput, late_keep, late_give = call(
        last_kernel, (place, tok, cot, w_in, w_out, skip[None, :], dproj_first, *dgated_blocks),
        (jax.ShapeDtypeStruct((rows, width), BF16), piece, piece),
        [signal, pltpu.VMEM((width, 2 * width), F32)], flops=18 * rows * width * width,
    )
    late_sum = reduce_rows(late_keep, late_give)

    grad_sum = spread_rows(jnp.concatenate([early_sum, late_sum], axis=1))
    term_sum = halve(term_parts)
    swap = [
        (i * parts + j, (j // share) * parts + i * share + j % share)
        for i in range(groups)
        for j in range(parts)
    ]
    term_sum = lax.ppermute(term_sum, ("dp", "seq"), swap)
    term_sum = term_sum.reshape(share, size, LANES)
    pieces = [term_sum] + [mirror(term_sum[k], "seq", k) for k in range(1, share)]

    def join_kernel(at_ref, *refs):
        sums, terms = refs[:2], refs[2 : 2 + share]
        in_ref, out_ref, taps_out_ref, skip_out_ref, skip_ref = refs[2 + share :]
        for flip, ref in enumerate(sums):
            row = pl.multiple_of(((at_ref[0] & 1) ^ flip) * half, half)
            span = pl.ds(row, half)
            in_ref[span, :width] = ref[:, :width]
            out_ref[span, :] = ref[:, width : 2 * width]
            skip_ref[span, :] = ref[:, 2 * width : early]
            in_ref[span, width:] = ref[:, early:]
        skip_out_ref[...] = jnp.sum(skip_ref[...], axis=1, keepdims=True).T
        for k in range(share):
            start = pl.multiple_of((k ^ (at_ref[0] % share)) * chans, chans)
            for t in range(tiles):
                span = slice(t * chans, (t + 1) * chans)
                piece = terms[k][span, :] if k else terms[0][0, span, :]
                taps_out_ref[pl.ds(start, chans), t * LANES : (t + 1) * LANES] = piece

    grad_in, grad_out, grad_taps, grad_skip = call(
        join_kernel, (place, *grad_sum, *pieces),
        (
            jax.ShapeDtypeStruct((2 * half, 3 * width), F32),
            jax.ShapeDtypeStruct((2 * half, width), F32),
            jax.ShapeDtypeStruct((share * chans, rows), F32),
            jax.ShapeDtypeStruct((1, 2 * half), F32),
        ),
        [pltpu.VMEM((2 * half, LANES), F32)], flops=rows * width,
    )
    return output[None], dinput[None], grad_in, grad_out, grad_taps.T, grad_skip[0]


def solution(mesh):
    return jax.shard_map(
        shards,
        mesh=mesh,
        in_specs=(P("dp", "seq", None), P("dp", "seq", None), P(), P(), P("seq", None), P()),
        out_specs=(
            P("dp", "seq", None),
            P("dp", "seq", None),
            P("dp", None),
            P("dp", None),
            P("seq", "dp"),
            P("dp"),
        ),
        check_vma=False,
    )
```

time: 134 us -> 96 us (0.72)
  the two profiles are of different devices: /device:TPU:0 before, /device:TPU:5 now
where the time goes in v2:
time: 96 us; the launch traced here: 95.8 us
  starting transfers between devices  46.9 us (49%)
  waiting for transfers between devices  25.1 us (26%)
  Pallas kernels  21.2 us (22%)
  local copies, waits for them, and re-layouts  1.16 us (1%)
  between operations  1.03 us (1%)
    ppermute x33, starting transfers between devices, mirror(): return lax.ppermute(x, axis, [(i, i ^ mask) for i in range(count)])  44.3 us
    ppermute x33, waiting for transfers between devices, mirror(): return lax.ppermute(x, axis, [(i, i ^ mask) for i in range(count)])  25.1 us
    pallas_call x7, Pallas kernels, call(): pl.pallas_call(body, out_shape=tuple(outs), in_specs=specs, out_specs=tup...  21.2 us
    ppermute x1, starting transfers between devices, shards(): term_sum = lax.ppermute(term_sum, ('dp', 'seq'), swap)  2.58 us
  transfers between devices with their start and end apart: 34, of which 14 were waited for; matrix products, arithmetic and copies ran while one was open for 1% of the time, Pallas kernels for 9%

profile of v2, /device:TPU:5, one launch (start us, length us, event | category | flops | bytes accessed | tf_op | source)
XLA Modules:
  0.0 95.8 jit_solution(11382411787706701886)
XLA Ops:
  1.6 3.1 %shard_map.154 = (f32[4,128,128]{2,1,0:T(8,128)S(1)}, f32[4,128,128]{2,1,0:T(8,128)S(1)}, f32[4,128,128]{2,1,0:T(8,128)S(1)}, f32[4,128,128]{2,1,0:T(8,128)S(1)}...) custom-call(s32[2]{0:T(128)S(1)} %pad_add_fusion.at_ref, f32[512,256]{1,0:T(8,128)} %refs_0_.1, ...), custom_call_target="tpu_custom_call" | custom-call | flops 268435456 | bytes 3145736 | tf_op jit(solution)/shard_map/pallas_call | solution.py:171
  6.7 1.2 %collective-permute-start.3 = (f32[2,128,128]{2,1,0:T(8,128)S(1)}, f32[2,128,128]{2,1,0:T(8,128)S(1)}, u32[]{:S(2)}, u32[]{:S(2)}) collective-permute-start(f32[2,128,128]{2,1,0:T(8,128)S(1)} %pad_maximum_fusion.3), channel_id=1, source_target_pairs={{0,6},{1,7},{2,4},{3,5},{4,2},{5,3},{6,0},{7,1},{8,14},{9,15},{10,... | collective-permute-start | bytes 393224 | tf_op jit(solution)/shard_map/ppermute | solution.py:184
  7.9 1.3 %collective-permute-start.2 = (f32[2,128,128]{2,1,0:T(8,128)S(1)}, f32[2,128,128]{2,1,0:T(8,128)S(1)}, u32[]{:S(2)}, u32[]{:S(2)}) collective-permute-start(f32[2,128,128]{2,1,0:T(8,128)S(1)} %pad_maximum_fusion.2), channel_id=1, source_target_pairs={{0,4},{1,5},{2,6},{3,7},{4,0},{5,1},{6,2},{7,3},{8,12},{9,13},{10,... | collective-permute-start | bytes 393224 | tf_op jit(solution)/shard_map/ppermute | solution.py:184
  9.6 1.3 %collective-permute-start.5 = (f32[2,128,128]{2,1,0:T(8,128)S(1)}, f32[2,128,128]{2,1,0:T(8,128)S(1)}, u32[]{:S(2)}, u32[]{:S(2)}) collective-permute-start(f32[2,128,128]{2,1,0:T(8,128)S(1)} %pad_maximum_fusion.4), channel_id=1, source_target_pairs={{0,2},{1,3},{2,0},{3,1},{4,6},{5,7},{6,4},{7,5},{8,10},{9,11},{10,... | collective-permute-start | bytes 393224 | tf_op jit(solution)/shard_map/ppermute | solution.py:184
  12.3 1.1 %collective-permute-start.7 = (f32[2,128,128]{2,1,0:T(8,128)S(1)}, f32[2,128,128]{2,1,0:T(8,128)S(1)}, u32[]{:S(2)}, u32[]{:S(2)}) collective-permute-start(f32[2,128,128]{2,1,0:T(8,128)S(1)} %pad_maximum_fusion.6), channel_id=1, source_target_pairs={{0,6},{1,7},{2,4},{3,5},{4,2},{5,3},{6,0},{7,1},{8,14},{9,15},{10,... | collective-permute-start | bytes 393224 | tf_op jit(solution)/shard_map/ppermute | solution.py:184
  13.5 2.3 %collective-permute-done.2.refs_3_ = f32[2,128,128]{2,1,0:T(8,128)S(1)} collective-permute-done((f32[2,128,128]{2,1,0:T(8,128)S(1)}, f32[2,128,128]{2,1,0:T(8,128)S(1)}, u32[]{:S(2)}, u32[]{:S(2)}) %collective-permute-start.2) | collective-permute-done | bytes 131104 | tf_op jit(solution)/shard_map/ppermute | solution.py:184
  15.9 1.4 %collective-permute-start.14 = (f32[2,128,128]{2,1,0:T(8,128)S(1)}, f32[2,128,128]{2,1,0:T(8,128)S(1)}, u32[]{:S(2)}, u32[]{:S(2)}) collective-permute-start(f32[2,128,128]{2,1,0:T(8,128)S(1)} %pad_maximum_fusion.11), channel_id=1, source_target_pairs={{0,4},{1,5},{2,6},{3,7},{4,0},{5,1},{6,2},{7,3},{8,12},{9,13},{10,... | collective-permute-start | bytes 393224 | tf_op jit(solution)/shard_map/ppermute | solution.py:184
  17.3 1.9 %collective-permute-start.15 = (f32[2,128,128]{2,1,0:T(8,128)S(1)}, f32[2,128,128]{2,1,0:T(8,128)S(1)}, u32[]{:S(2)}, u32[]{:S(2)}) collective-permute-start(f32[2,128,128]{2,1,0:T(8,128)S(1)} %pad_maximum_fusion.12), channel_id=1, source_target_pairs={{0,6},{1,7},{2,4},{3,5},{4,2},{5,3},{6,0},{7,1},{8,14},{9,15},{10,... | collective-permute-start | bytes 393224 | tf_op jit(solution)/shard_map/ppermute | solution.py:184
  19.2 2.2 %shard_map.155.h_ref = f32[1024,256]{1,0:T(8,128)S(1)} custom-call(s32[2]{0:T(128)S(1)} %pad_add_fusion.at_ref, bf16[64,96]{1,0:T(8,128)(2,1)S(1)} %copy-done.6, f32[2,32,128]{2,1,0:T(8,128)S(1)} %copy-done.5, bf16[2,256,256]{2,1,0:T(8,128)(2,1)S(1)} %copy-done.4, f32[4,128,128]{2,1,0:T(8,128)S(1)} %get-tuple-element.29.refs_0_, ...), custom_call_target="tpu_custom_call" | custom-call | flops 503316480 | bytes 2273288 | tf_op jit(solution)/shard_map/pallas_call | solution.py:171
  21.4 4.3 %shard_map.156 = (f32[1024,256]{1,0:T(8,128)S(1)}, f32[4,128,128]{2,1,0:T(8,128)S(1)}, f32[4,128,128]{2,1,0:T(8,128)S(1)}) custom-call(s32[2]{0:T(128)S(1)} %pad_add_fusion.at_ref, bf16[64,96]{1,0:T(8,128)(2,1)S(1)} %copy-done.6, bf16[32,192]{1,0:T(8,128)(2,1)S(1)} %copy-done.9, f32[2,32,128]{2,1,0:T(8,128)S(1)} %copy-done.5, ...), custom_call_target="tpu_custom_call" | custom-call | flops 1006632960 | bytes 4120584 | tf_op jit(solution)/shard_map/pallas_call | solution.py:171
  26.4 5.7 %shard_map.158 = (f32[4,128,128]{2,1,0:T(8,128)S(1)}, f32[4,128,128]{2,1,0:T(8,128)S(1)}, f32[4,256,128]{2,1,0:T(8,128)S(1)}) custom-call(s32[2]{0:T(128)S(1)} %pad_add_fusion.at_ref, bf16[64,96]{1,0:T(8,128)(2,1)S(1)} %copy-done.6, bf16[32,192]{1,0:T(8,128)(2,1)S(1)} %copy-done.9, f32[2,32,128]{2,1,0:T(8,128)S(1)} %copy-done.5, ...), custom_call_target="tpu_custom_call" | custom-call | flops 1509949440 | bytes 4644872 | tf_op jit(solution)/shard_map/pallas_call | solution.py:171
  32.1 1.8 %collective-permute-start.16 = (f32[4,128,128]{2,1,0:T(8,128)S(1)}, f32[4,128,128]{2,1,0:T(8,128)S(1)}, u32[]{:S(2)}, u32[]{:S(2)}) collective-permute-start(f32[4,128,128]{2,1,0:T(8,128)S(1)} %get-tuple-element.41), channel_id=1, source_target_pairs={{0,1},{1,0},{2,3},{3,2},{4,5},{5,4},{6,7},{7,6},{8,9},{9,8},{10,11... | collective-permute-start | bytes 786440 | tf_op jit(solution)/shard_map/ppermute | solution.py:184
  37.0 1.3 %collective-permute-start.10 = (f32[2,128,128]{2,1,0:T(8,128)S(1)}, f32[2,128,128]{2,1,0:T(8,128)S(1)}, u32[]{:S(2)}, u32[]{:S(2)}) collective-permute-start(f32[2,128,128]{2,1,0:T(8,128)S(1)} %pad_maximum_fusion.8), channel_id=1, source_target_pairs={{0,4},{1,5},{2,6},{3,7},{4,0},{5,1},{6,2},{7,3},{8,12},{9,13},{10,... | collective-permute-start | bytes 393224 | tf_op jit(solution)/shard_map/ppermute | solution.py:184
  39.2 3.5 %collective-permute-done.9.refs_2_ = f32[2,128,128]{2,1,0:T(8,128)S(1)} collective-permute-done((f32[2,128,128]{2,1,0:T(8,128)S(1)}, f32[2,128,128]{2,1,0:T(8,128)S(1)}, u32[]{:S(2)}, u32[]{:S(2)}) %collective-permute-start.9) | collective-permute-done | bytes 131104 | tf_op jit(solution)/shard_map/ppermute | solution.py:184
  43.9 1.5 %collective-permute-done.11.refs_4_ = f32[2,128,128]{2,1,0:T(8,128)S(1)} collective-permute-done((f32[2,128,128]{2,1,0:T(8,128)S(1)}, f32[2,128,128]{2,1,0:T(8,128)S(1)}, u32[]{:S(2)}, u32[]{:S(2)}) %collective-permute-start.11) | collective-permute-done | bytes 131104 | tf_op jit(solution)/shard_map/ppermute | solution.py:184
  45.4 2.0 %shard_map.157 = (bf16[512,256]{1,0:T(8,128)(2,1)}, bf16[256,512]{1,0:T(8,128)(2,1)S(1)}, f32[4,32,640]{2,1,0:T(8,128)S(1)}, f32[4,32,640]{2,1,0:T(8,128)S(1)}) custom-call(s32[2]{0:T(128)S(1)} %pad_add_fusion.at_ref, bf16[512,256]{1,0:T(8,128)(2,1)S(1)} %bitcast.17, bf16[512,256]{1,0:T(8,128)(2,1)S(1)} %bitcast.20, bf16[256,768]{1,0:T(8,128)(2,1)S(1)} %copy-done, ...), custom_call_target="tpu_custom_call" | custom-call | flops 469762048 | bytes 3146760 | tf_op jit(solution)/shard_map/pallas_call | solution.py:171
  47.5 2.6 %shard_map.159 = (bf16[512,256]{1,0:T(8,128)(2,1)}, f32[4,32,512]{2,1,0:T(8,128)S(1)}, f32[4,32,512]{2,1,0:T(8,128)S(1)}) custom-call(s32[2]{0:T(128)S(1)} %pad_add_fusion.at_ref, bf16[512,256]{1,0:T(8,128)(2,1)S(1)} %bitcast.18, bf16[512,256]{1,0:T(8,128)(2,1)S(1)} %bitcast.21, bf16[256,768]{1,0:T(8,128)(2,1)S(1)} %copy-done, ...), custom_call_target="tpu_custom_call" | custom-call | flops 603979776 | bytes 3015688 | tf_op jit(solution)/shard_map/pallas_call | solution.py:171
  50.1 3.5 %collective-permute-start.23 = (f32[4,32,512]{2,1,0:T(8,128)S(1)}, f32[4,32,512]{2,1,0:T(8,128)S(1)}, u32[]{:S(2)}, u32[]{:S(2)}) collective-permute-start(f32[4,32,512]{2,1,0:T(8,128)S(1)} %get-tuple-element.46), channel_id=1, source_target_pairs={{0,1},{1,0},{2,3},{3,2},{4,5},{5,4},{6,7},{7,6},{8,9},{9,8},{10,11... | collective-permute-start | bytes 786440 | tf_op jit(solution)/shard_map/ppermute | solution.py:184
  53.6 1.4 %collective-permute-start.30 = (f32[2,256,128]{2,1,0:T(8,128)S(1)}, f32[2,256,128]{2,1,0:T(8,128)S(1)}, u32[]{:S(2)}, u32[]{:S(2)}) collective-permute-start(f32[2,256,128]{2,1,0:T(8,128)S(1)} %slice.169), channel_id=1, source_target_pairs={{0,8},{8,0},{16,24},{24,16},{1,9},{9,1},{17,25},{25,17},{2,10},{10... | collective-permute-start | bytes 786440 | tf_op jit(solution)/shard_map/ppermute | solution.py:184
  56.2 5.4 %collective-permute-done.30 = f32[2,256,128]{2,1,0:T(8,128)S(1)} collective-permute-done((f32[2,256,128]{2,1,0:T(8,128)S(1)}, f32[2,256,128]{2,1,0:T(8,128)S(1)}, u32[]{:S(2)}, u32[]{:S(2)}) %collective-permute-start.30) | collective-permute-done | bytes 262176 | tf_op jit(solution)/shard_map/ppermute | solution.py:184
  61.6 2.4 %collective-permute-start.31 = (f32[1,256,128]{2,1,0:T(8,128)S(1)}, f32[1,256,128]{2,1,0:T(8,128)S(1)}, u32[]{:S(2)}, u32[]{:S(2)}) collective-permute-start(f32[1,256,128]{2,1,0:T(8,128)S(1)} %slice.197), channel_id=1, source_target_pairs={{0,16},{8,24},{16,0},{24,8},{1,17},{9,25},{17,1},{25,9},{2,18},{10... | collective-permute-start | bytes 393224 | tf_op jit(solution)/shard_map/ppermute | solution.py:184
  64.0 1.4 %collective-permute-start.21 = (f32[2,32,640]{2,1,0:T(8,128)S(1)}, f32[2,32,640]{2,1,0:T(8,128)S(1)}, u32[]{:S(2)}, u32[]{:S(2)}) collective-permute-start(f32[2,32,640]{2,1,0:T(8,128)S(1)} %slice.189), channel_id=1, source_target_pairs={{0,8},{8,0},{16,24},{24,16},{1,9},{9,1},{17,25},{25,17},{2,10},{10... | collective-permute-start | bytes 491528 | tf_op jit(solution)/shard_map/ppermute | solution.py:184
  65.4 1.3 %collective-permute-start.25 = (f32[1,32,512]{2,1,0:T(8,128)S(1)}, f32[1,32,512]{2,1,0:T(8,128)S(1)}, u32[]{:S(2)}, u32[]{:S(2)}) collective-permute-start(f32[1,32,512]{2,1,0:T(8,128)S(1)} %slice.195), channel_id=1, source_target_pairs={{0,16},{8,24},{16,0},{24,8},{1,17},{9,25},{17,1},{25,9},{2,18},{10... | collective-permute-start | bytes 196616 | tf_op jit(solution)/shard_map/ppermute | solution.py:184
  66.8 2.6 %collective-permute-done.21 = f32[2,32,640]{2,1,0:T(8,128)S(1)} collective-permute-done((f32[2,32,640]{2,1,0:T(8,128)S(1)}, f32[2,32,640]{2,1,0:T(8,128)S(1)}, u32[]{:S(2)}, u32[]{:S(2)}) %collective-permute-start.21) | collective-permute-done | bytes 163872 | tf_op jit(solution)/shard_map/ppermute | solution.py:184
  69.5 2.9 %collective-permute-start.22 = (f32[1,32,640]{2,1,0:T(8,128)S(1)}, f32[1,32,640]{2,1,0:T(8,128)S(1)}, u32[]{:S(2)}, u32[]{:S(2)}) collective-permute-start(f32[1,32,640]{2,1,0:T(8,128)S(1)} %slice.191), channel_id=1, source_target_pairs={{0,16},{8,24},{16,0},{24,8},{1,17},{9,25},{17,1},{25,9},{2,18},{10... | collective-permute-start | bytes 245768 | tf_op jit(solution)/shard_map/ppermute | solution.py:184
  72.4 3.4 %collective-permute-done.22 = f32[1,32,640]{2,1,0:T(8,128)S(1)} collective-permute-done((f32[1,32,640]{2,1,0:T(8,128)S(1)}, f32[1,32,640]{2,1,0:T(8,128)S(1)}, u32[]{:S(2)}, u32[]{:S(2)}) %collective-permute-start.22) | collective-permute-done | bytes 81952 | tf_op jit(solution)/shard_map/ppermute | solution.py:184
  75.9 1.8 %collective-permute-start.28 = (f32[32,1152]{1,0:T(8,128)S(1)}, f32[32,1152]{1,0:T(8,128)S(1)}, u32[]{:S(2)}, u32[]{:S(2)}) collective-permute-start(f32[32,1152]{1,0:T(8,128)S(1)} %pad_maximum_fusion), channel_id=1, source_target_pairs={{0,6},{1,7},{2,4},{3,5},{4,2},{5,3},{6,0},{7,1},{8,14},{9,15},{10,... | collective-permute-start | bytes 442376 | tf_op jit(solution)/shard_map/ppermute | solution.py:184
  78.6 2.6 %collective-permute-start.32 = (f32[256,128]{1,0:T(8,128)S(1)}, f32[256,128]{1,0:T(8,128)S(1)}, u32[]{:S(2)}, u32[]{:S(2)}) collective-permute-start(f32[256,128]{1,0:T(8,128)S(1)} %fusion), channel_id=1, source_target_pairs={{0,0},{1,1},{2,8},{3,9},{4,16},{5,17},{6,24},{7,25},{8,2},{9,3},{1... | collective-permute-start | bytes 393224 | tf_op jit(solution)/shard_map/ppermute | solution.py:424
  81.5 1.2 %collective-permute-done.26 = f32[32,1152]{1,0:T(8,128)S(1)} collective-permute-done((f32[32,1152]{1,0:T(8,128)S(1)}, f32[32,1152]{1,0:T(8,128)S(1)}, u32[]{:S(2)}, u32[]{:S(2)}) %collective-permute-start.26) | collective-permute-done | bytes 147488 | tf_op jit(solution)/shard_map/ppermute | solution.py:184
  82.7 5.6 %collective-permute-start.29 = (f32[32,1152]{1,0:T(8,128)S(1)}, f32[32,1152]{1,0:T(8,128)S(1)}, u32[]{:S(2)}, u32[]{:S(2)}) collective-permute-start(f32[32,1152]{1,0:T(8,128)S(1)} %add_add_fusion.refs_0_), channel_id=1, source_target_pairs={{0,1},{1,0},{2,3},{3,2},{4,5},{5,4},{6,7},{7,6},{8,9},{9,8},{10,11... | collective-permute-start | bytes 442376 | tf_op jit(solution)/shard_map/ppermute | solution.py:184
  88.3 5.3 %collective-permute-start.33 = (f32[128,128]{1,0:T(8,128)S(1)}, f32[128,128]{1,0:T(8,128)S(1)}, u32[]{:S(2)}, u32[]{:S(2)}) collective-permute-start(f32[128,128]{1,0:T(8,128)S(1)} %slice.198), channel_id=1, source_target_pairs={{0,1},{1,0},{2,3},{3,2},{4,5},{5,4},{6,7},{7,6},{8,9},{9,8},{10,11... | collective-permute-start | bytes 196616 | tf_op jit(solution)/shard_map/ppermute | solution.py:184
  94.5 1.3 %shard_map.160 = (f32[64,768]{1,0:T(8,128)}, f32[64,256]{1,0:T(8,128)}, f32[64,512]{1,0:T(8,128)}, f32[1,64]{1,0:T(1,128)}) custom-call(s32[2]{0:T(128)S(1)} %pad_add_fusion.at_ref, f32[32,1152]{1,0:T(8,128)S(1)} %add_add_fusion.refs_0_, f32[32,1152]{1,0:T(8,128)S(1)} %collective-permute-done.29.refs_1_, f32[2,128,128]{2,1,0:T(8,128)S(1)} %bitcast.22, ...), custom_call_target="tpu_custom_call" | custom-call | flops 131072 | bytes 885000 | tf_op jit(solution)/shard_map/pallas_call | solution.py:171
  (105 shorter events, 14.0 us)
Async XLA Ops:
  5.5 4.1 %collective-permute-start.4 = (f32[4,128,128]{2,1,0:T(8,128)S(1)}, f32[4,128,128]{2,1,0:T(8,128)S(1)}, u32[]{:S(2)}, u32[]{:S(2)}) collective-permute-start(f32[4,128,128]{2,1,0:T(8,128)S(1)} %get-tuple-element.32), channel_id=1, source_target_pairs={{0,1},{1,0},{2,3},{3,2},{4,5},{5,4},{6,7},{7,6},{8,9},{9,8},{10,11... | collective-permute-start | bytes 786440 | tf_op jit(solution)/shard_map/ppermute | solution.py:184
  5.6 5.3 %collective-permute-start.12 = (f32[4,128,128]{2,1,0:T(8,128)}, f32[4,128,128]{2,1,0:T(8,128)S(1)}, u32[]{:S(2)}, u32[]{:S(2)}) collective-permute-start(f32[4,128,128]{2,1,0:T(8,128)} %get-tuple-element.39), channel_id=1, source_target_pairs={{0,1},{1,0},{2,3},{3,2},{4,5},{5,4},{6,7},{7,6},{8,9},{9,8},{10,11... | collective-permute-start | bytes 786440 | tf_op jit(solution)/shard_map/ppermute | solution.py:184
  6.7 5.7 %collective-permute-start.3 = (f32[2,128,128]{2,1,0:T(8,128)S(1)}, f32[2,128,128]{2,1,0:T(8,128)S(1)}, u32[]{:S(2)}, u32[]{:S(2)}) collective-permute-start(f32[2,128,128]{2,1,0:T(8,128)S(1)} %pad_maximum_fusion.3), channel_id=1, source_target_pairs={{0,6},{1,7},{2,4},{3,5},{4,2},{5,3},{6,0},{7,1},{8,14},{9,15},{10,... | collective-permute-start | bytes 393224 | tf_op jit(solution)/shard_map/ppermute | solution.py:184
  7.9 8.0 %collective-permute-start.2 = (f32[2,128,128]{2,1,0:T(8,128)S(1)}, f32[2,128,128]{2,1,0:T(8,128)S(1)}, u32[]{:S(2)}, u32[]{:S(2)}) collective-permute-start(f32[2,128,128]{2,1,0:T(8,128)S(1)} %pad_maximum_fusion.2), channel_id=1, source_target_pairs={{0,4},{1,5},{2,6},{3,7},{4,0},{5,1},{6,2},{7,3},{8,12},{9,13},{10,... | collective-permute-start | bytes 393224 | tf_op jit(solution)/shard_map/ppermute | solution.py:184
  9.2 6.6 %collective-permute-start.1 = (f32[2,128,128]{2,1,0:T(8,128)S(1)}, f32[2,128,128]{2,1,0:T(8,128)S(1)}, u32[]{:S(2)}, u32[]{:S(2)}) collective-permute-start(f32[2,128,128]{2,1,0:T(8,128)S(1)} %pad_maximum_fusion.1), channel_id=1, source_target_pairs={{0,2},{1,3},{2,0},{3,1},{4,6},{5,7},{6,4},{7,5},{8,10},{9,11},{10,... | collective-permute-start | bytes 393224 | tf_op jit(solution)/shard_map/ppermute | solution.py:184
  9.6 7.7 %collective-permute-start.5 = (f32[2,128,128]{2,1,0:T(8,128)S(1)}, f32[2,128,128]{2,1,0:T(8,128)S(1)}, u32[]{:S(2)}, u32[]{:S(2)}) collective-permute-start(f32[2,128,128]{2,1,0:T(8,128)S(1)} %pad_maximum_fusion.4), channel_id=1, source_target_pairs={{0,2},{1,3},{2,0},{3,1},{4,6},{5,7},{6,4},{7,5},{8,10},{9,11},{10,... | collective-permute-start | bytes 393224 | tf_op jit(solution)/shard_map/ppermute | solution.py:184
  10.9 10.5 %collective-permute-start.6 = (f32[2,128,128]{2,1,0:T(8,128)S(1)}, f32[2,128,128]{2,1,0:T(8,128)S(1)}, u32[]{:S(2)}, u32[]{:S(2)}) collective-permute-start(f32[2,128,128]{2,1,0:T(8,128)S(1)} %pad_maximum_fusion.5), channel_id=1, source_target_pairs={{0,4},{1,5},{2,6},{3,7},{4,0},{5,1},{6,2},{7,3},{8,12},{9,13},{10,... | collective-permute-start | bytes 393224 | tf_op jit(solution)/shard_map/ppermute | solution.py:184
  12.3 9.1 %collective-permute-start.7 = (f32[2,128,128]{2,1,0:T(8,128)S(1)}, f32[2,128,128]{2,1,0:T(8,128)S(1)}, u32[]{:S(2)}, u32[]{:S(2)}) collective-permute-start(f32[2,128,128]{2,1,0:T(8,128)S(1)} %pad_maximum_fusion.6), channel_id=1, source_target_pairs={{0,6},{1,7},{2,4},{3,5},{4,2},{5,3},{6,0},{7,1},{8,14},{9,15},{10,... | collective-permute-start | bytes 393224 | tf_op jit(solution)/shard_map/ppermute | solution.py:184
  15.9 9.9 %collective-permute-start.13 = (f32[2,128,128]{2,1,0:T(8,128)S(1)}, f32[2,128,128]{2,1,0:T(8,128)S(1)}, u32[]{:S(2)}, u32[]{:S(2)}) collective-permute-start(f32[2,128,128]{2,1,0:T(8,128)S(1)} %pad_maximum_fusion.10), channel_id=1, source_target_pairs={{0,2},{1,3},{2,0},{3,1},{4,6},{5,7},{6,4},{7,5},{8,10},{9,11},{10,... | collective-permute-start | bytes 393224 | tf_op jit(solution)/shard_map/ppermute | solution.py:184
  15.9 9.9 %collective-permute-start.14 = (f32[2,128,128]{2,1,0:T(8,128)S(1)}, f32[2,128,128]{2,1,0:T(8,128)S(1)}, u32[]{:S(2)}, u32[]{:S(2)}) collective-permute-start(f32[2,128,128]{2,1,0:T(8,128)S(1)} %pad_maximum_fusion.11), channel_id=1, source_target_pairs={{0,4},{1,5},{2,6},{3,7},{4,0},{5,1},{6,2},{7,3},{8,12},{9,13},{10,... | collective-permute-start | bytes 393224 | tf_op jit(solution)/shard_map/ppermute | solution.py:184
  17.3 9.1 %collective-permute-start.15 = (f32[2,128,128]{2,1,0:T(8,128)S(1)}, f32[2,128,128]{2,1,0:T(8,128)S(1)}, u32[]{:S(2)}, u32[]{:S(2)}) collective-permute-start(f32[2,128,128]{2,1,0:T(8,128)S(1)} %pad_maximum_fusion.12), channel_id=1, source_target_pairs={{0,6},{1,7},{2,4},{3,5},{4,2},{5,3},{6,0},{7,1},{8,14},{9,15},{10,... | collective-permute-start | bytes 393224 | tf_op jit(solution)/shard_map/ppermute | solution.py:184
  32.1 2.9 %collective-permute-start.16 = (f32[4,128,128]{2,1,0:T(8,128)S(1)}, f32[4,128,128]{2,1,0:T(8,128)S(1)}, u32[]{:S(2)}, u32[]{:S(2)}) collective-permute-start(f32[4,128,128]{2,1,0:T(8,128)S(1)} %get-tuple-element.41), channel_id=1, source_target_pairs={{0,1},{1,0},{2,3},{3,2},{4,5},{5,4},{6,7},{7,6},{8,9},{9,8},{10,11... | collective-permute-start | bytes 786440 | tf_op jit(solution)/shard_map/ppermute | solution.py:184
  35.1 12.3 %collective-permute-start.17 = (f32[2,128,128]{2,1,0:T(8,128)S(1)}, f32[2,128,128]{2,1,0:T(8,128)S(1)}, u32[]{:S(2)}, u32[]{:S(2)}) collective-permute-start(f32[2,128,128]{2,1,0:T(8,128)S(1)} %pad_maximum_fusion.13), channel_id=1, source_target_pairs={{0,2},{1,3},{2,0},{3,1},{4,6},{5,7},{6,4},{7,5},{8,10},{9,11},{10,... | collective-permute-start | bytes 393224 | tf_op jit(solution)/shard_map/ppermute | solution.py:184
  36.0 11.5 %collective-permute-start.18 = (f32[2,128,128]{2,1,0:T(8,128)S(1)}, f32[2,128,128]{2,1,0:T(8,128)S(1)}, u32[]{:S(2)}, u32[]{:S(2)}) collective-permute-start(f32[2,128,128]{2,1,0:T(8,128)S(1)} %pad_maximum_fusion.14), channel_id=1, source_target_pairs={{0,4},{1,5},{2,6},{3,7},{4,0},{5,1},{6,2},{7,3},{8,12},{9,13},{10,... | collective-permute-start | bytes 393224 | tf_op jit(solution)/shard_map/ppermute | solution.py:184
  36.3 6.4 %collective-permute-start.9 = (f32[2,128,128]{2,1,0:T(8,128)S(1)}, f32[2,128,128]{2,1,0:T(8,128)S(1)}, u32[]{:S(2)}, u32[]{:S(2)}) collective-permute-start(f32[2,128,128]{2,1,0:T(8,128)S(1)} %pad_maximum_fusion.7), channel_id=1, source_target_pairs={{0,2},{1,3},{2,0},{3,1},{4,6},{5,7},{6,4},{7,5},{8,10},{9,11},{10,... | collective-permute-start | bytes 393224 | tf_op jit(solution)/shard_map/ppermute | solution.py:184
  37.0 6.8 %collective-permute-start.10 = (f32[2,128,128]{2,1,0:T(8,128)S(1)}, f32[2,128,128]{2,1,0:T(8,128)S(1)}, u32[]{:S(2)}, u32[]{:S(2)}) collective-permute-start(f32[2,128,128]{2,1,0:T(8,128)S(1)} %pad_maximum_fusion.8), channel_id=1, source_target_pairs={{0,4},{1,5},{2,6},{3,7},{4,0},{5,1},{6,2},{7,3},{8,12},{9,13},{10,... | collective-permute-start | bytes 393224 | tf_op jit(solution)/shard_map/ppermute | solution.py:184
  38.4 7.0 %collective-permute-start.11 = (f32[2,128,128]{2,1,0:T(8,128)S(1)}, f32[2,128,128]{2,1,0:T(8,128)S(1)}, u32[]{:S(2)}, u32[]{:S(2)}) collective-permute-start(f32[2,128,128]{2,1,0:T(8,128)S(1)} %pad_maximum_fusion.9), channel_id=1, source_target_pairs={{0,6},{1,7},{2,4},{3,5},{4,2},{5,3},{6,0},{7,1},{8,14},{9,15},{10,... | collective-permute-start | bytes 393224 | tf_op jit(solution)/shard_map/ppermute | solution.py:184
  42.7 4.8 %collective-permute-start.19 = (f32[2,128,128]{2,1,0:T(8,128)S(1)}, f32[2,128,128]{2,1,0:T(8,128)S(1)}, u32[]{:S(2)}, u32[]{:S(2)}) collective-permute-start(f32[2,128,128]{2,1,0:T(8,128)S(1)} %pad_maximum_fusion.15), channel_id=1, source_target_pairs={{0,6},{1,7},{2,4},{3,5},{4,2},{5,3},{6,0},{7,1},{8,14},{9,15},{10,... | collective-permute-start | bytes 393224 | tf_op jit(solution)/shard_map/ppermute | solution.py:184
  50.1 5.2 %collective-permute-start.23 = (f32[4,32,512]{2,1,0:T(8,128)S(1)}, f32[4,32,512]{2,1,0:T(8,128)S(1)}, u32[]{:S(2)}, u32[]{:S(2)}) collective-permute-start(f32[4,32,512]{2,1,0:T(8,128)S(1)} %get-tuple-element.46), channel_id=1, source_target_pairs={{0,1},{1,0},{2,3},{3,2},{4,5},{5,4},{6,7},{7,6},{8,9},{9,8},{10,11... | collective-permute-start | bytes 786440 | tf_op jit(solution)/shard_map/ppermute | solution.py:184
  53.6 7.9 %collective-permute-start.30 = (f32[2,256,128]{2,1,0:T(8,128)S(1)}, f32[2,256,128]{2,1,0:T(8,128)S(1)}, u32[]{:S(2)}, u32[]{:S(2)}) collective-permute-start(f32[2,256,128]{2,1,0:T(8,128)S(1)} %slice.169), channel_id=1, source_target_pairs={{0,8},{8,0},{16,24},{24,16},{1,9},{9,1},{17,25},{25,17},{2,10},{10... | collective-permute-start | bytes 786440 | tf_op jit(solution)/shard_map/ppermute | solution.py:184
  55.0 9.0 %collective-permute-start.20 = (f32[4,32,640]{2,1,0:T(8,128)S(1)}, f32[4,32,640]{2,1,0:T(8,128)S(1)}, u32[]{:S(2)}, u32[]{:S(2)}) collective-permute-start(f32[4,32,640]{2,1,0:T(8,128)S(1)} %get-tuple-element.44), channel_id=1, source_target_pairs={{0,1},{1,0},{2,3},{3,2},{4,5},{5,4},{6,7},{7,6},{8,9},{9,8},{10,11... | collective-permute-start | bytes 983048 | tf_op jit(solution)/shard_map/ppermute | solution.py:184
  55.3 10.1 %collective-permute-start.24 = (f32[2,32,512]{2,1,0:T(8,128)S(1)}, f32[2,32,512]{2,1,0:T(8,128)S(1)}, u32[]{:S(2)}, u32[]{:S(2)}) collective-permute-start(f32[2,32,512]{2,1,0:T(8,128)S(1)} %slice.193), channel_id=1, source_target_pairs={{0,8},{8,0},{16,24},{24,16},{1,9},{9,1},{17,25},{25,17},{2,10},{10... | collective-permute-start | bytes 393224 | tf_op jit(solution)/shard_map/ppermute | solution.py:184
  61.6 16.9 %collective-permute-start.31 = (f32[1,256,128]{2,1,0:T(8,128)S(1)}, f32[1,256,128]{2,1,0:T(8,128)S(1)}, u32[]{:S(2)}, u32[]{:S(2)}) collective-permute-start(f32[1,256,128]{2,1,0:T(8,128)S(1)} %slice.197), channel_id=1, source_target_pairs={{0,16},{8,24},{16,0},{24,8},{1,17},{9,25},{17,1},{25,9},{2,18},{10... | collective-permute-start | bytes 393224 | tf_op jit(solution)/shard_map/ppermute | solution.py:184
  64.0 5.4 %collective-permute-start.21 = (f32[2,32,640]{2,1,0:T(8,128)S(1)}, f32[2,32,640]{2,1,0:T(8,128)S(1)}, u32[]{:S(2)}, u32[]{:S(2)}) collective-permute-start(f32[2,32,640]{2,1,0:T(8,128)S(1)} %slice.189), channel_id=1, source_target_pairs={{0,8},{8,0},{16,24},{24,16},{1,9},{9,1},{17,25},{25,17},{2,10},{10... | collective-permute-start | bytes 491528 | tf_op jit(solution)/shard_map/ppermute | solution.py:184
  65.4 6.9 %collective-permute-start.25 = (f32[1,32,512]{2,1,0:T(8,128)S(1)}, f32[1,32,512]{2,1,0:T(8,128)S(1)}, u32[]{:S(2)}, u32[]{:S(2)}) collective-permute-start(f32[1,32,512]{2,1,0:T(8,128)S(1)} %slice.195), channel_id=1, source_target_pairs={{0,16},{8,24},{16,0},{24,8},{1,17},{9,25},{17,1},{25,9},{2,18},{10... | collective-permute-start | bytes 196616 | tf_op jit(solution)/shard_map/ppermute | solution.py:184
  69.5 6.3 %collective-permute-start.22 = (f32[1,32,640]{2,1,0:T(8,128)S(1)}, f32[1,32,640]{2,1,0:T(8,128)S(1)}, u32[]{:S(2)}, u32[]{:S(2)}) collective-permute-start(f32[1,32,640]{2,1,0:T(8,128)S(1)} %slice.191), channel_id=1, source_target_pairs={{0,16},{8,24},{16,0},{24,8},{1,17},{9,25},{17,1},{25,9},{2,18},{10... | collective-permute-start | bytes 245768 | tf_op jit(solution)/shard_map/ppermute | solution.py:184
  75.8 5.6 %collective-permute-start.27 = (f32[32,1152]{1,0:T(8,128)S(1)}, f32[32,1152]{1,0:T(8,128)S(1)}, u32[]{:S(2)}, u32[]{:S(2)}) collective-permute-start(f32[32,1152]{1,0:T(8,128)S(1)} %pad_maximum_fusion), channel_id=1, source_target_pairs={{0,4},{1,5},{2,6},{3,7},{4,0},{5,1},{6,2},{7,3},{8,12},{9,13},{10,... | collective-permute-start | bytes 442376 | tf_op jit(solution)/shard_map/ppermute | solution.py:184
  75.9 5.6 %collective-permute-start.28 = (f32[32,1152]{1,0:T(8,128)S(1)}, f32[32,1152]{1,0:T(8,128)S(1)}, u32[]{:S(2)}, u32[]{:S(2)}) collective-permute-start(f32[32,1152]{1,0:T(8,128)S(1)} %pad_maximum_fusion), channel_id=1, source_target_pairs={{0,6},{1,7},{2,4},{3,5},{4,2},{5,3},{6,0},{7,1},{8,14},{9,15},{10,... | collective-permute-start | bytes 442376 | tf_op jit(solution)/shard_map/ppermute | solution.py:184
  77.8 4.9 %collective-permute-start.26 = (f32[32,1152]{1,0:T(8,128)S(1)}, f32[32,1152]{1,0:T(8,128)S(1)}, u32[]{:S(2)}, u32[]{:S(2)}) collective-permute-start(f32[32,1152]{1,0:T(8,128)S(1)} %pad_maximum_fusion), channel_id=1, source_target_pairs={{0,2},{1,3},{2,0},{3,1},{4,6},{5,7},{6,4},{7,5},{8,10},{9,11},{10,... | collective-permute-start | bytes 442376 | tf_op jit(solution)/shard_map/ppermute | solution.py:184
  78.6 9.7 %collective-permute-start.32 = (f32[256,128]{1,0:T(8,128)S(1)}, f32[256,128]{1,0:T(8,128)S(1)}, u32[]{:S(2)}, u32[]{:S(2)}) collective-permute-start(f32[256,128]{1,0:T(8,128)S(1)} %fusion), channel_id=1, source_target_pairs={{0,0},{1,1},{2,8},{3,9},{4,16},{5,17},{6,24},{7,25},{8,2},{9,3},{1... | collective-permute-start | bytes 393224 | tf_op jit(solution)/shard_map/ppermute | solution.py:424
  82.7 11.8 %collective-permute-start.29 = (f32[32,1152]{1,0:T(8,128)S(1)}, f32[32,1152]{1,0:T(8,128)S(1)}, u32[]{:S(2)}, u32[]{:S(2)}) collective-permute-start(f32[32,1152]{1,0:T(8,128)S(1)} %add_add_fusion.refs_0_), channel_id=1, source_target_pairs={{0,1},{1,0},{2,3},{3,2},{4,5},{5,4},{6,7},{7,6},{8,9},{9,8},{10,11... | collective-permute-start | bytes 442376 | tf_op jit(solution)/shard_map/ppermute | solution.py:184
  88.3 6.2 %collective-permute-start.33 = (f32[128,128]{1,0:T(8,128)S(1)}, f32[128,128]{1,0:T(8,128)S(1)}, u32[]{:S(2)}, u32[]{:S(2)}) collective-permute-start(f32[128,128]{1,0:T(8,128)S(1)} %slice.198), channel_id=1, source_target_pairs={{0,1},{1,0},{2,3},{3,2},{4,5},{5,4},{6,7},{7,6},{8,9},{9,8},{10,11... | collective-permute-start | bytes 196616 | tf_op jit(solution)/shard_map/ppermute | solution.py:184
  (12 other events, 71.2 us)

commit v3 on v2

--- a/solution.py
+++ b/solution.py
@@ -239,7 +239,7 @@
     chans = width // parts
     share = parts // groups
     outer = parts * tiles
-    chunk = min(chans, 8)
+    chunk = min(chans, 32)
     size = tiles * chans
     half = width // groups // 2
     scale = 1.0 / math.sqrt(groups * parts * rows)
@@ -347,6 +347,7 @@
         for k in range(groups):
             for v in range(share):
                 dest = at_ref[1] ^ reversed_bits(k, groups)
+                dest = dest ^ (at_ref[0] // share)
                 row = (dest * share + ((at_ref[0] % share) ^ v)) * size
                 term_ref[k, v * size : (v + 1) * size, :] = (
                     k_ref[pl.ds(pl.multiple_of(row, size), size), :] * scale
@@ -367,7 +368,7 @@
 
     def mix_kernel(at_ref, tok_ref, cot_ref, win_ref, wout_ref, skip_ref, *refs):
         blocks = split_blocks(refs[:n_blocks])
-        out_ref, dproj_ref, keep_ref, give_ref, c_ref, part_ref = refs[n_blocks:]
+        mixed_ref, dproj_ref, keep_ref, give_ref, c_ref, part_ref = refs[n_blocks:]
         gate_out, gate_in, values, dmixed = projections(tok_ref, cot_ref, win_ref, wout_ref)
         gated = values * gate_in
         collect_signal(at_ref[0], c_ref, blocks)
@@ -375,7 +376,7 @@
         mixed = (conv * gate_out).astype(BF16)
         dproj = (dmixed * conv).astype(BF16)
         dproj_ref[...] = dproj
-        out_ref[...] = dot(mixed, wout_ref[...], ((0,), (0,))).astype(BF16)
+        mixed_ref[...] = mixed
         part_ref[:, :width] = dot(tok_ref[...], dproj, ((0,), (1,))) * scale
         part_ref[:, width : 2 * width] = dot(mixed, cot_ref[...]) * scale
         product = dmixed * gate_out * gated * scale
@@ -387,37 +388,53 @@
 
     early = 2 * width + LANES
     piece = jax.ShapeDtypeStruct((groups, half, early), F32)
-    output, dproj_first, early_keep, early_give = call(
+    mixed, dproj_first, early_keep, early_give = call(
         mix_kernel, (place, tok, cot, w_in, w_out, skip[None, :], *conv_blocks),
-        (jax.ShapeDtypeStruct((rows, width), BF16), jax.ShapeDtypeStruct((width, rows), BF16), piece, piece),
+        (jax.ShapeDtypeStruct((width, rows), BF16),) * 2 + (piece, piece),
         [signal, pltpu.VMEM((width, early), F32)], flops=14 * rows * width * width,
     )
     early_sum = reduce_rows(early_keep, early_give)
 
-    def last_kernel(at_ref, tok_ref, cot_ref, win_ref, wout_ref, skip_ref, dproj_ref, *refs):
+    def last_kernel(at_ref, tok_ref, cot_ref, win_ref, wout_ref, skip_ref, *refs):
         blocks = split_blocks(refs[:n_blocks])
-        din_ref, keep_ref, give_ref, c_ref, part_ref = refs[n_blocks:]
+        dproj_late_ref, keep_ref, give_ref, c_ref, part_ref = refs[n_blocks:]
         gate_out, gate_in, values, dmixed = projections(tok_ref, cot_ref, win_ref, wout_ref)
         collect_signal(at_ref[0], c_ref, blocks)
         dgated = c_ref[...] + skip_column(skip_ref, tiles) * (dmixed * gate_out)
         dproj = jnp.concatenate([(dgated * values).astype(BF16), (dgated * gate_in).astype(BF16)], axis=0)
         part_ref[...] = dot(tok_ref[...], dproj, ((0,), (1,))) * scale
         deal_part(at_ref, part_ref, keep_ref, give_ref)
-        dproj = jnp.concatenate([dproj_ref[...], dproj], axis=0)
+        dproj_late_ref[...] = dproj
+
+    piece = jax.ShapeDtypeStruct((groups, half, 2 * width), F32)
+    dproj_late, late_keep, late_give = call(
+        last_kernel, (place, tok, cot, w_in, w_out, skip[None, :], *dgated_blocks),
+        (jax.ShapeDtypeStruct((2 * width, rows), BF16), piece, piece),
+        [signal, pltpu.VMEM((width, 2 * width), F32)], flops=18 * rows * width * width,
+    )
+
+    def inputs_kernel(at_ref, win_ref, first_dproj_ref, late_dproj_ref, din_ref):
+        dproj = jnp.concatenate([first_dproj_ref[...], late_dproj_ref[...]], axis=0)
         din_ref[...] = dot(dproj, win_ref[...], ((0,), (1,))).astype(BF16)
 
-    piece = jax.ShapeDtypeStruct((groups, half, 2 * width), F32)
-    dinput, late_keep, late_give = call(
-        last_kernel, (place, tok, cot, w_in, w_out, skip[None, :], dproj_first, *dgated_blocks),
-        (jax.ShapeDtypeStruct((rows, width), BF16), piece, piece),
-        [signal, pltpu.VMEM((width, 2 * width), F32)], flops=18 * rows * width * width,
+    (dinput,) = call(
+        inputs_kernel, (place, w_in, dproj_first, dproj_late), (jax.ShapeDtypeStruct((rows, width), BF16),),
+        flops=6 * rows * width * width,
+    )
+
+    def outputs_kernel(at_ref, wout_ref, mixed_ref, out_ref):
+        out_ref[...] = dot(mixed_ref[...], wout_ref[...], ((0,), (0,))).astype(BF16)
+
+    (output,) = call(
+        outputs_kernel, (place, w_out, mixed), (jax.ShapeDtypeStruct((rows, width), BF16),),
+        flops=2 * rows * width * width,
     )
     late_sum = reduce_rows(late_keep, late_give)
 
     grad_sum = spread_rows(jnp.concatenate([early_sum, late_sum], axis=1))
     term_sum = halve(term_parts)
     swap = [
-        (i * parts + j, (j // share) * parts + i * share + j % share)
+        (i * parts + j, (j // share) * parts + (i ^ (j // share)) * share + j % share)
         for i in range(groups)
         for j in range(parts)
     ]

time: 96 us -> 93 us (0.969)
  the two profiles are of different devices: /device:TPU:5 before, /device:TPU:0 now
where the time goes in v3:
time: 93 us; the launch traced here: 92.6 us
  starting transfers between devices  38.4 us (41%)
  waiting for transfers between devices  32.5 us (35%)
  Pallas kernels  18.9 us (20%)
  local copies, waits for them, and re-layouts  1.17 us (1%)
  between operations  1.12 us (1%)
    ppermute x33, starting transfers between devices, mirror(): return lax.ppermute(x, axis, [(i, i ^ mask) for i in range(count)])  37.7 us
    ppermute x33, waiting for transfers between devices, mirror(): return lax.ppermute(x, axis, [(i, i ^ mask) for i in range(count)])  32.5 us
    pallas_call x9, Pallas kernels, call(): pl.pallas_call(body, out_shape=tuple(outs), in_specs=specs, out_specs=tup...  18.9 us
  transfers between devices with their start and end apart: 34, of which 15 were waited for; matrix products, arithmetic and copies ran while one was open for 1% of the time, Pallas kernels for 11%

profile of v3, /device:TPU:0, one launch (start us, length us, event | category | flops | bytes accessed | tf_op | source)
XLA Modules:
  0.0 92.6 jit_solution(11897828297448761434)
XLA Ops:
  1.6 3.1 %shard_map.154 = (f32[4,128,128]{2,1,0:T(8,128)S(1)}, f32[4,128,128]{2,1,0:T(8,128)S(1)}, f32[4,128,128]{2,1,0:T(8,128)S(1)}, f32[4,128,128]{2,1,0:T(8,128)S(1)}...) custom-call(s32[2]{0:T(128)S(1)} %pad_add_fusion.at_ref, f32[512,256]{1,0:T(8,128)} %refs_0_.1, ...), custom_call_target="tpu_custom_call" | custom-call | flops 268435456 | bytes 3145736 | tf_op jit(solution)/shard_map/pallas_call | solution.py:171
  6.5 3.9 %collective-permute-start.3 = (f32[2,128,128]{2,1,0:T(8,128)S(1)}, f32[2,128,128]{2,1,0:T(8,128)S(1)}, u32[]{:S(2)}, u32[]{:S(2)}) collective-permute-start(f32[2,128,128]{2,1,0:T(8,128)S(1)} %pad_maximum_fusion.3), channel_id=1, source_target_pairs={{0,6},{1,7},{2,4},{3,5},{4,2},{5,3},{6,0},{7,1},{8,14},{9,15},{10,... | collective-permute-start | bytes 393224 | tf_op jit(solution)/shard_map/ppermute | solution.py:184
  11.1 2.0 %collective-permute-start.5 = (f32[2,128,128]{2,1,0:T(8,128)S(1)}, f32[2,128,128]{2,1,0:T(8,128)S(1)}, u32[]{:S(2)}, u32[]{:S(2)}) collective-permute-start(f32[2,128,128]{2,1,0:T(8,128)S(1)} %pad_maximum_fusion.4), channel_id=1, source_target_pairs={{0,2},{1,3},{2,0},{3,1},{4,6},{5,7},{6,4},{7,5},{8,10},{9,11},{10,... | collective-permute-start | bytes 393224 | tf_op jit(solution)/shard_map/ppermute | solution.py:184
  13.2 1.6 %collective-permute-start.6 = (f32[2,128,128]{2,1,0:T(8,128)S(1)}, f32[2,128,128]{2,1,0:T(8,128)S(1)}, u32[]{:S(2)}, u32[]{:S(2)}) collective-permute-start(f32[2,128,128]{2,1,0:T(8,128)S(1)} %pad_maximum_fusion.5), channel_id=1, source_target_pairs={{0,4},{1,5},{2,6},{3,7},{4,0},{5,1},{6,2},{7,3},{8,12},{9,13},{10,... | collective-permute-start | bytes 393224 | tf_op jit(solution)/shard_map/ppermute | solution.py:184
  14.9 2.8 %collective-permute-start.7 = (f32[2,128,128]{2,1,0:T(8,128)S(1)}, f32[2,128,128]{2,1,0:T(8,128)S(1)}, u32[]{:S(2)}, u32[]{:S(2)}) collective-permute-start(f32[2,128,128]{2,1,0:T(8,128)S(1)} %pad_maximum_fusion.6), channel_id=1, source_target_pairs={{0,6},{1,7},{2,4},{3,5},{4,2},{5,3},{6,0},{7,1},{8,14},{9,15},{10,... | collective-permute-start | bytes 393224 | tf_op jit(solution)/shard_map/ppermute | solution.py:184
  18.8 1.4 %collective-permute-start.14 = (f32[2,128,128]{2,1,0:T(8,128)S(1)}, f32[2,128,128]{2,1,0:T(8,128)S(1)}, u32[]{:S(2)}, u32[]{:S(2)}) collective-permute-start(f32[2,128,128]{2,1,0:T(8,128)S(1)} %pad_maximum_fusion.11), channel_id=1, source_target_pairs={{0,4},{1,5},{2,6},{3,7},{4,0},{5,1},{6,2},{7,3},{8,12},{9,13},{10,... | collective-permute-start | bytes 393224 | tf_op jit(solution)/shard_map/ppermute | solution.py:184
  20.9 1.4 %collective-permute-start.15 = (f32[2,128,128]{2,1,0:T(8,128)S(1)}, f32[2,128,128]{2,1,0:T(8,128)S(1)}, u32[]{:S(2)}, u32[]{:S(2)}) collective-permute-start(f32[2,128,128]{2,1,0:T(8,128)S(1)} %pad_maximum_fusion.12), channel_id=1, source_target_pairs={{0,6},{1,7},{2,4},{3,5},{4,2},{5,3},{6,0},{7,1},{8,14},{9,15},{10,... | collective-permute-start | bytes 393224 | tf_op jit(solution)/shard_map/ppermute | solution.py:184
  22.3 1.5 %shard_map.155.h_ref = f32[1024,256]{1,0:T(8,128)S(1)} custom-call(s32[2]{0:T(128)S(1)} %pad_add_fusion.at_ref, bf16[64,96]{1,0:T(8,128)(2,1)S(1)} %copy-done.6, f32[2,32,128]{2,1,0:T(8,128)S(1)} %copy-done.5, bf16[2,256,256]{2,1,0:T(8,128)(2,1)S(1)} %copy-done.4, f32[4,128,128]{2,1,0:T(8,128)S(1)} %get-tuple-element.29.refs_0_, ...), custom_call_target="tpu_custom_call" | custom-call | flops 503316480 | bytes 2273288 | tf_op jit(solution)/shard_map/pallas_call | solution.py:171
  24.0 2.9 %shard_map.156 = (f32[1024,256]{1,0:T(8,128)S(1)}, f32[4,128,128]{2,1,0:T(8,128)S(1)}, f32[4,128,128]{2,1,0:T(8,128)S(1)}) custom-call(s32[2]{0:T(128)S(1)} %pad_add_fusion.at_ref, bf16[64,96]{1,0:T(8,128)(2,1)S(1)} %copy-done.6, bf16[32,192]{1,0:T(8,128)(2,1)S(1)} %copy-done.9, f32[2,32,128]{2,1,0:T(8,128)S(1)} %copy-done.5, ...), custom_call_target="tpu_custom_call" | custom-call | flops 1006632960 | bytes 4120584 | tf_op jit(solution)/shard_map/pallas_call | solution.py:171
  26.9 1.3 %collective-permute-done.15.refs_4_ = f32[2,128,128]{2,1,0:T(8,128)S(1)} collective-permute-done((f32[2,128,128]{2,1,0:T(8,128)S(1)}, f32[2,128,128]{2,1,0:T(8,128)S(1)}, u32[]{:S(2)}, u32[]{:S(2)}) %collective-permute-start.15) | collective-permute-done | bytes 131104 | tf_op jit(solution)/shard_map/ppermute | solution.py:184
  28.2 4.1 %shard_map.159 = (f32[4,128,128]{2,1,0:T(8,128)S(1)}, f32[4,128,128]{2,1,0:T(8,128)S(1)}, f32[4,256,128]{2,1,0:T(8,128)S(1)}) custom-call(s32[2]{0:T(128)S(1)} %pad_add_fusion.at_ref, bf16[64,96]{1,0:T(8,128)(2,1)S(1)} %copy-done.6, bf16[32,192]{1,0:T(8,128)(2,1)S(1)} %copy-done.9, f32[2,32,128]{2,1,0:T(8,128)S(1)} %copy-done.5, ...), custom_call_target="tpu_custom_call" | custom-call | flops 1509949440 | bytes 4644872 | tf_op jit(solution)/shard_map/pallas_call | solution.py:171
  32.4 1.8 %collective-permute-start.30 = (f32[2,256,128]{2,1,0:T(8,128)S(1)}, f32[2,256,128]{2,1,0:T(8,128)S(1)}, u32[]{:S(2)}, u32[]{:S(2)}) collective-permute-start(f32[2,256,128]{2,1,0:T(8,128)S(1)} %slice.169), channel_id=1, source_target_pairs={{0,8},{8,0},{16,24},{24,16},{1,9},{9,1},{17,25},{25,17},{2,10},{10... | collective-permute-start | bytes 786440 | tf_op jit(solution)/shard_map/ppermute | solution.py:184
  34.5 1.6 %collective-permute-start.17 = (f32[2,128,128]{2,1,0:T(8,128)S(1)}, f32[2,128,128]{2,1,0:T(8,128)S(1)}, u32[]{:S(2)}, u32[]{:S(2)}) collective-permute-start(f32[2,128,128]{2,1,0:T(8,128)S(1)} %pad_maximum_fusion.13), channel_id=1, source_target_pairs={{0,2},{1,3},{2,0},{3,1},{4,6},{5,7},{6,4},{7,5},{8,10},{9,11},{10,... | collective-permute-start | bytes 393224 | tf_op jit(solution)/shard_map/ppermute | solution.py:184
  36.1 1.6 %collective-permute-start.18 = (f32[2,128,128]{2,1,0:T(8,128)S(1)}, f32[2,128,128]{2,1,0:T(8,128)S(1)}, u32[]{:S(2)}, u32[]{:S(2)}) collective-permute-start(f32[2,128,128]{2,1,0:T(8,128)S(1)} %pad_maximum_fusion.14), channel_id=1, source_target_pairs={{0,4},{1,5},{2,6},{3,7},{4,0},{5,1},{6,2},{7,3},{8,12},{9,13},{10,... | collective-permute-start | bytes 393224 | tf_op jit(solution)/shard_map/ppermute | solution.py:184
  38.3 1.6 %collective-permute-start.9 = (f32[2,128,128]{2,1,0:T(8,128)S(1)}, f32[2,128,128]{2,1,0:T(8,128)S(1)}, u32[]{:S(2)}, u32[]{:S(2)}) collective-permute-start(f32[2,128,128]{2,1,0:T(8,128)S(1)} %pad_maximum_fusion.7), channel_id=1, source_target_pairs={{0,2},{1,3},{2,0},{3,1},{4,6},{5,7},{6,4},{7,5},{8,10},{9,11},{10,... | collective-permute-start | bytes 393224 | tf_op jit(solution)/shard_map/ppermute | solution.py:184
  40.5 1.6 %collective-permute-start.10 = (f32[2,128,128]{2,1,0:T(8,128)S(1)}, f32[2,128,128]{2,1,0:T(8,128)S(1)}, u32[]{:S(2)}, u32[]{:S(2)}) collective-permute-start(f32[2,128,128]{2,1,0:T(8,128)S(1)} %pad_maximum_fusion.8), channel_id=1, source_target_pairs={{0,4},{1,5},{2,6},{3,7},{4,0},{5,1},{6,2},{7,3},{8,12},{9,13},{10,... | collective-permute-start | bytes 393224 | tf_op jit(solution)/shard_map/ppermute | solution.py:184
  42.1 2.4 %collective-permute-done.18.refs_3_ = f32[2,128,128]{2,1,0:T(8,128)S(1)} collective-permute-done((f32[2,128,128]{2,1,0:T(8,128)S(1)}, f32[2,128,128]{2,1,0:T(8,128)S(1)}, u32[]{:S(2)}, u32[]{:S(2)}) %collective-permute-start.18) | collective-permute-done | bytes 131104 | tf_op jit(solution)/shard_map/ppermute | solution.py:184
  45.2 1.4 %shard_map.160 = (bf16[512,512]{1,0:T(8,128)(2,1)S(1)}, f32[4,32,512]{2,1,0:T(8,128)S(1)}, f32[4,32,512]{2,1,0:T(8,128)S(1)}) custom-call(s32[2]{0:T(128)S(1)} %pad_add_fusion.at_ref, bf16[512,256]{1,0:T(8,128)(2,1)S(1)} %bitcast.17, bf16[512,256]{1,0:T(8,128)(2,1)S(1)} %bitcast.20, bf16[256,768]{1,0:T(8,128)(2,1)S(1)} %copy-done, ...), custom_call_target="tpu_custom_call" | custom-call | flops 603979776 | bytes 3015688 | tf_op jit(solution)/shard_map/pallas_call | solution.py:171
  47.8 5.7 %collective-permute-done.11.refs_4_ = f32[2,128,128]{2,1,0:T(8,128)S(1)} collective-permute-done((f32[2,128,128]{2,1,0:T(8,128)S(1)}, f32[2,128,128]{2,1,0:T(8,128)S(1)}, u32[]{:S(2)}, u32[]{:S(2)}) %collective-permute-start.11) | collective-permute-done | bytes 131104 | tf_op jit(solution)/shard_map/ppermute | solution.py:184
  53.5 1.4 %shard_map.157 = (bf16[256,512]{1,0:T(8,128)(2,1)S(1)}, bf16[256,512]{1,0:T(8,128)(2,1)S(1)}, f32[4,32,640]{2,1,0:T(8,128)S(1)}, f32[4,32,640]{2,1,0:T(8,128)S(1)}) custom-call(s32[2]{0:T(128)S(1)} %pad_add_fusion.at_ref, bf16[512,256]{1,0:T(8,128)(2,1)S(1)} %bitcast.18, bf16[512,256]{1,0:T(8,128)(2,1)S(1)} %bitcast.21, bf16[256,768]{1,0:T(8,128)(2,1)S(1)} %copy-done, ...), custom_call_target="tpu_custom_call" | custom-call | flops 469762048 | bytes 3146760 | tf_op jit(solution)/shard_map/pallas_call | solution.py:171
  56.4 2.7 %collective-permute-start.31 = (f32[1,256,128]{2,1,0:T(8,128)S(1)}, f32[1,256,128]{2,1,0:T(8,128)S(1)}, u32[]{:S(2)}, u32[]{:S(2)}) collective-permute-start(f32[1,256,128]{2,1,0:T(8,128)S(1)} %slice.197), channel_id=1, source_target_pairs={{0,16},{8,24},{16,0},{24,8},{1,17},{9,25},{17,1},{25,9},{2,18},{10... | collective-permute-start | bytes 393224 | tf_op jit(solution)/shard_map/ppermute | solution.py:184
  60.1 4.3 %collective-permute-done.24 = f32[2,32,512]{2,1,0:T(8,128)S(1)} collective-permute-done((f32[2,32,512]{2,1,0:T(8,128)S(1)}, f32[2,32,512]{2,1,0:T(8,128)S(1)}, u32[]{:S(2)}, u32[]{:S(2)}) %collective-permute-start.24) | collective-permute-done | bytes 131104 | tf_op jit(solution)/shard_map/ppermute | solution.py:184
  64.5 3.6 %collective-permute-done.21 = f32[2,32,640]{2,1,0:T(8,128)S(1)} collective-permute-done((f32[2,32,640]{2,1,0:T(8,128)S(1)}, f32[2,32,640]{2,1,0:T(8,128)S(1)}, u32[]{:S(2)}, u32[]{:S(2)}) %collective-permute-start.21) | collective-permute-done | bytes 163872 | tf_op jit(solution)/shard_map/ppermute | solution.py:184
  68.2 2.4 %collective-permute-start.22 = (f32[1,32,640]{2,1,0:T(8,128)S(1)}, f32[1,32,640]{2,1,0:T(8,128)S(1)}, u32[]{:S(2)}, u32[]{:S(2)}) collective-permute-start(f32[1,32,640]{2,1,0:T(8,128)S(1)} %slice.191), channel_id=1, source_target_pairs={{0,16},{8,24},{16,0},{24,8},{1,17},{9,25},{17,1},{25,9},{2,18},{10... | collective-permute-start | bytes 245768 | tf_op jit(solution)/shard_map/ppermute | solution.py:184
  71.2 3.7 %collective-permute-done.22 = f32[1,32,640]{2,1,0:T(8,128)S(1)} collective-permute-done((f32[1,32,640]{2,1,0:T(8,128)S(1)}, f32[1,32,640]{2,1,0:T(8,128)S(1)}, u32[]{:S(2)}, u32[]{:S(2)}) %collective-permute-start.22) | collective-permute-done | bytes 81952 | tf_op jit(solution)/shard_map/ppermute | solution.py:184
  74.9 1.8 %collective-permute-start.27 = (f32[32,1152]{1,0:T(8,128)S(1)}, f32[32,1152]{1,0:T(8,128)S(1)}, u32[]{:S(2)}, u32[]{:S(2)}) collective-permute-start(f32[32,1152]{1,0:T(8,128)S(1)} %pad_maximum_fusion), channel_id=1, source_target_pairs={{0,4},{1,5},{2,6},{3,7},{4,0},{5,1},{6,2},{7,3},{8,12},{9,13},{10,... | collective-permute-start | bytes 442376 | tf_op jit(solution)/shard_map/ppermute | solution.py:184
  79.1 2.6 %collective-permute-done.27 = f32[32,1152]{1,0:T(8,128)S(1)} collective-permute-done((f32[32,1152]{1,0:T(8,128)S(1)}, f32[32,1152]{1,0:T(8,128)S(1)}, u32[]{:S(2)}, u32[]{:S(2)}) %collective-permute-start.27) | collective-permute-done | bytes 147488 | tf_op jit(solution)/shard_map/ppermute | solution.py:184
  81.7 1.2 %collective-permute-done.28 = f32[32,1152]{1,0:T(8,128)S(1)} collective-permute-done((f32[32,1152]{1,0:T(8,128)S(1)}, f32[32,1152]{1,0:T(8,128)S(1)}, u32[]{:S(2)}, u32[]{:S(2)}) %collective-permute-start.28) | collective-permute-done | bytes 147488 | tf_op jit(solution)/shard_map/ppermute | solution.py:184
  83.0 4.4 %collective-permute-done.26 = f32[32,1152]{1,0:T(8,128)S(1)} collective-permute-done((f32[32,1152]{1,0:T(8,128)S(1)}, f32[32,1152]{1,0:T(8,128)S(1)}, u32[]{:S(2)}, u32[]{:S(2)}) %collective-permute-start.26) | collective-permute-done | bytes 147488 | tf_op jit(solution)/shard_map/ppermute | solution.py:184
  88.1 1.5 %shard_map.158 = bf16[512,256]{1,0:T(8,128)(2,1)} custom-call(s32[2]{0:T(128)S(1)} %pad_add_fusion.at_ref, bf16[256,256]{1,0:T(8,128)(2,1)S(1)} %copy-done.1, bf16[256,512]{1,0:T(8,128)(2,1)S(1)} %get-tuple-element.35.mixed_ref), custom_call_target="tpu_custom_call" | custom-call | flops 67108864 | bytes 655368 | tf_op jit(solution)/shard_map/pallas_call | solution.py:171
  89.6 1.7 %shard_map.161 = bf16[512,256]{1,0:T(8,128)(2,1)} custom-call(s32[2]{0:T(128)S(1)} %pad_add_fusion.at_ref, bf16[256,768]{1,0:T(8,128)(2,1)S(1)} %copy-done, bf16[256,512]{1,0:T(8,128)(2,1)S(1)} %get-tuple-element.36.first_dproj_ref, bf16[512,512]{1,0:T(8,128)(2,1)S(1)} %get-tuple-element.42.late_dproj_ref), custom_call_target="tpu_custom_call" | custom-call | flops 201326592 | bytes 1441800 | tf_op jit(solution)/shard_map/pallas_call | solution.py:171
  91.2 1.3 %shard_map.162 = (f32[64,768]{1,0:T(8,128)}, f32[64,256]{1,0:T(8,128)}, f32[64,512]{1,0:T(8,128)}, f32[1,64]{1,0:T(1,128)}) custom-call(s32[2]{0:T(128)S(1)} %pad_add_fusion.at_ref, f32[32,1152]{1,0:T(8,128)S(1)} %add_add_fusion.refs_0_, f32[32,1152]{1,0:T(8,128)S(1)} %collective-permute-done.29.refs_1_, f32[2,128,128]{2,1,0:T(8,128)S(1)} %bitcast.22, ...), custom_call_target="tpu_custom_call" | custom-call | flops 131072 | bytes 885000 | tf_op jit(solution)/shard_map/pallas_call | solution.py:171
  (107 shorter events, 14.9 us)
Async XLA Ops:
  5.3 5.8 %collective-permute-start.4 = (f32[4,128,128]{2,1,0:T(8,128)S(1)}, f32[4,128,128]{2,1,0:T(8,128)S(1)}, u32[]{:S(2)}, u32[]{:S(2)}) collective-permute-start(f32[4,128,128]{2,1,0:T(8,128)S(1)} %get-tuple-element.32), channel_id=1, source_target_pairs={{0,1},{1,0},{2,3},{3,2},{4,5},{5,4},{6,7},{7,6},{8,9},{9,8},{10,11... | collective-permute-start | bytes 786440 | tf_op jit(solution)/shard_map/ppermute | solution.py:184
  5.4 7.8 %collective-permute-start.12 = (f32[4,128,128]{2,1,0:T(8,128)}, f32[4,128,128]{2,1,0:T(8,128)S(1)}, u32[]{:S(2)}, u32[]{:S(2)}) collective-permute-start(f32[4,128,128]{2,1,0:T(8,128)} %get-tuple-element.39), channel_id=1, source_target_pairs={{0,1},{1,0},{2,3},{3,2},{4,5},{5,4},{6,7},{7,6},{8,9},{9,8},{10,11... | collective-permute-start | bytes 786440 | tf_op jit(solution)/shard_map/ppermute | solution.py:184
  6.5 8.4 %collective-permute-start.3 = (f32[2,128,128]{2,1,0:T(8,128)S(1)}, f32[2,128,128]{2,1,0:T(8,128)S(1)}, u32[]{:S(2)}, u32[]{:S(2)}) collective-permute-start(f32[2,128,128]{2,1,0:T(8,128)S(1)} %pad_maximum_fusion.3), channel_id=1, source_target_pairs={{0,6},{1,7},{2,4},{3,5},{4,2},{5,3},{6,0},{7,1},{8,14},{9,15},{10,... | collective-permute-start | bytes 393224 | tf_op jit(solution)/shard_map/ppermute | solution.py:184
  10.4 7.3 %collective-permute-start.2 = (f32[2,128,128]{2,1,0:T(8,128)S(1)}, f32[2,128,128]{2,1,0:T(8,128)S(1)}, u32[]{:S(2)}, u32[]{:S(2)}) collective-permute-start(f32[2,128,128]{2,1,0:T(8,128)S(1)} %pad_maximum_fusion.2), channel_id=1, source_target_pairs={{0,4},{1,5},{2,6},{3,7},{4,0},{5,1},{6,2},{7,3},{8,12},{9,13},{10,... | collective-permute-start | bytes 393224 | tf_op jit(solution)/shard_map/ppermute | solution.py:184
  11.0 7.8 %collective-permute-start.1 = (f32[2,128,128]{2,1,0:T(8,128)S(1)}, f32[2,128,128]{2,1,0:T(8,128)S(1)}, u32[]{:S(2)}, u32[]{:S(2)}) collective-permute-start(f32[2,128,128]{2,1,0:T(8,128)S(1)} %pad_maximum_fusion.1), channel_id=1, source_target_pairs={{0,2},{1,3},{2,0},{3,1},{4,6},{5,7},{6,4},{7,5},{8,10},{9,11},{10,... | collective-permute-start | bytes 393224 | tf_op jit(solution)/shard_map/ppermute | solution.py:184
  11.1 9.7 %collective-permute-start.5 = (f32[2,128,128]{2,1,0:T(8,128)S(1)}, f32[2,128,128]{2,1,0:T(8,128)S(1)}, u32[]{:S(2)}, u32[]{:S(2)}) collective-permute-start(f32[2,128,128]{2,1,0:T(8,128)S(1)} %pad_maximum_fusion.4), channel_id=1, source_target_pairs={{0,2},{1,3},{2,0},{3,1},{4,6},{5,7},{6,4},{7,5},{8,10},{9,11},{10,... | collective-permute-start | bytes 393224 | tf_op jit(solution)/shard_map/ppermute | solution.py:184
  13.2 10.7 %collective-permute-start.6 = (f32[2,128,128]{2,1,0:T(8,128)S(1)}, f32[2,128,128]{2,1,0:T(8,128)S(1)}, u32[]{:S(2)}, u32[]{:S(2)}) collective-permute-start(f32[2,128,128]{2,1,0:T(8,128)S(1)} %pad_maximum_fusion.5), channel_id=1, source_target_pairs={{0,4},{1,5},{2,6},{3,7},{4,0},{5,1},{6,2},{7,3},{8,12},{9,13},{10,... | collective-permute-start | bytes 393224 | tf_op jit(solution)/shard_map/ppermute | solution.py:184
  14.9 9.1 %collective-permute-start.7 = (f32[2,128,128]{2,1,0:T(8,128)S(1)}, f32[2,128,128]{2,1,0:T(8,128)S(1)}, u32[]{:S(2)}, u32[]{:S(2)}) collective-permute-start(f32[2,128,128]{2,1,0:T(8,128)S(1)} %pad_maximum_fusion.6), channel_id=1, source_target_pairs={{0,6},{1,7},{2,4},{3,5},{4,2},{5,3},{6,0},{7,1},{8,14},{9,15},{10,... | collective-permute-start | bytes 393224 | tf_op jit(solution)/shard_map/ppermute | solution.py:184
  17.7 9.1 %collective-permute-start.13 = (f32[2,128,128]{2,1,0:T(8,128)S(1)}, f32[2,128,128]{2,1,0:T(8,128)S(1)}, u32[]{:S(2)}, u32[]{:S(2)}) collective-permute-start(f32[2,128,128]{2,1,0:T(8,128)S(1)} %pad_maximum_fusion.10), channel_id=1, source_target_pairs={{0,2},{1,3},{2,0},{3,1},{4,6},{5,7},{6,4},{7,5},{8,10},{9,11},{10,... | collective-permute-start | bytes 393224 | tf_op jit(solution)/shard_map/ppermute | solution.py:184
  18.8 8.1 %collective-permute-start.14 = (f32[2,128,128]{2,1,0:T(8,128)S(1)}, f32[2,128,128]{2,1,0:T(8,128)S(1)}, u32[]{:S(2)}, u32[]{:S(2)}) collective-permute-start(f32[2,128,128]{2,1,0:T(8,128)S(1)} %pad_maximum_fusion.11), channel_id=1, source_target_pairs={{0,4},{1,5},{2,6},{3,7},{4,0},{5,1},{6,2},{7,3},{8,12},{9,13},{10,... | collective-permute-start | bytes 393224 | tf_op jit(solution)/shard_map/ppermute | solution.py:184
  20.9 7.3 %collective-permute-start.15 = (f32[2,128,128]{2,1,0:T(8,128)S(1)}, f32[2,128,128]{2,1,0:T(8,128)S(1)}, u32[]{:S(2)}, u32[]{:S(2)}) collective-permute-start(f32[2,128,128]{2,1,0:T(8,128)S(1)} %pad_maximum_fusion.12), channel_id=1, source_target_pairs={{0,6},{1,7},{2,4},{3,5},{4,2},{5,3},{6,0},{7,1},{8,14},{9,15},{10,... | collective-permute-start | bytes 393224 | tf_op jit(solution)/shard_map/ppermute | solution.py:184
  32.4 24.0 %collective-permute-start.30 = (f32[2,256,128]{2,1,0:T(8,128)S(1)}, f32[2,256,128]{2,1,0:T(8,128)S(1)}, u32[]{:S(2)}, u32[]{:S(2)}) collective-permute-start(f32[2,256,128]{2,1,0:T(8,128)S(1)} %slice.169), channel_id=1, source_target_pairs={{0,8},{8,0},{16,24},{24,16},{1,9},{9,1},{17,25},{25,17},{2,10},{10... | collective-permute-start | bytes 786440 | tf_op jit(solution)/shard_map/ppermute | solution.py:184
  34.2 4.0 %collective-permute-start.8 = (f32[4,128,128]{2,1,0:T(8,128)S(1)}, f32[4,128,128]{2,1,0:T(8,128)S(1)}, u32[]{:S(2)}, u32[]{:S(2)}) collective-permute-start(f32[4,128,128]{2,1,0:T(8,128)S(1)} %get-tuple-element.34), channel_id=1, source_target_pairs={{0,1},{1,0},{2,3},{3,2},{4,5},{5,4},{6,7},{7,6},{8,9},{9,8},{10,11... | collective-permute-start | bytes 786440 | tf_op jit(solution)/shard_map/ppermute | solution.py:184
  34.5 6.0 %collective-permute-start.17 = (f32[2,128,128]{2,1,0:T(8,128)S(1)}, f32[2,128,128]{2,1,0:T(8,128)S(1)}, u32[]{:S(2)}, u32[]{:S(2)}) collective-permute-start(f32[2,128,128]{2,1,0:T(8,128)S(1)} %pad_maximum_fusion.13), channel_id=1, source_target_pairs={{0,2},{1,3},{2,0},{3,1},{4,6},{5,7},{6,4},{7,5},{8,10},{9,11},{10,... | collective-permute-start | bytes 393224 | tf_op jit(solution)/shard_map/ppermute | solution.py:184
  36.1 8.3 %collective-permute-start.18 = (f32[2,128,128]{2,1,0:T(8,128)S(1)}, f32[2,128,128]{2,1,0:T(8,128)S(1)}, u32[]{:S(2)}, u32[]{:S(2)}) collective-permute-start(f32[2,128,128]{2,1,0:T(8,128)S(1)} %pad_maximum_fusion.14), channel_id=1, source_target_pairs={{0,4},{1,5},{2,6},{3,7},{4,0},{5,1},{6,2},{7,3},{8,12},{9,13},{10,... | collective-permute-start | bytes 393224 | tf_op jit(solution)/shard_map/ppermute | solution.py:184
  37.8 7.4 %collective-permute-start.19 = (f32[2,128,128]{2,1,0:T(8,128)S(1)}, f32[2,128,128]{2,1,0:T(8,128)S(1)}, u32[]{:S(2)}, u32[]{:S(2)}) collective-permute-start(f32[2,128,128]{2,1,0:T(8,128)S(1)} %pad_maximum_fusion.15), channel_id=1, source_target_pairs={{0,6},{1,7},{2,4},{3,5},{4,2},{5,3},{6,0},{7,1},{8,14},{9,15},{10,... | collective-permute-start | bytes 393224 | tf_op jit(solution)/shard_map/ppermute | solution.py:184
  38.3 9.5 %collective-permute-start.9 = (f32[2,128,128]{2,1,0:T(8,128)S(1)}, f32[2,128,128]{2,1,0:T(8,128)S(1)}, u32[]{:S(2)}, u32[]{:S(2)}) collective-permute-start(f32[2,128,128]{2,1,0:T(8,128)S(1)} %pad_maximum_fusion.7), channel_id=1, source_target_pairs={{0,2},{1,3},{2,0},{3,1},{4,6},{5,7},{6,4},{7,5},{8,10},{9,11},{10,... | collective-permute-start | bytes 393224 | tf_op jit(solution)/shard_map/ppermute | solution.py:184
  40.5 7.4 %collective-permute-start.10 = (f32[2,128,128]{2,1,0:T(8,128)S(1)}, f32[2,128,128]{2,1,0:T(8,128)S(1)}, u32[]{:S(2)}, u32[]{:S(2)}) collective-permute-start(f32[2,128,128]{2,1,0:T(8,128)S(1)} %pad_maximum_fusion.8), channel_id=1, source_target_pairs={{0,4},{1,5},{2,6},{3,7},{4,0},{5,1},{6,2},{7,3},{8,12},{9,13},{10,... | collective-permute-start | bytes 393224 | tf_op jit(solution)/shard_map/ppermute | solution.py:184
  46.6 8.5 %collective-permute-start.23 = (f32[4,32,512]{2,1,0:T(8,128)S(1)}, f32[4,32,512]{2,1,0:T(8,128)S(1)}, u32[]{:S(2)}, u32[]{:S(2)}) collective-permute-start(f32[4,32,512]{2,1,0:T(8,128)S(1)} %get-tuple-element.46), channel_id=1, source_target_pairs={{0,1},{1,0},{2,3},{3,2},{4,5},{5,4},{6,7},{7,6},{8,9},{9,8},{10,11... | collective-permute-start | bytes 786440 | tf_op jit(solution)/shard_map/ppermute | solution.py:184
  46.7 6.9 %collective-permute-start.11 = (f32[2,128,128]{2,1,0:T(8,128)S(1)}, f32[2,128,128]{2,1,0:T(8,128)S(1)}, u32[]{:S(2)}, u32[]{:S(2)}) collective-permute-start(f32[2,128,128]{2,1,0:T(8,128)S(1)} %pad_maximum_fusion.9), channel_id=1, source_target_pairs={{0,6},{1,7},{2,4},{3,5},{4,2},{5,3},{6,0},{7,1},{8,14},{9,15},{10,... | collective-permute-start | bytes 393224 | tf_op jit(solution)/shard_map/ppermute | solution.py:184
  55.0 4.1 %collective-permute-start.20 = (f32[4,32,640]{2,1,0:T(8,128)S(1)}, f32[4,32,640]{2,1,0:T(8,128)S(1)}, u32[]{:S(2)}, u32[]{:S(2)}) collective-permute-start(f32[4,32,640]{2,1,0:T(8,128)S(1)} %get-tuple-element.44), channel_id=1, source_target_pairs={{0,1},{1,0},{2,3},{3,2},{4,5},{5,4},{6,7},{7,6},{8,9},{9,8},{10,11... | collective-permute-start | bytes 983048 | tf_op jit(solution)/shard_map/ppermute | solution.py:184
  55.2 9.2 %collective-permute-start.24 = (f32[2,32,512]{2,1,0:T(8,128)S(1)}, f32[2,32,512]{2,1,0:T(8,128)S(1)}, u32[]{:S(2)}, u32[]{:S(2)}) collective-permute-start(f32[2,32,512]{2,1,0:T(8,128)S(1)} %slice.193), channel_id=1, source_target_pairs={{0,8},{8,0},{16,24},{24,16},{1,9},{9,1},{17,25},{25,17},{2,10},{10... | collective-permute-start | bytes 393224 | tf_op jit(solution)/shard_map/ppermute | solution.py:184
  56.4 22.0 %collective-permute-start.31 = (f32[1,256,128]{2,1,0:T(8,128)S(1)}, f32[1,256,128]{2,1,0:T(8,128)S(1)}, u32[]{:S(2)}, u32[]{:S(2)}) collective-permute-start(f32[1,256,128]{2,1,0:T(8,128)S(1)} %slice.197), channel_id=1, source_target_pairs={{0,16},{8,24},{16,0},{24,8},{1,17},{9,25},{17,1},{25,9},{2,18},{10... | collective-permute-start | bytes 393224 | tf_op jit(solution)/shard_map/ppermute | solution.py:184
  59.1 9.0 %collective-permute-start.21 = (f32[2,32,640]{2,1,0:T(8,128)S(1)}, f32[2,32,640]{2,1,0:T(8,128)S(1)}, u32[]{:S(2)}, u32[]{:S(2)}) collective-permute-start(f32[2,32,640]{2,1,0:T(8,128)S(1)} %slice.189), channel_id=1, source_target_pairs={{0,8},{8,0},{16,24},{24,16},{1,9},{9,1},{17,25},{25,17},{2,10},{10... | collective-permute-start | bytes 491528 | tf_op jit(solution)/shard_map/ppermute | solution.py:184
  64.4 6.7 %collective-permute-start.25 = (f32[1,32,512]{2,1,0:T(8,128)S(1)}, f32[1,32,512]{2,1,0:T(8,128)S(1)}, u32[]{:S(2)}, u32[]{:S(2)}) collective-permute-start(f32[1,32,512]{2,1,0:T(8,128)S(1)} %slice.195), channel_id=1, source_target_pairs={{0,16},{8,24},{16,0},{24,8},{1,17},{9,25},{17,1},{25,9},{2,18},{10... | collective-permute-start | bytes 196616 | tf_op jit(solution)/shard_map/ppermute | solution.py:184
  68.2 6.7 %collective-permute-start.22 = (f32[1,32,640]{2,1,0:T(8,128)S(1)}, f32[1,32,640]{2,1,0:T(8,128)S(1)}, u32[]{:S(2)}, u32[]{:S(2)}) collective-permute-start(f32[1,32,640]{2,1,0:T(8,128)S(1)} %slice.191), channel_id=1, source_target_pairs={{0,16},{8,24},{16,0},{24,8},{1,17},{9,25},{17,1},{25,9},{2,18},{10... | collective-permute-start | bytes 245768 | tf_op jit(solution)/shard_map/ppermute | solution.py:184
  74.9 6.8 %collective-permute-start.27 = (f32[32,1152]{1,0:T(8,128)S(1)}, f32[32,1152]{1,0:T(8,128)S(1)}, u32[]{:S(2)}, u32[]{:S(2)}) collective-permute-start(f32[32,1152]{1,0:T(8,128)S(1)} %pad_maximum_fusion), channel_id=1, source_target_pairs={{0,4},{1,5},{2,6},{3,7},{4,0},{5,1},{6,2},{7,3},{8,12},{9,13},{10,... | collective-permute-start | bytes 442376 | tf_op jit(solution)/shard_map/ppermute | solution.py:184
  76.7 6.2 %collective-permute-start.28 = (f32[32,1152]{1,0:T(8,128)S(1)}, f32[32,1152]{1,0:T(8,128)S(1)}, u32[]{:S(2)}, u32[]{:S(2)}) collective-permute-start(f32[32,1152]{1,0:T(8,128)S(1)} %pad_maximum_fusion), channel_id=1, source_target_pairs={{0,6},{1,7},{2,4},{3,5},{4,2},{5,3},{6,0},{7,1},{8,14},{9,15},{10,... | collective-permute-start | bytes 442376 | tf_op jit(solution)/shard_map/ppermute | solution.py:184
  77.5 9.8 %collective-permute-start.26 = (f32[32,1152]{1,0:T(8,128)S(1)}, f32[32,1152]{1,0:T(8,128)S(1)}, u32[]{:S(2)}, u32[]{:S(2)}) collective-permute-start(f32[32,1152]{1,0:T(8,128)S(1)} %pad_maximum_fusion), channel_id=1, source_target_pairs={{0,2},{1,3},{2,0},{3,1},{4,6},{5,7},{6,4},{7,5},{8,10},{9,11},{10,... | collective-permute-start | bytes 442376 | tf_op jit(solution)/shard_map/ppermute | solution.py:184
  78.5 9.0 %collective-permute-start.32 = (f32[256,128]{1,0:T(8,128)S(1)}, f32[256,128]{1,0:T(8,128)S(1)}, u32[]{:S(2)}, u32[]{:S(2)}) collective-permute-start(f32[256,128]{1,0:T(8,128)S(1)} %fusion), channel_id=1, source_target_pairs={{0,0},{1,1},{2,10},{3,11},{4,20},{5,21},{6,30},{7,31},{8,2},{9,3},... | collective-permute-start | bytes 393224 | tf_op jit(solution)/shard_map/ppermute | solution.py:441
  87.4 3.8 %collective-permute-start.29 = (f32[32,1152]{1,0:T(8,128)S(1)}, f32[32,1152]{1,0:T(8,128)S(1)}, u32[]{:S(2)}, u32[]{:S(2)}) collective-permute-start(f32[32,1152]{1,0:T(8,128)S(1)} %add_add_fusion.refs_0_), channel_id=1, source_target_pairs={{0,1},{1,0},{2,3},{3,2},{4,5},{5,4},{6,7},{7,6},{8,9},{9,8},{10,11... | collective-permute-start | bytes 442376 | tf_op jit(solution)/shard_map/ppermute | solution.py:184
  87.5 3.7 %collective-permute-start.33 = (f32[128,128]{1,0:T(8,128)S(1)}, f32[128,128]{1,0:T(8,128)S(1)}, u32[]{:S(2)}, u32[]{:S(2)}) collective-permute-start(f32[128,128]{1,0:T(8,128)S(1)} %slice.198), channel_id=1, source_target_pairs={{0,1},{1,0},{2,3},{3,2},{4,5},{5,4},{6,7},{7,6},{8,9},{9,8},{10,11... | collective-permute-start | bytes 196616 | tf_op jit(solution)/shard_map/ppermute | solution.py:184
  (12 other events, 60.6 us)

commit v4 on v3

--- a/solution.py
+++ b/solution.py
@@ -14,7 +14,6 @@
 BF16 = jnp.bfloat16
 SHIFT = 0.25
 VMEM_GRANT = 8 * 2**20
-PREP_GRANT = 54984704
 
 
 def split_const(table):
@@ -164,10 +163,10 @@
             field_ref[pl.ds(chan, outer, stride=chans), :] = y[:, side * LANES : (side + 1) * LANES]
 
 
-def call(body, operands, outs, scratch=(), flops=0, space=pltpu.VMEM, grant=VMEM_GRANT):
+def call(body, operands, outs, scratch=(), flops=0):
     size = sum(x.size * x.dtype.itemsize for x in list(operands) + list(outs))
     specs = [pl.BlockSpec(memory_space=pltpu.SMEM)]
-    specs += [pl.BlockSpec(memory_space=space)] * (len(operands) - 1)
+    specs += [pl.BlockSpec(memory_space=pltpu.VMEM)] * (len(operands) - 1)
     return pl.pallas_call(
         body,
         out_shape=tuple(outs),
@@ -175,7 +174,7 @@
         out_specs=tuple(pl.BlockSpec(memory_space=pltpu.VMEM) for _ in outs),
         scratch_shapes=list(scratch),
         cost_estimate=pl.CostEstimate(flops=flops, bytes_accessed=size, transcendentals=0),
-        compiler_params=pltpu.CompilerParams(vmem_limit_bytes=grant),
+        compiler_params=pltpu.CompilerParams(vmem_limit_bytes=VMEM_GRANT),
     )(*operands)
 
 
@@ -252,37 +251,26 @@
     split_rows = pltpu.VMEM((chunk * outer, 2 * LANES), BF16)
     n_blocks = parts // 2 + 1
 
-    inputs = (filter_taps, tok, cot, w_in, w_out)
-
-    def prep_kernel(at_ref, *refs):
-        signal_ref, sems = refs[-2:]
-        held = refs[-7:-2]
-        copies = [
-            pltpu.make_async_copy(source, target, sems.at[n])
-            for n, (source, target) in enumerate(zip(refs[:5], held))
-        ]
-        for copy in copies:
-            copy.start()
-        refs = refs[5:-7]
-        copies[0].wait()
-        signal_ref[...] = held[0][...].T
+    def taps_kernel(at_ref, taps_ref, keep_ref, give_ref, signal_ref):
+        signal_ref[...] = taps_ref[...].T
+        deal(at_ref[0], signal_ref, keep_ref, give_ref)
+
+    taps_blocks = exchange(*call(taps_kernel, (place, filter_taps), (block, block), [signal]))
+
+    def prep_kernel(at_ref, tok_ref, cot_ref, win_ref, wout_ref, *refs):
+        signal_ref = refs[-1]
+        gate_out, gate_in, values, dmixed = projections(tok_ref, cot_ref, win_ref, wout_ref)
+        signal_ref[...] = values * gate_in
         deal(at_ref[0], signal_ref, *refs[:2])
-        for copy in copies[1:]:
-            copy.wait()
-        gate_out, gate_in, values, dmixed = projections(*held[1:])
-        signal_ref[...] = values * gate_in
+        signal_ref[...] = dmixed * gate_out
         deal(at_ref[0], signal_ref, *refs[2:4])
-        signal_ref[...] = dmixed * gate_out
-        deal(at_ref[0], signal_ref, *refs[4:6])
 
     dealt = call(
-        prep_kernel, (place, *inputs), (block,) * 6,
-        [pltpu.VMEM(x.shape, x.dtype) for x in inputs] + [signal, pltpu.SemaphoreType.DMA((5,))],
-        flops=8 * rows * width * width, space=pltpu.MemorySpace.HBM, grant=PREP_GRANT,
-    )
-    taps_blocks = exchange(*dealt[:2])
-    gated_blocks = exchange(*dealt[2:4])
-    dconv_blocks = exchange(*dealt[4:])
+        prep_kernel, (place, tok, cot, w_in, w_out), (block,) * 4, [signal],
+        flops=8 * rows * width * width,
+    )
+    gated_blocks = exchange(*dealt[:2])
+    dconv_blocks = exchange(*dealt[2:])
 
     work = chans * outer * LANES * 4 * (3 * 2 * LANES + 6 * outer)
 

time: 93 us -> 92.6 us (level)
  the two profiles are of different devices: /device:TPU:0 before, /device:TPU:3 now
where the time goes in v4:
time: 92.6 us; the launch traced here: 92.4 us
  starting transfers between devices  44.3 us (48%)
  waiting for transfers between devices  25.6 us (28%)
  Pallas kernels  17.6 us (19%)
  local copies, waits for them, and re-layouts  3.24 us (3%)
  between operations  1.09 us (1%)
    ppermute x33, starting transfers between devices, mirror(): return lax.ppermute(x, axis, [(i, i ^ mask) for i in range(count)])  40.9 us
    ppermute x33, waiting for transfers between devices, mirror(): return lax.ppermute(x, axis, [(i, i ^ mask) for i in range(count)])  25.6 us
    pallas_call x10, Pallas kernels, call(): pl.pallas_call(body, out_shape=tuple(outs), in_specs=specs, out_specs=tup...  17.6 us
    ppermute x1, starting transfers between devices, shards(): term_sum = lax.ppermute(term_sum, ('dp', 'seq'), swap)  3.36 us
    unnamed x26, local copies, waits for them, and re-layouts  3.03 us
  transfers between devices with their start and end apart: 34, of which 12 were waited for; matrix products, arithmetic and copies ran while one was open for 1% of the time, Pallas kernels for 12%

profile of v4, /device:TPU:3, one launch (start us, length us, event | category | flops | bytes accessed | tf_op | source)
XLA Modules:
  0.0 92.4 jit_solution(2347409199101089840)
XLA Ops:
  7.1 1.5 %collective-permute-start.2 = (f32[2,128,128]{2,1,0:T(8,128)S(1)}, f32[2,128,128]{2,1,0:T(8,128)S(1)}, u32[]{:S(2)}, u32[]{:S(2)}) collective-permute-start(f32[2,128,128]{2,1,0:T(8,128)S(1)} %pad_maximum_fusion.2), channel_id=1, source_target_pairs={{0,4},{1,5},{2,6},{3,7},{4,0},{5,1},{6,2},{7,3},{8,12},{9,13},{10,... | collective-permute-start | bytes 393224 | tf_op jit(solution)/shard_map/ppermute | solution.py:183
  8.6 1.2 %collective-permute-start.3 = (f32[2,128,128]{2,1,0:T(8,128)S(1)}, f32[2,128,128]{2,1,0:T(8,128)S(1)}, u32[]{:S(2)}, u32[]{:S(2)}) collective-permute-start(f32[2,128,128]{2,1,0:T(8,128)S(1)} %pad_maximum_fusion.3), channel_id=1, source_target_pairs={{0,6},{1,7},{2,4},{3,5},{4,2},{5,3},{6,0},{7,1},{8,14},{9,15},{10,... | collective-permute-start | bytes 393224 | tf_op jit(solution)/shard_map/ppermute | solution.py:183
  10.1 1.5 %collective-permute-start.6 = (f32[2,128,128]{2,1,0:T(8,128)S(1)}, f32[2,128,128]{2,1,0:T(8,128)S(1)}, u32[]{:S(2)}, u32[]{:S(2)}) collective-permute-start(f32[2,128,128]{2,1,0:T(8,128)S(1)} %pad_maximum_fusion.5), channel_id=1, source_target_pairs={{0,4},{1,5},{2,6},{3,7},{4,0},{5,1},{6,2},{7,3},{8,12},{9,13},{10,... | collective-permute-start | bytes 393224 | tf_op jit(solution)/shard_map/ppermute | solution.py:183
  12.0 1.2 %collective-permute-start.7 = (f32[2,128,128]{2,1,0:T(8,128)S(1)}, f32[2,128,128]{2,1,0:T(8,128)S(1)}, u32[]{:S(2)}, u32[]{:S(2)}) collective-permute-start(f32[2,128,128]{2,1,0:T(8,128)S(1)} %pad_maximum_fusion.6), channel_id=1, source_target_pairs={{0,6},{1,7},{2,4},{3,5},{4,2},{5,3},{6,0},{7,1},{8,14},{9,15},{10,... | collective-permute-start | bytes 393224 | tf_op jit(solution)/shard_map/ppermute | solution.py:183
  13.3 1.3 %collective-permute-start.13 = (f32[2,128,128]{2,1,0:T(8,128)S(1)}, f32[2,128,128]{2,1,0:T(8,128)S(1)}, u32[]{:S(2)}, u32[]{:S(2)}) collective-permute-start(f32[2,128,128]{2,1,0:T(8,128)S(1)} %pad_maximum_fusion.10), channel_id=1, source_target_pairs={{0,2},{1,3},{2,0},{3,1},{4,6},{5,7},{6,4},{7,5},{8,10},{9,11},{10,... | collective-permute-start | bytes 393224 | tf_op jit(solution)/shard_map/ppermute | solution.py:183
  14.6 1.3 %collective-permute-done.3.refs_4_ = f32[2,128,128]{2,1,0:T(8,128)S(1)} collective-permute-done((f32[2,128,128]{2,1,0:T(8,128)S(1)}, f32[2,128,128]{2,1,0:T(8,128)S(1)}, u32[]{:S(2)}, u32[]{:S(2)}) %collective-permute-start.3) | collective-permute-done | bytes 131104 | tf_op jit(solution)/shard_map/ppermute | solution.py:183
  15.8 1.2 %collective-permute-start.14 = (f32[2,128,128]{2,1,0:T(8,128)S(1)}, f32[2,128,128]{2,1,0:T(8,128)S(1)}, u32[]{:S(2)}, u32[]{:S(2)}) collective-permute-start(f32[2,128,128]{2,1,0:T(8,128)S(1)} %pad_maximum_fusion.11), channel_id=1, source_target_pairs={{0,4},{1,5},{2,6},{3,7},{4,0},{5,1},{6,2},{7,3},{8,12},{9,13},{10,... | collective-permute-start | bytes 393224 | tf_op jit(solution)/shard_map/ppermute | solution.py:183
  18.6 1.5 %shard_map.155.h_ref = f32[1024,256]{1,0:T(8,128)S(1)} custom-call(s32[2]{0:T(128)S(1)} %pad_add_fusion.at_ref, bf16[64,96]{1,0:T(8,128)(2,1)S(1)} %copy-done.9, f32[2,32,128]{2,1,0:T(8,128)S(1)} %copy-done.8, bf16[2,256,256]{2,1,0:T(8,128)(2,1)S(1)} %copy-done.7, f32[4,128,128]{2,1,0:T(8,128)S(1)} %get-tuple-element.29.refs_0_, ...), custom_call_target="tpu_custom_call" | custom-call | flops 503316480 | bytes 2273288 | tf_op jit(solution)/shard_map/pallas_call | solution.py:170
  20.2 1.3 %collective-permute-done.7.refs_4_ = f32[2,128,128]{2,1,0:T(8,128)S(1)} collective-permute-done((f32[2,128,128]{2,1,0:T(8,128)S(1)}, f32[2,128,128]{2,1,0:T(8,128)S(1)}, u32[]{:S(2)}, u32[]{:S(2)}) %collective-permute-start.7) | collective-permute-done | bytes 131104 | tf_op jit(solution)/shard_map/ppermute | solution.py:183
  21.5 2.9 %shard_map.157 = (f32[1024,256]{1,0:T(8,128)S(1)}, f32[4,128,128]{2,1,0:T(8,128)S(1)}, f32[4,128,128]{2,1,0:T(8,128)S(1)}) custom-call(s32[2]{0:T(128)S(1)} %pad_add_fusion.at_ref, bf16[64,96]{1,0:T(8,128)(2,1)S(1)} %copy-done.9, bf16[32,192]{1,0:T(8,128)(2,1)S(1)} %copy-done.12, f32[2,32,128]{2,1,0:T(8,128)S(1)} %copy-done.8, ...), custom_call_target="tpu_custom_call" | custom-call | flops 1006632960 | bytes 4120584 | tf_op jit(solution)/shard_map/pallas_call | solution.py:170
  24.4 2.7 %collective-permute-done.15.refs_4_ = f32[2,128,128]{2,1,0:T(8,128)S(1)} collective-permute-done((f32[2,128,128]{2,1,0:T(8,128)S(1)}, f32[2,128,128]{2,1,0:T(8,128)S(1)}, u32[]{:S(2)}, u32[]{:S(2)}) %collective-permute-start.15) | collective-permute-done | bytes 131104 | tf_op jit(solution)/shard_map/ppermute | solution.py:183
  27.1 4.1 %shard_map.160 = (f32[4,128,128]{2,1,0:T(8,128)S(1)}, f32[4,128,128]{2,1,0:T(8,128)S(1)}, f32[4,256,128]{2,1,0:T(8,128)S(1)}) custom-call(s32[2]{0:T(128)S(1)} %pad_add_fusion.at_ref, bf16[64,96]{1,0:T(8,128)(2,1)S(1)} %copy-done.9, bf16[32,192]{1,0:T(8,128)(2,1)S(1)} %copy-done.12, f32[2,32,128]{2,1,0:T(8,128)S(1)} %copy-done.8, ...), custom_call_target="tpu_custom_call" | custom-call | flops 1509949440 | bytes 4644872 | tf_op jit(solution)/shard_map/pallas_call | solution.py:170
  32.2 1.4 %collective-permute-start.30 = (f32[2,256,128]{2,1,0:T(8,128)S(1)}, f32[2,256,128]{2,1,0:T(8,128)S(1)}, u32[]{:S(2)}, u32[]{:S(2)}) collective-permute-start(f32[2,256,128]{2,1,0:T(8,128)S(1)} %slice.169), channel_id=1, source_target_pairs={{0,8},{8,0},{16,24},{24,16},{1,9},{9,1},{17,25},{25,17},{2,10},{10... | collective-permute-start | bytes 786440 | tf_op jit(solution)/shard_map/ppermute | solution.py:183
  34.6 1.3 %collective-permute-start.18 = (f32[2,128,128]{2,1,0:T(8,128)S(1)}, f32[2,128,128]{2,1,0:T(8,128)S(1)}, u32[]{:S(2)}, u32[]{:S(2)}) collective-permute-start(f32[2,128,128]{2,1,0:T(8,128)S(1)} %pad_maximum_fusion.14), channel_id=1, source_target_pairs={{0,4},{1,5},{2,6},{3,7},{4,0},{5,1},{6,2},{7,3},{8,12},{9,13},{10,... | collective-permute-start | bytes 393224 | tf_op jit(solution)/shard_map/ppermute | solution.py:183
  37.5 1.4 %collective-permute-done.17.refs_2_ = f32[2,128,128]{2,1,0:T(8,128)S(1)} collective-permute-done((f32[2,128,128]{2,1,0:T(8,128)S(1)}, f32[2,128,128]{2,1,0:T(8,128)S(1)}, u32[]{:S(2)}, u32[]{:S(2)}) %collective-permute-start.17) | collective-permute-done | bytes 131104 | tf_op jit(solution)/shard_map/ppermute | solution.py:183
  39.4 2.3 %collective-permute-done.19.refs_4_ = f32[2,128,128]{2,1,0:T(8,128)S(1)} collective-permute-done((f32[2,128,128]{2,1,0:T(8,128)S(1)}, f32[2,128,128]{2,1,0:T(8,128)S(1)}, u32[]{:S(2)}, u32[]{:S(2)}) %collective-permute-start.19) | collective-permute-done | bytes 131104 | tf_op jit(solution)/shard_map/ppermute | solution.py:183
  41.7 1.4 %shard_map.161 = (bf16[512,512]{1,0:T(8,128)(2,1)S(1)}, f32[4,32,512]{2,1,0:T(8,128)S(1)}, f32[4,32,512]{2,1,0:T(8,128)S(1)}) custom-call(s32[2]{0:T(128)S(1)} %pad_add_fusion.at_ref, bf16[512,256]{1,0:T(8,128)(2,1)S(1)} %bitcast.17, bf16[512,256]{1,0:T(8,128)(2,1)S(1)} %bitcast.20, bf16[256,768]{1,0:T(8,128)(2,1)S(1)} %copy-done, ...), custom_call_target="tpu_custom_call" | custom-call | flops 603979776 | bytes 3015688 | tf_op jit(solution)/shard_map/pallas_call | solution.py:170
  43.1 2.4 %collective-permute-start.23 = (f32[4,32,512]{2,1,0:T(8,128)S(1)}, f32[4,32,512]{2,1,0:T(8,128)S(1)}, u32[]{:S(2)}, u32[]{:S(2)}) collective-permute-start(f32[4,32,512]{2,1,0:T(8,128)S(1)} %get-tuple-element.46), channel_id=1, source_target_pairs={{0,1},{1,0},{2,3},{3,2},{4,5},{5,4},{6,7},{7,6},{8,9},{9,8},{10,11... | collective-permute-start | bytes 786440 | tf_op jit(solution)/shard_map/ppermute | solution.py:183
  46.5 5.0 %collective-permute-done.11.refs_4_ = f32[2,128,128]{2,1,0:T(8,128)S(1)} collective-permute-done((f32[2,128,128]{2,1,0:T(8,128)S(1)}, f32[2,128,128]{2,1,0:T(8,128)S(1)}, u32[]{:S(2)}, u32[]{:S(2)}) %collective-permute-start.11) | collective-permute-done | bytes 131104 | tf_op jit(solution)/shard_map/ppermute | solution.py:183
  51.5 1.4 %shard_map.158 = (bf16[256,512]{1,0:T(8,128)(2,1)S(1)}, bf16[256,512]{1,0:T(8,128)(2,1)S(1)}, f32[4,32,640]{2,1,0:T(8,128)S(1)}, f32[4,32,640]{2,1,0:T(8,128)S(1)}) custom-call(s32[2]{0:T(128)S(1)} %pad_add_fusion.at_ref, bf16[512,256]{1,0:T(8,128)(2,1)S(1)} %bitcast.18, bf16[512,256]{1,0:T(8,128)(2,1)S(1)} %bitcast.21, bf16[256,768]{1,0:T(8,128)(2,1)S(1)} %copy-done, ...), custom_call_target="tpu_custom_call" | custom-call | flops 469762048 | bytes 3146760 | tf_op jit(solution)/shard_map/pallas_call | solution.py:170
  55.0 2.4 %collective-permute-start.31 = (f32[1,256,128]{2,1,0:T(8,128)S(1)}, f32[1,256,128]{2,1,0:T(8,128)S(1)}, u32[]{:S(2)}, u32[]{:S(2)}) collective-permute-start(f32[1,256,128]{2,1,0:T(8,128)S(1)} %slice.197), channel_id=1, source_target_pairs={{0,16},{8,24},{16,0},{24,8},{1,17},{9,25},{17,1},{25,9},{2,18},{10... | collective-permute-start | bytes 393224 | tf_op jit(solution)/shard_map/ppermute | solution.py:183
  58.1 3.8 %collective-permute-done.24 = f32[2,32,512]{2,1,0:T(8,128)S(1)} collective-permute-done((f32[2,32,512]{2,1,0:T(8,128)S(1)}, f32[2,32,512]{2,1,0:T(8,128)S(1)}, u32[]{:S(2)}, u32[]{:S(2)}) %collective-permute-start.24) | collective-permute-done | bytes 131104 | tf_op jit(solution)/shard_map/ppermute | solution.py:183
  61.9 3.4 %collective-permute-done.21 = f32[2,32,640]{2,1,0:T(8,128)S(1)} collective-permute-done((f32[2,32,640]{2,1,0:T(8,128)S(1)}, f32[2,32,640]{2,1,0:T(8,128)S(1)}, u32[]{:S(2)}, u32[]{:S(2)}) %collective-permute-start.21) | collective-permute-done | bytes 163872 | tf_op jit(solution)/shard_map/ppermute | solution.py:183
  65.4 2.4 %collective-permute-start.22 = (f32[1,32,640]{2,1,0:T(8,128)S(1)}, f32[1,32,640]{2,1,0:T(8,128)S(1)}, u32[]{:S(2)}, u32[]{:S(2)}) collective-permute-start(f32[1,32,640]{2,1,0:T(8,128)S(1)} %slice.191), channel_id=1, source_target_pairs={{0,16},{8,24},{16,0},{24,8},{1,17},{9,25},{17,1},{25,9},{2,18},{10... | collective-permute-start | bytes 245768 | tf_op jit(solution)/shard_map/ppermute | solution.py:183
  67.8 2.3 %collective-permute-done.22 = f32[1,32,640]{2,1,0:T(8,128)S(1)} collective-permute-done((f32[1,32,640]{2,1,0:T(8,128)S(1)}, f32[1,32,640]{2,1,0:T(8,128)S(1)}, u32[]{:S(2)}, u32[]{:S(2)}) %collective-permute-start.22) | collective-permute-done | bytes 81952 | tf_op jit(solution)/shard_map/ppermute | solution.py:183
  70.1 1.2 %collective-permute-start.27 = (f32[32,1152]{1,0:T(8,128)S(1)}, f32[32,1152]{1,0:T(8,128)S(1)}, u32[]{:S(2)}, u32[]{:S(2)}) collective-permute-start(f32[32,1152]{1,0:T(8,128)S(1)} %pad_maximum_fusion), channel_id=1, source_target_pairs={{0,4},{1,5},{2,6},{3,7},{4,0},{5,1},{6,2},{7,3},{8,12},{9,13},{10,... | collective-permute-start | bytes 442376 | tf_op jit(solution)/shard_map/ppermute | solution.py:183
  72.9 3.4 %collective-permute-start.32 = (f32[256,128]{1,0:T(8,128)S(1)}, f32[256,128]{1,0:T(8,128)S(1)}, u32[]{:S(2)}, u32[]{:S(2)}) collective-permute-start(f32[256,128]{1,0:T(8,128)S(1)} %fusion), channel_id=1, source_target_pairs={{0,0},{1,1},{2,10},{3,11},{4,20},{5,21},{6,30},{7,31},{8,2},{9,3},... | collective-permute-start | bytes 393224 | tf_op jit(solution)/shard_map/ppermute | solution.py:429
  77.3 8.2 %collective-permute-start.29 = (f32[32,1152]{1,0:T(8,128)S(1)}, f32[32,1152]{1,0:T(8,128)S(1)}, u32[]{:S(2)}, u32[]{:S(2)}) collective-permute-start(f32[32,1152]{1,0:T(8,128)S(1)} %add_add_fusion.refs_0_), channel_id=1, source_target_pairs={{0,1},{1,0},{2,3},{3,2},{4,5},{5,4},{6,7},{7,6},{8,9},{9,8},{10,11... | collective-permute-start | bytes 442376 | tf_op jit(solution)/shard_map/ppermute | solution.py:183
  85.6 2.3 %collective-permute-start.33 = (f32[128,128]{1,0:T(8,128)S(1)}, f32[128,128]{1,0:T(8,128)S(1)}, u32[]{:S(2)}, u32[]{:S(2)}) collective-permute-start(f32[128,128]{1,0:T(8,128)S(1)} %slice.198), channel_id=1, source_target_pairs={{0,1},{1,0},{2,3},{3,2},{4,5},{5,4},{6,7},{7,6},{8,9},{9,8},{10,11... | collective-permute-start | bytes 196616 | tf_op jit(solution)/shard_map/ppermute | solution.py:183
  87.9 1.5 %shard_map.159 = bf16[512,256]{1,0:T(8,128)(2,1)} custom-call(s32[2]{0:T(128)S(1)} %pad_add_fusion.at_ref, bf16[256,256]{1,0:T(8,128)(2,1)S(1)} %copy-done.1, bf16[256,512]{1,0:T(8,128)(2,1)S(1)} %get-tuple-element.35.mixed_ref), custom_call_target="tpu_custom_call" | custom-call | flops 67108864 | bytes 655368 | tf_op jit(solution)/shard_map/pallas_call | solution.py:170
  89.4 1.7 %shard_map.162 = bf16[512,256]{1,0:T(8,128)(2,1)} custom-call(s32[2]{0:T(128)S(1)} %pad_add_fusion.at_ref, bf16[256,768]{1,0:T(8,128)(2,1)S(1)} %copy-done, bf16[256,512]{1,0:T(8,128)(2,1)S(1)} %get-tuple-element.36.first_dproj_ref, bf16[512,512]{1,0:T(8,128)(2,1)S(1)} %get-tuple-element.42.late_dproj_ref), custom_call_target="tpu_custom_call" | custom-call | flops 201326592 | bytes 1441800 | tf_op jit(solution)/shard_map/pallas_call | solution.py:170
  91.0 1.3 %shard_map.163 = (f32[64,768]{1,0:T(8,128)}, f32[64,256]{1,0:T(8,128)}, f32[64,512]{1,0:T(8,128)}, f32[1,64]{1,0:T(1,128)}) custom-call(s32[2]{0:T(128)S(1)} %pad_add_fusion.at_ref, f32[32,1152]{1,0:T(8,128)S(1)} %add_add_fusion.refs_0_, f32[32,1152]{1,0:T(8,128)S(1)} %collective-permute-done.29.refs_1_, f32[2,128,128]{2,1,0:T(8,128)S(1)} %bitcast.22, ...), custom_call_target="tpu_custom_call" | custom-call | flops 131072 | bytes 885000 | tf_op jit(solution)/shard_map/pallas_call | solution.py:170
  (115 shorter events, 19.2 us)
Async XLA Ops:
  2.6 4.4 %collective-permute-start = (f32[4,128,128]{2,1,0:T(8,128)S(1)}, f32[4,128,128]{2,1,0:T(8,128)S(1)}, u32[]{:S(2)}, u32[]{:S(2)}) collective-permute-start(f32[4,128,128]{2,1,0:T(8,128)S(1)} %get-tuple-element.30), channel_id=1, source_target_pairs={{0,1},{1,0},{2,3},{3,2},{4,5},{5,4},{6,7},{7,6},{8,9},{9,8},{10,11... | collective-permute-start | bytes 786440 | tf_op jit(solution)/shard_map/ppermute | solution.py:183
  6.3 3.6 %collective-permute-start.4 = (f32[4,128,128]{2,1,0:T(8,128)S(1)}, f32[4,128,128]{2,1,0:T(8,128)S(1)}, u32[]{:S(2)}, u32[]{:S(2)}) collective-permute-start(f32[4,128,128]{2,1,0:T(8,128)S(1)} %get-tuple-element.32), channel_id=1, source_target_pairs={{0,1},{1,0},{2,3},{3,2},{4,5},{5,4},{6,7},{7,6},{8,9},{9,8},{10,11... | collective-permute-start | bytes 786440 | tf_op jit(solution)/shard_map/ppermute | solution.py:183
  6.4 3.7 %collective-permute-start.12 = (f32[4,128,128]{2,1,0:T(8,128)S(1)}, f32[4,128,128]{2,1,0:T(8,128)S(1)}, u32[]{:S(2)}, u32[]{:S(2)}) collective-permute-start(f32[4,128,128]{2,1,0:T(8,128)S(1)} %get-tuple-element.39), channel_id=1, source_target_pairs={{0,1},{1,0},{2,3},{3,2},{4,5},{5,4},{6,7},{7,6},{8,9},{9,8},{10,11... | collective-permute-start | bytes 786440 | tf_op jit(solution)/shard_map/ppermute | solution.py:183
  7.0 5.0 %collective-permute-start.1 = (f32[2,128,128]{2,1,0:T(8,128)S(1)}, f32[2,128,128]{2,1,0:T(8,128)S(1)}, u32[]{:S(2)}, u32[]{:S(2)}) collective-permute-start(f32[2,128,128]{2,1,0:T(8,128)S(1)} %pad_maximum_fusion.1), channel_id=1, source_target_pairs={{0,2},{1,3},{2,0},{3,1},{4,6},{5,7},{6,4},{7,5},{8,10},{9,11},{10,... | collective-permute-start | bytes 393224 | tf_op jit(solution)/shard_map/ppermute | solution.py:183
  7.1 6.2 %collective-permute-start.2 = (f32[2,128,128]{2,1,0:T(8,128)S(1)}, f32[2,128,128]{2,1,0:T(8,128)S(1)}, u32[]{:S(2)}, u32[]{:S(2)}) collective-permute-start(f32[2,128,128]{2,1,0:T(8,128)S(1)} %pad_maximum_fusion.2), channel_id=1, source_target_pairs={{0,4},{1,5},{2,6},{3,7},{4,0},{5,1},{6,2},{7,3},{8,12},{9,13},{10,... | collective-permute-start | bytes 393224 | tf_op jit(solution)/shard_map/ppermute | solution.py:183
  8.6 7.2 %collective-permute-start.3 = (f32[2,128,128]{2,1,0:T(8,128)S(1)}, f32[2,128,128]{2,1,0:T(8,128)S(1)}, u32[]{:S(2)}, u32[]{:S(2)}) collective-permute-start(f32[2,128,128]{2,1,0:T(8,128)S(1)} %pad_maximum_fusion.3), channel_id=1, source_target_pairs={{0,6},{1,7},{2,4},{3,5},{4,2},{5,3},{6,0},{7,1},{8,14},{9,15},{10,... | collective-permute-start | bytes 393224 | tf_op jit(solution)/shard_map/ppermute | solution.py:183
  9.9 7.8 %collective-permute-start.5 = (f32[2,128,128]{2,1,0:T(8,128)S(1)}, f32[2,128,128]{2,1,0:T(8,128)S(1)}, u32[]{:S(2)}, u32[]{:S(2)}) collective-permute-start(f32[2,128,128]{2,1,0:T(8,128)S(1)} %pad_maximum_fusion.4), channel_id=1, source_target_pairs={{0,2},{1,3},{2,0},{3,1},{4,6},{5,7},{6,4},{7,5},{8,10},{9,11},{10,... | collective-permute-start | bytes 393224 | tf_op jit(solution)/shard_map/ppermute | solution.py:183
  10.1 10.1 %collective-permute-start.6 = (f32[2,128,128]{2,1,0:T(8,128)S(1)}, f32[2,128,128]{2,1,0:T(8,128)S(1)}, u32[]{:S(2)}, u32[]{:S(2)}) collective-permute-start(f32[2,128,128]{2,1,0:T(8,128)S(1)} %pad_maximum_fusion.5), channel_id=1, source_target_pairs={{0,4},{1,5},{2,6},{3,7},{4,0},{5,1},{6,2},{7,3},{8,12},{9,13},{10,... | collective-permute-start | bytes 393224 | tf_op jit(solution)/shard_map/ppermute | solution.py:183
  12.0 9.5 %collective-permute-start.7 = (f32[2,128,128]{2,1,0:T(8,128)S(1)}, f32[2,128,128]{2,1,0:T(8,128)S(1)}, u32[]{:S(2)}, u32[]{:S(2)}) collective-permute-start(f32[2,128,128]{2,1,0:T(8,128)S(1)} %pad_maximum_fusion.6), channel_id=1, source_target_pairs={{0,6},{1,7},{2,4},{3,5},{4,2},{5,3},{6,0},{7,1},{8,14},{9,15},{10,... | collective-permute-start | bytes 393224 | tf_op jit(solution)/shard_map/ppermute | solution.py:183
  13.3 11.1 %collective-permute-start.13 = (f32[2,128,128]{2,1,0:T(8,128)S(1)}, f32[2,128,128]{2,1,0:T(8,128)S(1)}, u32[]{:S(2)}, u32[]{:S(2)}) collective-permute-start(f32[2,128,128]{2,1,0:T(8,128)S(1)} %pad_maximum_fusion.10), channel_id=1, source_target_pairs={{0,2},{1,3},{2,0},{3,1},{4,6},{5,7},{6,4},{7,5},{8,10},{9,11},{10,... | collective-permute-start | bytes 393224 | tf_op jit(solution)/shard_map/ppermute | solution.py:183
  15.8 8.6 %collective-permute-start.14 = (f32[2,128,128]{2,1,0:T(8,128)S(1)}, f32[2,128,128]{2,1,0:T(8,128)S(1)}, u32[]{:S(2)}, u32[]{:S(2)}) collective-permute-start(f32[2,128,128]{2,1,0:T(8,128)S(1)} %pad_maximum_fusion.11), channel_id=1, source_target_pairs={{0,4},{1,5},{2,6},{3,7},{4,0},{5,1},{6,2},{7,3},{8,12},{9,13},{10,... | collective-permute-start | bytes 393224 | tf_op jit(solution)/shard_map/ppermute | solution.py:183
  17.7 9.4 %collective-permute-start.15 = (f32[2,128,128]{2,1,0:T(8,128)S(1)}, f32[2,128,128]{2,1,0:T(8,128)S(1)}, u32[]{:S(2)}, u32[]{:S(2)}) collective-permute-start(f32[2,128,128]{2,1,0:T(8,128)S(1)} %pad_maximum_fusion.12), channel_id=1, source_target_pairs={{0,6},{1,7},{2,4},{3,5},{4,2},{5,3},{6,0},{7,1},{8,14},{9,15},{10,... | collective-permute-start | bytes 393224 | tf_op jit(solution)/shard_map/ppermute | solution.py:183
  32.2 22.7 %collective-permute-start.30 = (f32[2,256,128]{2,1,0:T(8,128)S(1)}, f32[2,256,128]{2,1,0:T(8,128)S(1)}, u32[]{:S(2)}, u32[]{:S(2)}) collective-permute-start(f32[2,256,128]{2,1,0:T(8,128)S(1)} %slice.169), channel_id=1, source_target_pairs={{0,8},{8,0},{16,24},{24,16},{1,9},{9,1},{17,25},{25,17},{2,10},{10... | collective-permute-start | bytes 786440 | tf_op jit(solution)/shard_map/ppermute | solution.py:183
  34.0 4.9 %collective-permute-start.17 = (f32[2,128,128]{2,1,0:T(8,128)S(1)}, f32[2,128,128]{2,1,0:T(8,128)S(1)}, u32[]{:S(2)}, u32[]{:S(2)}) collective-permute-start(f32[2,128,128]{2,1,0:T(8,128)S(1)} %pad_maximum_fusion.13), channel_id=1, source_target_pairs={{0,2},{1,3},{2,0},{3,1},{4,6},{5,7},{6,4},{7,5},{8,10},{9,11},{10,... | collective-permute-start | bytes 393224 | tf_op jit(solution)/shard_map/ppermute | solution.py:183
  34.6 4.9 %collective-permute-start.18 = (f32[2,128,128]{2,1,0:T(8,128)S(1)}, f32[2,128,128]{2,1,0:T(8,128)S(1)}, u32[]{:S(2)}, u32[]{:S(2)}) collective-permute-start(f32[2,128,128]{2,1,0:T(8,128)S(1)} %pad_maximum_fusion.14), channel_id=1, source_target_pairs={{0,4},{1,5},{2,6},{3,7},{4,0},{5,1},{6,2},{7,3},{8,12},{9,13},{10,... | collective-permute-start | bytes 393224 | tf_op jit(solution)/shard_map/ppermute | solution.py:183
  35.9 5.8 %collective-permute-start.19 = (f32[2,128,128]{2,1,0:T(8,128)S(1)}, f32[2,128,128]{2,1,0:T(8,128)S(1)}, u32[]{:S(2)}, u32[]{:S(2)}) collective-permute-start(f32[2,128,128]{2,1,0:T(8,128)S(1)} %pad_maximum_fusion.15), channel_id=1, source_target_pairs={{0,6},{1,7},{2,4},{3,5},{4,2},{5,3},{6,0},{7,1},{8,14},{9,15},{10,... | collective-permute-start | bytes 393224 | tf_op jit(solution)/shard_map/ppermute | solution.py:183
  36.9 9.6 %collective-permute-start.9 = (f32[2,128,128]{2,1,0:T(8,128)S(1)}, f32[2,128,128]{2,1,0:T(8,128)S(1)}, u32[]{:S(2)}, u32[]{:S(2)}) collective-permute-start(f32[2,128,128]{2,1,0:T(8,128)S(1)} %pad_maximum_fusion.7), channel_id=1, source_target_pairs={{0,2},{1,3},{2,0},{3,1},{4,6},{5,7},{6,4},{7,5},{8,10},{9,11},{10,... | collective-permute-start | bytes 393224 | tf_op jit(solution)/shard_map/ppermute | solution.py:183
  38.9 7.6 %collective-permute-start.10 = (f32[2,128,128]{2,1,0:T(8,128)S(1)}, f32[2,128,128]{2,1,0:T(8,128)S(1)}, u32[]{:S(2)}, u32[]{:S(2)}) collective-permute-start(f32[2,128,128]{2,1,0:T(8,128)S(1)} %pad_maximum_fusion.8), channel_id=1, source_target_pairs={{0,4},{1,5},{2,6},{3,7},{4,0},{5,1},{6,2},{7,3},{8,12},{9,13},{10,... | collective-permute-start | bytes 393224 | tf_op jit(solution)/shard_map/ppermute | solution.py:183
  43.1 10.8 %collective-permute-start.23 = (f32[4,32,512]{2,1,0:T(8,128)S(1)}, f32[4,32,512]{2,1,0:T(8,128)S(1)}, u32[]{:S(2)}, u32[]{:S(2)}) collective-permute-start(f32[4,32,512]{2,1,0:T(8,128)S(1)} %get-tuple-element.46), channel_id=1, source_target_pairs={{0,1},{1,0},{2,3},{3,2},{4,5},{5,4},{6,7},{7,6},{8,9},{9,8},{10,11... | collective-permute-start | bytes 786440 | tf_op jit(solution)/shard_map/ppermute | solution.py:183
  45.5 6.0 %collective-permute-start.11 = (f32[2,128,128]{2,1,0:T(8,128)S(1)}, f32[2,128,128]{2,1,0:T(8,128)S(1)}, u32[]{:S(2)}, u32[]{:S(2)}) collective-permute-start(f32[2,128,128]{2,1,0:T(8,128)S(1)} %pad_maximum_fusion.9), channel_id=1, source_target_pairs={{0,6},{1,7},{2,4},{3,5},{4,2},{5,3},{6,0},{7,1},{8,14},{9,15},{10,... | collective-permute-start | bytes 393224 | tf_op jit(solution)/shard_map/ppermute | solution.py:183
  53.0 4.4 %collective-permute-start.20 = (f32[4,32,640]{2,1,0:T(8,128)S(1)}, f32[4,32,640]{2,1,0:T(8,128)S(1)}, u32[]{:S(2)}, u32[]{:S(2)}) collective-permute-start(f32[4,32,640]{2,1,0:T(8,128)S(1)} %get-tuple-element.44), channel_id=1, source_target_pairs={{0,1},{1,0},{2,3},{3,2},{4,5},{5,4},{6,7},{7,6},{8,9},{9,8},{10,11... | collective-permute-start | bytes 983048 | tf_op jit(solution)/shard_map/ppermute | solution.py:183
  54.0 7.8 %collective-permute-start.24 = (f32[2,32,512]{2,1,0:T(8,128)S(1)}, f32[2,32,512]{2,1,0:T(8,128)S(1)}, u32[]{:S(2)}, u32[]{:S(2)}) collective-permute-start(f32[2,32,512]{2,1,0:T(8,128)S(1)} %slice.193), channel_id=1, source_target_pairs={{0,8},{8,0},{16,24},{24,16},{1,9},{9,1},{17,25},{25,17},{2,10},{10... | collective-permute-start | bytes 393224 | tf_op jit(solution)/shard_map/ppermute | solution.py:183
  55.0 17.9 %collective-permute-start.31 = (f32[1,256,128]{2,1,0:T(8,128)S(1)}, f32[1,256,128]{2,1,0:T(8,128)S(1)}, u32[]{:S(2)}, u32[]{:S(2)}) collective-permute-start(f32[1,256,128]{2,1,0:T(8,128)S(1)} %slice.197), channel_id=1, source_target_pairs={{0,16},{8,24},{16,0},{24,8},{1,17},{9,25},{17,1},{25,9},{2,18},{10... | collective-permute-start | bytes 393224 | tf_op jit(solution)/shard_map/ppermute | solution.py:183
  57.4 8.0 %collective-permute-start.21 = (f32[2,32,640]{2,1,0:T(8,128)S(1)}, f32[2,32,640]{2,1,0:T(8,128)S(1)}, u32[]{:S(2)}, u32[]{:S(2)}) collective-permute-start(f32[2,32,640]{2,1,0:T(8,128)S(1)} %slice.189), channel_id=1, source_target_pairs={{0,8},{8,0},{16,24},{24,16},{1,9},{9,1},{17,25},{25,17},{2,10},{10... | collective-permute-start | bytes 491528 | tf_op jit(solution)/shard_map/ppermute | solution.py:183
  61.9 5.9 %collective-permute-start.25 = (f32[1,32,512]{2,1,0:T(8,128)S(1)}, f32[1,32,512]{2,1,0:T(8,128)S(1)}, u32[]{:S(2)}, u32[]{:S(2)}) collective-permute-start(f32[1,32,512]{2,1,0:T(8,128)S(1)} %slice.195), channel_id=1, source_target_pairs={{0,16},{8,24},{16,0},{24,8},{1,17},{9,25},{17,1},{25,9},{2,18},{10... | collective-permute-start | bytes 196616 | tf_op jit(solution)/shard_map/ppermute | solution.py:183
  65.4 4.7 %collective-permute-start.22 = (f32[1,32,640]{2,1,0:T(8,128)S(1)}, f32[1,32,640]{2,1,0:T(8,128)S(1)}, u32[]{:S(2)}, u32[]{:S(2)}) collective-permute-start(f32[1,32,640]{2,1,0:T(8,128)S(1)} %slice.191), channel_id=1, source_target_pairs={{0,16},{8,24},{16,0},{24,8},{1,17},{9,25},{17,1},{25,9},{2,18},{10... | collective-permute-start | bytes 245768 | tf_op jit(solution)/shard_map/ppermute | solution.py:183
  70.1 6.1 %collective-permute-start.27 = (f32[32,1152]{1,0:T(8,128)S(1)}, f32[32,1152]{1,0:T(8,128)S(1)}, u32[]{:S(2)}, u32[]{:S(2)}) collective-permute-start(f32[32,1152]{1,0:T(8,128)S(1)} %pad_maximum_fusion), channel_id=1, source_target_pairs={{0,4},{1,5},{2,6},{3,7},{4,0},{5,1},{6,2},{7,3},{8,12},{9,13},{10,... | collective-permute-start | bytes 442376 | tf_op jit(solution)/shard_map/ppermute | solution.py:183
  71.3 4.9 %collective-permute-start.28 = (f32[32,1152]{1,0:T(8,128)S(1)}, f32[32,1152]{1,0:T(8,128)S(1)}, u32[]{:S(2)}, u32[]{:S(2)}) collective-permute-start(f32[32,1152]{1,0:T(8,128)S(1)} %pad_maximum_fusion), channel_id=1, source_target_pairs={{0,6},{1,7},{2,4},{3,5},{4,2},{5,3},{6,0},{7,1},{8,14},{9,15},{10,... | collective-permute-start | bytes 442376 | tf_op jit(solution)/shard_map/ppermute | solution.py:183
  72.3 5.0 %collective-permute-start.26 = (f32[32,1152]{1,0:T(8,128)S(1)}, f32[32,1152]{1,0:T(8,128)S(1)}, u32[]{:S(2)}, u32[]{:S(2)}) collective-permute-start(f32[32,1152]{1,0:T(8,128)S(1)} %pad_maximum_fusion), channel_id=1, source_target_pairs={{0,2},{1,3},{2,0},{3,1},{4,6},{5,7},{6,4},{7,5},{8,10},{9,11},{10,... | collective-permute-start | bytes 442376 | tf_op jit(solution)/shard_map/ppermute | solution.py:183
  72.9 12.7 %collective-permute-start.32 = (f32[256,128]{1,0:T(8,128)S(1)}, f32[256,128]{1,0:T(8,128)S(1)}, u32[]{:S(2)}, u32[]{:S(2)}) collective-permute-start(f32[256,128]{1,0:T(8,128)S(1)} %fusion), channel_id=1, source_target_pairs={{0,0},{1,1},{2,10},{3,11},{4,20},{5,21},{6,30},{7,31},{8,2},{9,3},... | collective-permute-start | bytes 393224 | tf_op jit(solution)/shard_map/ppermute | solution.py:429
  77.3 13.7 %collective-permute-start.29 = (f32[32,1152]{1,0:T(8,128)S(1)}, f32[32,1152]{1,0:T(8,128)S(1)}, u32[]{:S(2)}, u32[]{:S(2)}) collective-permute-start(f32[32,1152]{1,0:T(8,128)S(1)} %add_add_fusion.refs_0_), channel_id=1, source_target_pairs={{0,1},{1,0},{2,3},{3,2},{4,5},{5,4},{6,7},{7,6},{8,9},{9,8},{10,11... | collective-permute-start | bytes 442376 | tf_op jit(solution)/shard_map/ppermute | solution.py:183
  85.6 5.4 %collective-permute-start.33 = (f32[128,128]{1,0:T(8,128)S(1)}, f32[128,128]{1,0:T(8,128)S(1)}, u32[]{:S(2)}, u32[]{:S(2)}) collective-permute-start(f32[128,128]{1,0:T(8,128)S(1)} %slice.198), channel_id=1, source_target_pairs={{0,1},{1,0},{2,3},{3,2},{4,5},{5,4},{6,7},{7,6},{8,9},{9,8},{10,11... | collective-permute-start | bytes 196616 | tf_op jit(solution)/shard_map/ppermute | solution.py:183
  (15 other events, 61.2 us)

commit v5 on v4

--- a/solution.py
+++ b/solution.py
@@ -164,11 +164,16 @@
 
 
 def call(body, operands, outs, scratch=(), flops=0):
+    operands = operands[1:]
+    specs = [pl.BlockSpec(memory_space=pltpu.VMEM)] * len(operands)
+
     size = sum(x.size * x.dtype.itemsize for x in list(operands) + list(outs))
-    specs = [pl.BlockSpec(memory_space=pltpu.SMEM)]
-    specs += [pl.BlockSpec(memory_space=pltpu.VMEM)] * (len(operands) - 1)
+
+    def placed(*refs):
+        body((lax.axis_index("seq"), lax.axis_index("dp")), *refs)
+
     return pl.pallas_call(
-        body,
+        placed,
         out_shape=tuple(outs),
         in_specs=specs,
         out_specs=tuple(pl.BlockSpec(memory_space=pltpu.VMEM) for _ in outs),
@@ -243,7 +248,7 @@
     half = width // groups // 2
     scale = 1.0 / math.sqrt(groups * parts * rows)
     first, last, twiddle, fwd, inv = tables(outer)
-    place = jnp.stack([lax.axis_index("seq"), lax.axis_index("dp")]).astype(jnp.int32)
+    place = None
     block = jax.ShapeDtypeStruct((parts // 2, size, LANES), F32)
     spectrum = jax.ShapeDtypeStruct((chans * outer, 2 * LANES), F32)
     signal = pltpu.VMEM((width, rows), F32)

time: 92.6 us -> 88.2 us (0.952)
  Pallas kernels: 17.6 us -> 12.2 us
  waiting for transfers between devices: 25.6 us -> 26.7 us
    pallas_call x10, Pallas kernels: 17.6 us -> 12.2 us  [call(): pl.pallas_call(placed, out_shape=tuple(outs), in_specs=specs, out_specs=t...]
    ppermute x33, waiting for transfers between devices: 25.6 us -> 26.7 us  [mirror(): return lax.ppermute(x, axis, [(i, i ^ mask) for i in range(count)])]
  transfers between devices with their start and end apart: 34 -> 34, of which waited for: 12 -> 12; matrix products, arithmetic and copies ran while one was open for 1% -> 1% of each run, Pallas kernels for 12% -> 9%
where the time goes in v5:
time: 88.2 us; the launch traced here: 88 us
  starting transfers between devices  44.3 us (50%)
  waiting for transfers between devices  26.7 us (30%)
  Pallas kernels  12.2 us (14%)
  local copies, waits for them, and re-layouts  3.26 us (4%)
  between operations  1.1 us (1%)
    ppermute x33, starting transfers between devices, mirror(): return lax.ppermute(x, axis, [(i, i ^ mask) for i in range(count)])  40.9 us
    ppermute x33, waiting for transfers between devices, mirror(): return lax.ppermute(x, axis, [(i, i ^ mask) for i in range(count)])  26.7 us
    pallas_call x10, Pallas kernels, call(): pl.pallas_call(placed, out_shape=tuple(outs), in_specs=specs, out_specs=t...  12.2 us
    ppermute x1, starting transfers between devices, shards(): term_sum = lax.ppermute(term_sum, ('dp', 'seq'), swap)  3.36 us
    unnamed x26, local copies, waits for them, and re-layouts  3.05 us
  transfers between devices with their start and end apart: 34, of which 12 were waited for; matrix products, arithmetic and copies ran while one was open for 1% of the time, Pallas kernels for 9%

profile of v5, /device:TPU:3, one launch (start us, length us, event | category | flops | bytes accessed | tf_op | source)
XLA Modules:
  0.0 88.0 jit_solution(1468185623942198819)
XLA Ops:
  0.7 1.1 %copy-done.6 = f32[512,256]{1,0:T(8,128)S(1)} copy-done((f32[512,256]{1,0:T(8,128)S(1)}, f32[512,256]{1,0:T(8,128)}, u32[]{:S(2)}) %copy-start.6) | copy-done | bytes 524312
  6.0 1.5 %collective-permute-start.2 = (f32[2,128,128]{2,1,0:T(8,128)S(1)}, f32[2,128,128]{2,1,0:T(8,128)S(1)}, u32[]{:S(2)}, u32[]{:S(2)}) collective-permute-start(f32[2,128,128]{2,1,0:T(8,128)S(1)} %pad_maximum_fusion.2), channel_id=1, source_target_pairs={{0,4},{1,5},{2,6},{3,7},{4,0},{5,1},{6,2},{7,3},{8,12},{9,13},{10,... | collective-permute-start | bytes 393224 | tf_op jit(solution)/shard_map/ppermute | solution.py:188
  7.5 1.2 %collective-permute-start.3 = (f32[2,128,128]{2,1,0:T(8,128)S(1)}, f32[2,128,128]{2,1,0:T(8,128)S(1)}, u32[]{:S(2)}, u32[]{:S(2)}) collective-permute-start(f32[2,128,128]{2,1,0:T(8,128)S(1)} %pad_maximum_fusion.3), channel_id=1, source_target_pairs={{0,6},{1,7},{2,4},{3,5},{4,2},{5,3},{6,0},{7,1},{8,14},{9,15},{10,... | collective-permute-start | bytes 393224 | tf_op jit(solution)/shard_map/ppermute | solution.py:188
  9.0 1.5 %collective-permute-start.6 = (f32[2,128,128]{2,1,0:T(8,128)S(1)}, f32[2,128,128]{2,1,0:T(8,128)S(1)}, u32[]{:S(2)}, u32[]{:S(2)}) collective-permute-start(f32[2,128,128]{2,1,0:T(8,128)S(1)} %pad_maximum_fusion.5), channel_id=1, source_target_pairs={{0,4},{1,5},{2,6},{3,7},{4,0},{5,1},{6,2},{7,3},{8,12},{9,13},{10,... | collective-permute-start | bytes 393224 | tf_op jit(solution)/shard_map/ppermute | solution.py:188
  10.9 1.2 %collective-permute-start.7 = (f32[2,128,128]{2,1,0:T(8,128)S(1)}, f32[2,128,128]{2,1,0:T(8,128)S(1)}, u32[]{:S(2)}, u32[]{:S(2)}) collective-permute-start(f32[2,128,128]{2,1,0:T(8,128)S(1)} %pad_maximum_fusion.6), channel_id=1, source_target_pairs={{0,6},{1,7},{2,4},{3,5},{4,2},{5,3},{6,0},{7,1},{8,14},{9,15},{10,... | collective-permute-start | bytes 393224 | tf_op jit(solution)/shard_map/ppermute | solution.py:188
  12.2 1.3 %collective-permute-start.13 = (f32[2,128,128]{2,1,0:T(8,128)S(1)}, f32[2,128,128]{2,1,0:T(8,128)S(1)}, u32[]{:S(2)}, u32[]{:S(2)}) collective-permute-start(f32[2,128,128]{2,1,0:T(8,128)S(1)} %pad_maximum_fusion.10), channel_id=1, source_target_pairs={{0,2},{1,3},{2,0},{3,1},{4,6},{5,7},{6,4},{7,5},{8,10},{9,11},{10,... | collective-permute-start | bytes 393224 | tf_op jit(solution)/shard_map/ppermute | solution.py:188
  13.4 1.3 %collective-permute-done.3.refs_7_ = f32[2,128,128]{2,1,0:T(8,128)S(1)} collective-permute-done((f32[2,128,128]{2,1,0:T(8,128)S(1)}, f32[2,128,128]{2,1,0:T(8,128)S(1)}, u32[]{:S(2)}, u32[]{:S(2)}) %collective-permute-start.3) | collective-permute-done | bytes 131104 | tf_op jit(solution)/shard_map/ppermute | solution.py:188
  14.7 1.2 %collective-permute-start.14 = (f32[2,128,128]{2,1,0:T(8,128)S(1)}, f32[2,128,128]{2,1,0:T(8,128)S(1)}, u32[]{:S(2)}, u32[]{:S(2)}) collective-permute-start(f32[2,128,128]{2,1,0:T(8,128)S(1)} %pad_maximum_fusion.11), channel_id=1, source_target_pairs={{0,4},{1,5},{2,6},{3,7},{4,0},{5,1},{6,2},{7,3},{8,12},{9,13},{10,... | collective-permute-start | bytes 393224 | tf_op jit(solution)/shard_map/ppermute | solution.py:188
  17.5 1.0 %shard_map.155.refs_5_ = f32[1024,256]{1,0:T(8,128)S(1)} custom-call(bf16[64,96]{1,0:T(8,128)(2,1)S(1)} %copy-done.9, f32[2,32,128]{2,1,0:T(8,128)S(1)} %copy-done.8, bf16[2,256,256]{2,1,0:T(8,128)(2,1)S(1)} %copy-done.7, f32[4,128,128]{2,1,0:T(8,128)S(1)} %get-tuple-element.29.refs_3_, f32[4,128,128]{2,1,0:T(8,128)S(1)} %collective-permute-done.refs_4_, ...), custom_call_target="tpu_custom_call" | custom-call | flops 503316480 | bytes 2273280 | tf_op jit(solution)/shard_map/pallas_call | solution.py:175
  18.5 1.9 %collective-permute-done.7.refs_10_ = f32[2,128,128]{2,1,0:T(8,128)S(1)} collective-permute-done((f32[2,128,128]{2,1,0:T(8,128)S(1)}, f32[2,128,128]{2,1,0:T(8,128)S(1)}, u32[]{:S(2)}, u32[]{:S(2)}) %collective-permute-start.7) | collective-permute-done | bytes 131104 | tf_op jit(solution)/shard_map/ppermute | solution.py:188
  20.4 2.3 %shard_map.157 = (f32[1024,256]{1,0:T(8,128)S(1)}, f32[4,128,128]{2,1,0:T(8,128)S(1)}, f32[4,128,128]{2,1,0:T(8,128)S(1)}) custom-call(bf16[64,96]{1,0:T(8,128)(2,1)S(1)} %copy-done.9, bf16[32,192]{1,0:T(8,128)(2,1)S(1)} %copy-done.12, f32[2,32,128]{2,1,0:T(8,128)S(1)} %copy-done.8, bf16[2,256,256]{2,1,0:T(8,128)(2,1)S(1)} %copy-done.7, ...), custom_call_target="tpu_custom_call" | custom-call | flops 1006632960 | bytes 4120576 | tf_op jit(solution)/shard_map/pallas_call | solution.py:175
  22.7 3.3 %collective-permute-done.15.refs_11_ = f32[2,128,128]{2,1,0:T(8,128)S(1)} collective-permute-done((f32[2,128,128]{2,1,0:T(8,128)S(1)}, f32[2,128,128]{2,1,0:T(8,128)S(1)}, u32[]{:S(2)}, u32[]{:S(2)}) %collective-permute-start.15) | collective-permute-done | bytes 131104 | tf_op jit(solution)/shard_map/ppermute | solution.py:188
  26.0 3.5 %shard_map.160 = (f32[4,128,128]{2,1,0:T(8,128)S(1)}, f32[4,128,128]{2,1,0:T(8,128)S(1)}, f32[4,256,128]{2,1,0:T(8,128)S(1)}) custom-call(bf16[64,96]{1,0:T(8,128)(2,1)S(1)} %copy-done.9, bf16[32,192]{1,0:T(8,128)(2,1)S(1)} %copy-done.12, f32[2,32,128]{2,1,0:T(8,128)S(1)} %copy-done.8, bf16[2,256,256]{2,1,0:T(8,128)(2,1)S(1)} %copy-done.7, ...), custom_call_target="tpu_custom_call" | custom-call | flops 1509949440 | bytes 4644864 | tf_op jit(solution)/shard_map/pallas_call | solution.py:175
  29.5 1.0 %collective-permute-start.16 = (f32[4,128,128]{2,1,0:T(8,128)S(1)}, f32[4,128,128]{2,1,0:T(8,128)S(1)}, u32[]{:S(2)}, u32[]{:S(2)}) collective-permute-start(f32[4,128,128]{2,1,0:T(8,128)S(1)} %get-tuple-element.41), channel_id=1, source_target_pairs={{0,1},{1,0},{2,3},{3,2},{4,5},{5,4},{6,7},{7,6},{8,9},{9,8},{10,11... | collective-permute-start | bytes 786440 | tf_op jit(solution)/shard_map/ppermute | solution.py:188
  30.6 1.4 %collective-permute-start.30 = (f32[2,256,128]{2,1,0:T(8,128)S(1)}, f32[2,256,128]{2,1,0:T(8,128)S(1)}, u32[]{:S(2)}, u32[]{:S(2)}) collective-permute-start(f32[2,256,128]{2,1,0:T(8,128)S(1)} %slice.169), channel_id=1, source_target_pairs={{0,8},{8,0},{16,24},{24,16},{1,9},{9,1},{17,25},{25,17},{2,10},{10... | collective-permute-start | bytes 786440 | tf_op jit(solution)/shard_map/ppermute | solution.py:188
  32.9 1.3 %collective-permute-start.18 = (f32[2,128,128]{2,1,0:T(8,128)S(1)}, f32[2,128,128]{2,1,0:T(8,128)S(1)}, u32[]{:S(2)}, u32[]{:S(2)}) collective-permute-start(f32[2,128,128]{2,1,0:T(8,128)S(1)} %pad_maximum_fusion.14), channel_id=1, source_target_pairs={{0,4},{1,5},{2,6},{3,7},{4,0},{5,1},{6,2},{7,3},{8,12},{9,13},{10,... | collective-permute-start | bytes 393224 | tf_op jit(solution)/shard_map/ppermute | solution.py:188
  35.8 1.4 %collective-permute-done.17.refs_7_ = f32[2,128,128]{2,1,0:T(8,128)S(1)} collective-permute-done((f32[2,128,128]{2,1,0:T(8,128)S(1)}, f32[2,128,128]{2,1,0:T(8,128)S(1)}, u32[]{:S(2)}, u32[]{:S(2)}) %collective-permute-start.17) | collective-permute-done | bytes 131104 | tf_op jit(solution)/shard_map/ppermute | solution.py:188
  37.7 2.3 %collective-permute-done.19.refs_9_ = f32[2,128,128]{2,1,0:T(8,128)S(1)} collective-permute-done((f32[2,128,128]{2,1,0:T(8,128)S(1)}, f32[2,128,128]{2,1,0:T(8,128)S(1)}, u32[]{:S(2)}, u32[]{:S(2)}) %collective-permute-start.19) | collective-permute-done | bytes 131104 | tf_op jit(solution)/shard_map/ppermute | solution.py:188
  40.9 2.4 %collective-permute-start.23 = (f32[4,32,512]{2,1,0:T(8,128)S(1)}, f32[4,32,512]{2,1,0:T(8,128)S(1)}, u32[]{:S(2)}, u32[]{:S(2)}) collective-permute-start(f32[4,32,512]{2,1,0:T(8,128)S(1)} %get-tuple-element.46), channel_id=1, source_target_pairs={{0,1},{1,0},{2,3},{3,2},{4,5},{5,4},{6,7},{7,6},{8,9},{9,8},{10,11... | collective-permute-start | bytes 786440 | tf_op jit(solution)/shard_map/ppermute | solution.py:188
  44.3 5.0 %collective-permute-done.11.refs_9_ = f32[2,128,128]{2,1,0:T(8,128)S(1)} collective-permute-done((f32[2,128,128]{2,1,0:T(8,128)S(1)}, f32[2,128,128]{2,1,0:T(8,128)S(1)}, u32[]{:S(2)}, u32[]{:S(2)}) %collective-permute-start.11) | collective-permute-done | bytes 131104 | tf_op jit(solution)/shard_map/ppermute | solution.py:188
  52.2 2.4 %collective-permute-start.31 = (f32[1,256,128]{2,1,0:T(8,128)S(1)}, f32[1,256,128]{2,1,0:T(8,128)S(1)}, u32[]{:S(2)}, u32[]{:S(2)}) collective-permute-start(f32[1,256,128]{2,1,0:T(8,128)S(1)} %slice.197), channel_id=1, source_target_pairs={{0,16},{8,24},{16,0},{24,8},{1,17},{9,25},{17,1},{25,9},{2,18},{10... | collective-permute-start | bytes 393224 | tf_op jit(solution)/shard_map/ppermute | solution.py:188
  55.3 3.8 %collective-permute-done.24 = f32[2,32,512]{2,1,0:T(8,128)S(1)} collective-permute-done((f32[2,32,512]{2,1,0:T(8,128)S(1)}, f32[2,32,512]{2,1,0:T(8,128)S(1)}, u32[]{:S(2)}, u32[]{:S(2)}) %collective-permute-start.24) | collective-permute-done | bytes 131104 | tf_op jit(solution)/shard_map/ppermute | solution.py:188
  59.2 3.4 %collective-permute-done.21 = f32[2,32,640]{2,1,0:T(8,128)S(1)} collective-permute-done((f32[2,32,640]{2,1,0:T(8,128)S(1)}, f32[2,32,640]{2,1,0:T(8,128)S(1)}, u32[]{:S(2)}, u32[]{:S(2)}) %collective-permute-start.21) | collective-permute-done | bytes 163872 | tf_op jit(solution)/shard_map/ppermute | solution.py:188
  62.7 2.4 %collective-permute-start.22 = (f32[1,32,640]{2,1,0:T(8,128)S(1)}, f32[1,32,640]{2,1,0:T(8,128)S(1)}, u32[]{:S(2)}, u32[]{:S(2)}) collective-permute-start(f32[1,32,640]{2,1,0:T(8,128)S(1)} %slice.191), channel_id=1, source_target_pairs={{0,16},{8,24},{16,0},{24,8},{1,17},{9,25},{17,1},{25,9},{2,18},{10... | collective-permute-start | bytes 245768 | tf_op jit(solution)/shard_map/ppermute | solution.py:188
  65.1 2.3 %collective-permute-done.22 = f32[1,32,640]{2,1,0:T(8,128)S(1)} collective-permute-done((f32[1,32,640]{2,1,0:T(8,128)S(1)}, f32[1,32,640]{2,1,0:T(8,128)S(1)}, u32[]{:S(2)}, u32[]{:S(2)}) %collective-permute-start.22) | collective-permute-done | bytes 81952 | tf_op jit(solution)/shard_map/ppermute | solution.py:188
  67.4 1.2 %collective-permute-start.27 = (f32[32,1152]{1,0:T(8,128)S(1)}, f32[32,1152]{1,0:T(8,128)S(1)}, u32[]{:S(2)}, u32[]{:S(2)}) collective-permute-start(f32[32,1152]{1,0:T(8,128)S(1)} %pad_maximum_fusion), channel_id=1, source_target_pairs={{0,4},{1,5},{2,6},{3,7},{4,0},{5,1},{6,2},{7,3},{8,12},{9,13},{10,... | collective-permute-start | bytes 442376 | tf_op jit(solution)/shard_map/ppermute | solution.py:188
  68.5 1.0 %collective-permute-start.28 = (f32[32,1152]{1,0:T(8,128)S(1)}, f32[32,1152]{1,0:T(8,128)S(1)}, u32[]{:S(2)}, u32[]{:S(2)}) collective-permute-start(f32[32,1152]{1,0:T(8,128)S(1)} %pad_maximum_fusion), channel_id=1, source_target_pairs={{0,6},{1,7},{2,4},{3,5},{4,2},{5,3},{6,0},{7,1},{8,14},{9,15},{10,... | collective-permute-start | bytes 442376 | tf_op jit(solution)/shard_map/ppermute | solution.py:188
  70.1 3.4 %collective-permute-start.32 = (f32[256,128]{1,0:T(8,128)S(1)}, f32[256,128]{1,0:T(8,128)S(1)}, u32[]{:S(2)}, u32[]{:S(2)}) collective-permute-start(f32[256,128]{1,0:T(8,128)S(1)} %fusion), channel_id=1, source_target_pairs={{0,0},{1,1},{2,10},{3,11},{4,20},{5,21},{6,30},{7,31},{8,2},{9,3},... | collective-permute-start | bytes 393224 | tf_op jit(solution)/shard_map/ppermute | solution.py:434
  73.5 1.0 %collective-permute-done.26 = f32[32,1152]{1,0:T(8,128)S(1)} collective-permute-done((f32[32,1152]{1,0:T(8,128)S(1)}, f32[32,1152]{1,0:T(8,128)S(1)}, u32[]{:S(2)}, u32[]{:S(2)}) %collective-permute-start.26) | collective-permute-done | bytes 147488 | tf_op jit(solution)/shard_map/ppermute | solution.py:188
  74.6 8.2 %collective-permute-start.29 = (f32[32,1152]{1,0:T(8,128)S(1)}, f32[32,1152]{1,0:T(8,128)S(1)}, u32[]{:S(2)}, u32[]{:S(2)}) collective-permute-start(f32[32,1152]{1,0:T(8,128)S(1)} %add_add_fusion.refs_0_), channel_id=1, source_target_pairs={{0,1},{1,0},{2,3},{3,2},{4,5},{5,4},{6,7},{7,6},{8,9},{9,8},{10,11... | collective-permute-start | bytes 442376 | tf_op jit(solution)/shard_map/ppermute | solution.py:188
  82.8 2.3 %collective-permute-start.33 = (f32[128,128]{1,0:T(8,128)S(1)}, f32[128,128]{1,0:T(8,128)S(1)}, u32[]{:S(2)}, u32[]{:S(2)}) collective-permute-start(f32[128,128]{1,0:T(8,128)S(1)} %slice.198), channel_id=1, source_target_pairs={{0,1},{1,0},{2,3},{3,2},{4,5},{5,4},{6,7},{7,6},{8,9},{9,8},{10,11... | collective-permute-start | bytes 196616 | tf_op jit(solution)/shard_map/ppermute | solution.py:188
  86.1 1.1 %shard_map.162 = bf16[512,256]{1,0:T(8,128)(2,1)} custom-call(bf16[256,768]{1,0:T(8,128)(2,1)S(1)} %copy-done, bf16[256,512]{1,0:T(8,128)(2,1)S(1)} %get-tuple-element.36.refs_1_, bf16[512,512]{1,0:T(8,128)(2,1)S(1)} %get-tuple-element.42.refs_2_), custom_call_target="tpu_custom_call" | custom-call | flops 201326592 | bytes 1441792 | tf_op jit(solution)/shard_map/pallas_call | solution.py:175
  (114 shorter events, 17.5 us)
Async XLA Ops:
  2.0 3.8 %collective-permute-start = (f32[4,128,128]{2,1,0:T(8,128)S(1)}, f32[4,128,128]{2,1,0:T(8,128)S(1)}, u32[]{:S(2)}, u32[]{:S(2)}) collective-permute-start(f32[4,128,128]{2,1,0:T(8,128)S(1)} %get-tuple-element.30), channel_id=1, source_target_pairs={{0,1},{1,0},{2,3},{3,2},{4,5},{5,4},{6,7},{7,6},{8,9},{9,8},{10,11... | collective-permute-start | bytes 786440 | tf_op jit(solution)/shard_map/ppermute | solution.py:188
  5.2 3.6 %collective-permute-start.4 = (f32[4,128,128]{2,1,0:T(8,128)S(1)}, f32[4,128,128]{2,1,0:T(8,128)S(1)}, u32[]{:S(2)}, u32[]{:S(2)}) collective-permute-start(f32[4,128,128]{2,1,0:T(8,128)S(1)} %get-tuple-element.32), channel_id=1, source_target_pairs={{0,1},{1,0},{2,3},{3,2},{4,5},{5,4},{6,7},{7,6},{8,9},{9,8},{10,11... | collective-permute-start | bytes 786440 | tf_op jit(solution)/shard_map/ppermute | solution.py:188
  5.3 3.7 %collective-permute-start.12 = (f32[4,128,128]{2,1,0:T(8,128)S(1)}, f32[4,128,128]{2,1,0:T(8,128)S(1)}, u32[]{:S(2)}, u32[]{:S(2)}) collective-permute-start(f32[4,128,128]{2,1,0:T(8,128)S(1)} %get-tuple-element.39), channel_id=1, source_target_pairs={{0,1},{1,0},{2,3},{3,2},{4,5},{5,4},{6,7},{7,6},{8,9},{9,8},{10,11... | collective-permute-start | bytes 786440 | tf_op jit(solution)/shard_map/ppermute | solution.py:188
  5.9 5.0 %collective-permute-start.1 = (f32[2,128,128]{2,1,0:T(8,128)S(1)}, f32[2,128,128]{2,1,0:T(8,128)S(1)}, u32[]{:S(2)}, u32[]{:S(2)}) collective-permute-start(f32[2,128,128]{2,1,0:T(8,128)S(1)} %pad_maximum_fusion.1), channel_id=1, source_target_pairs={{0,2},{1,3},{2,0},{3,1},{4,6},{5,7},{6,4},{7,5},{8,10},{9,11},{10,... | collective-permute-start | bytes 393224 | tf_op jit(solution)/shard_map/ppermute | solution.py:188
  6.0 6.2 %collective-permute-start.2 = (f32[2,128,128]{2,1,0:T(8,128)S(1)}, f32[2,128,128]{2,1,0:T(8,128)S(1)}, u32[]{:S(2)}, u32[]{:S(2)}) collective-permute-start(f32[2,128,128]{2,1,0:T(8,128)S(1)} %pad_maximum_fusion.2), channel_id=1, source_target_pairs={{0,4},{1,5},{2,6},{3,7},{4,0},{5,1},{6,2},{7,3},{8,12},{9,13},{10,... | collective-permute-start | bytes 393224 | tf_op jit(solution)/shard_map/ppermute | solution.py:188
  7.5 7.2 %collective-permute-start.3 = (f32[2,128,128]{2,1,0:T(8,128)S(1)}, f32[2,128,128]{2,1,0:T(8,128)S(1)}, u32[]{:S(2)}, u32[]{:S(2)}) collective-permute-start(f32[2,128,128]{2,1,0:T(8,128)S(1)} %pad_maximum_fusion.3), channel_id=1, source_target_pairs={{0,6},{1,7},{2,4},{3,5},{4,2},{5,3},{6,0},{7,1},{8,14},{9,15},{10,... | collective-permute-start | bytes 393224 | tf_op jit(solution)/shard_map/ppermute | solution.py:188
  8.8 7.8 %collective-permute-start.5 = (f32[2,128,128]{2,1,0:T(8,128)S(1)}, f32[2,128,128]{2,1,0:T(8,128)S(1)}, u32[]{:S(2)}, u32[]{:S(2)}) collective-permute-start(f32[2,128,128]{2,1,0:T(8,128)S(1)} %pad_maximum_fusion.4), channel_id=1, source_target_pairs={{0,2},{1,3},{2,0},{3,1},{4,6},{5,7},{6,4},{7,5},{8,10},{9,11},{10,... | collective-permute-start | bytes 393224 | tf_op jit(solution)/shard_map/ppermute | solution.py:188
  9.0 9.5 %collective-permute-start.6 = (f32[2,128,128]{2,1,0:T(8,128)S(1)}, f32[2,128,128]{2,1,0:T(8,128)S(1)}, u32[]{:S(2)}, u32[]{:S(2)}) collective-permute-start(f32[2,128,128]{2,1,0:T(8,128)S(1)} %pad_maximum_fusion.5), channel_id=1, source_target_pairs={{0,4},{1,5},{2,6},{3,7},{4,0},{5,1},{6,2},{7,3},{8,12},{9,13},{10,... | collective-permute-start | bytes 393224 | tf_op jit(solution)/shard_map/ppermute | solution.py:188
  10.9 9.5 %collective-permute-start.7 = (f32[2,128,128]{2,1,0:T(8,128)S(1)}, f32[2,128,128]{2,1,0:T(8,128)S(1)}, u32[]{:S(2)}, u32[]{:S(2)}) collective-permute-start(f32[2,128,128]{2,1,0:T(8,128)S(1)} %pad_maximum_fusion.6), channel_id=1, source_target_pairs={{0,6},{1,7},{2,4},{3,5},{4,2},{5,3},{6,0},{7,1},{8,14},{9,15},{10,... | collective-permute-start | bytes 393224 | tf_op jit(solution)/shard_map/ppermute | solution.py:188
  12.2 10.6 %collective-permute-start.13 = (f32[2,128,128]{2,1,0:T(8,128)S(1)}, f32[2,128,128]{2,1,0:T(8,128)S(1)}, u32[]{:S(2)}, u32[]{:S(2)}) collective-permute-start(f32[2,128,128]{2,1,0:T(8,128)S(1)} %pad_maximum_fusion.10), channel_id=1, source_target_pairs={{0,2},{1,3},{2,0},{3,1},{4,6},{5,7},{6,4},{7,5},{8,10},{9,11},{10,... | collective-permute-start | bytes 393224 | tf_op jit(solution)/shard_map/ppermute | solution.py:188
  14.7 8.0 %collective-permute-start.14 = (f32[2,128,128]{2,1,0:T(8,128)S(1)}, f32[2,128,128]{2,1,0:T(8,128)S(1)}, u32[]{:S(2)}, u32[]{:S(2)}) collective-permute-start(f32[2,128,128]{2,1,0:T(8,128)S(1)} %pad_maximum_fusion.11), channel_id=1, source_target_pairs={{0,4},{1,5},{2,6},{3,7},{4,0},{5,1},{6,2},{7,3},{8,12},{9,13},{10,... | collective-permute-start | bytes 393224 | tf_op jit(solution)/shard_map/ppermute | solution.py:188
  16.6 9.4 %collective-permute-start.15 = (f32[2,128,128]{2,1,0:T(8,128)S(1)}, f32[2,128,128]{2,1,0:T(8,128)S(1)}, u32[]{:S(2)}, u32[]{:S(2)}) collective-permute-start(f32[2,128,128]{2,1,0:T(8,128)S(1)} %pad_maximum_fusion.12), channel_id=1, source_target_pairs={{0,6},{1,7},{2,4},{3,5},{4,2},{5,3},{6,0},{7,1},{8,14},{9,15},{10,... | collective-permute-start | bytes 393224 | tf_op jit(solution)/shard_map/ppermute | solution.py:188
  30.6 21.6 %collective-permute-start.30 = (f32[2,256,128]{2,1,0:T(8,128)S(1)}, f32[2,256,128]{2,1,0:T(8,128)S(1)}, u32[]{:S(2)}, u32[]{:S(2)}) collective-permute-start(f32[2,256,128]{2,1,0:T(8,128)S(1)} %slice.169), channel_id=1, source_target_pairs={{0,8},{8,0},{16,24},{24,16},{1,9},{9,1},{17,25},{25,17},{2,10},{10... | collective-permute-start | bytes 786440 | tf_op jit(solution)/shard_map/ppermute | solution.py:188
  32.3 4.9 %collective-permute-start.17 = (f32[2,128,128]{2,1,0:T(8,128)S(1)}, f32[2,128,128]{2,1,0:T(8,128)S(1)}, u32[]{:S(2)}, u32[]{:S(2)}) collective-permute-start(f32[2,128,128]{2,1,0:T(8,128)S(1)} %pad_maximum_fusion.13), channel_id=1, source_target_pairs={{0,2},{1,3},{2,0},{3,1},{4,6},{5,7},{6,4},{7,5},{8,10},{9,11},{10,... | collective-permute-start | bytes 393224 | tf_op jit(solution)/shard_map/ppermute | solution.py:188
  32.9 4.9 %collective-permute-start.18 = (f32[2,128,128]{2,1,0:T(8,128)S(1)}, f32[2,128,128]{2,1,0:T(8,128)S(1)}, u32[]{:S(2)}, u32[]{:S(2)}) collective-permute-start(f32[2,128,128]{2,1,0:T(8,128)S(1)} %pad_maximum_fusion.14), channel_id=1, source_target_pairs={{0,4},{1,5},{2,6},{3,7},{4,0},{5,1},{6,2},{7,3},{8,12},{9,13},{10,... | collective-permute-start | bytes 393224 | tf_op jit(solution)/shard_map/ppermute | solution.py:188
  34.2 5.8 %collective-permute-start.19 = (f32[2,128,128]{2,1,0:T(8,128)S(1)}, f32[2,128,128]{2,1,0:T(8,128)S(1)}, u32[]{:S(2)}, u32[]{:S(2)}) collective-permute-start(f32[2,128,128]{2,1,0:T(8,128)S(1)} %pad_maximum_fusion.15), channel_id=1, source_target_pairs={{0,6},{1,7},{2,4},{3,5},{4,2},{5,3},{6,0},{7,1},{8,14},{9,15},{10,... | collective-permute-start | bytes 393224 | tf_op jit(solution)/shard_map/ppermute | solution.py:188
  35.2 9.0 %collective-permute-start.9 = (f32[2,128,128]{2,1,0:T(8,128)S(1)}, f32[2,128,128]{2,1,0:T(8,128)S(1)}, u32[]{:S(2)}, u32[]{:S(2)}) collective-permute-start(f32[2,128,128]{2,1,0:T(8,128)S(1)} %pad_maximum_fusion.7), channel_id=1, source_target_pairs={{0,2},{1,3},{2,0},{3,1},{4,6},{5,7},{6,4},{7,5},{8,10},{9,11},{10,... | collective-permute-start | bytes 393224 | tf_op jit(solution)/shard_map/ppermute | solution.py:188
  37.2 7.1 %collective-permute-start.10 = (f32[2,128,128]{2,1,0:T(8,128)S(1)}, f32[2,128,128]{2,1,0:T(8,128)S(1)}, u32[]{:S(2)}, u32[]{:S(2)}) collective-permute-start(f32[2,128,128]{2,1,0:T(8,128)S(1)} %pad_maximum_fusion.8), channel_id=1, source_target_pairs={{0,4},{1,5},{2,6},{3,7},{4,0},{5,1},{6,2},{7,3},{8,12},{9,13},{10,... | collective-permute-start | bytes 393224 | tf_op jit(solution)/shard_map/ppermute | solution.py:188
  40.9 10.3 %collective-permute-start.23 = (f32[4,32,512]{2,1,0:T(8,128)S(1)}, f32[4,32,512]{2,1,0:T(8,128)S(1)}, u32[]{:S(2)}, u32[]{:S(2)}) collective-permute-start(f32[4,32,512]{2,1,0:T(8,128)S(1)} %get-tuple-element.46), channel_id=1, source_target_pairs={{0,1},{1,0},{2,3},{3,2},{4,5},{5,4},{6,7},{7,6},{8,9},{9,8},{10,11... | collective-permute-start | bytes 786440 | tf_op jit(solution)/shard_map/ppermute | solution.py:188
  43.3 6.0 %collective-permute-start.11 = (f32[2,128,128]{2,1,0:T(8,128)S(1)}, f32[2,128,128]{2,1,0:T(8,128)S(1)}, u32[]{:S(2)}, u32[]{:S(2)}) collective-permute-start(f32[2,128,128]{2,1,0:T(8,128)S(1)} %pad_maximum_fusion.9), channel_id=1, source_target_pairs={{0,6},{1,7},{2,4},{3,5},{4,2},{5,3},{6,0},{7,1},{8,14},{9,15},{10,... | collective-permute-start | bytes 393224 | tf_op jit(solution)/shard_map/ppermute | solution.py:188
  50.2 4.4 %collective-permute-start.20 = (f32[4,32,640]{2,1,0:T(8,128)S(1)}, f32[4,32,640]{2,1,0:T(8,128)S(1)}, u32[]{:S(2)}, u32[]{:S(2)}) collective-permute-start(f32[4,32,640]{2,1,0:T(8,128)S(1)} %get-tuple-element.44), channel_id=1, source_target_pairs={{0,1},{1,0},{2,3},{3,2},{4,5},{5,4},{6,7},{7,6},{8,9},{9,8},{10,11... | collective-permute-start | bytes 983048 | tf_op jit(solution)/shard_map/ppermute | solution.py:188
  51.2 7.9 %collective-permute-start.24 = (f32[2,32,512]{2,1,0:T(8,128)S(1)}, f32[2,32,512]{2,1,0:T(8,128)S(1)}, u32[]{:S(2)}, u32[]{:S(2)}) collective-permute-start(f32[2,32,512]{2,1,0:T(8,128)S(1)} %slice.193), channel_id=1, source_target_pairs={{0,8},{8,0},{16,24},{24,16},{1,9},{9,1},{17,25},{25,17},{2,10},{10... | collective-permute-start | bytes 393224 | tf_op jit(solution)/shard_map/ppermute | solution.py:188
  52.2 17.9 %collective-permute-start.31 = (f32[1,256,128]{2,1,0:T(8,128)S(1)}, f32[1,256,128]{2,1,0:T(8,128)S(1)}, u32[]{:S(2)}, u32[]{:S(2)}) collective-permute-start(f32[1,256,128]{2,1,0:T(8,128)S(1)} %slice.197), channel_id=1, source_target_pairs={{0,16},{8,24},{16,0},{24,8},{1,17},{9,25},{17,1},{25,9},{2,18},{10... | collective-permute-start | bytes 393224 | tf_op jit(solution)/shard_map/ppermute | solution.py:188
  54.6 8.0 %collective-permute-start.21 = (f32[2,32,640]{2,1,0:T(8,128)S(1)}, f32[2,32,640]{2,1,0:T(8,128)S(1)}, u32[]{:S(2)}, u32[]{:S(2)}) collective-permute-start(f32[2,32,640]{2,1,0:T(8,128)S(1)} %slice.189), channel_id=1, source_target_pairs={{0,8},{8,0},{16,24},{24,16},{1,9},{9,1},{17,25},{25,17},{2,10},{10... | collective-permute-start | bytes 491528 | tf_op jit(solution)/shard_map/ppermute | solution.py:188
  59.1 5.9 %collective-permute-start.25 = (f32[1,32,512]{2,1,0:T(8,128)S(1)}, f32[1,32,512]{2,1,0:T(8,128)S(1)}, u32[]{:S(2)}, u32[]{:S(2)}) collective-permute-start(f32[1,32,512]{2,1,0:T(8,128)S(1)} %slice.195), channel_id=1, source_target_pairs={{0,16},{8,24},{16,0},{24,8},{1,17},{9,25},{17,1},{25,9},{2,18},{10... | collective-permute-start | bytes 196616 | tf_op jit(solution)/shard_map/ppermute | solution.py:188
  62.7 4.7 %collective-permute-start.22 = (f32[1,32,640]{2,1,0:T(8,128)S(1)}, f32[1,32,640]{2,1,0:T(8,128)S(1)}, u32[]{:S(2)}, u32[]{:S(2)}) collective-permute-start(f32[1,32,640]{2,1,0:T(8,128)S(1)} %slice.191), channel_id=1, source_target_pairs={{0,16},{8,24},{16,0},{24,8},{1,17},{9,25},{17,1},{25,9},{2,18},{10... | collective-permute-start | bytes 245768 | tf_op jit(solution)/shard_map/ppermute | solution.py:188
  67.4 6.1 %collective-permute-start.27 = (f32[32,1152]{1,0:T(8,128)S(1)}, f32[32,1152]{1,0:T(8,128)S(1)}, u32[]{:S(2)}, u32[]{:S(2)}) collective-permute-start(f32[32,1152]{1,0:T(8,128)S(1)} %pad_maximum_fusion), channel_id=1, source_target_pairs={{0,4},{1,5},{2,6},{3,7},{4,0},{5,1},{6,2},{7,3},{8,12},{9,13},{10,... | collective-permute-start | bytes 442376 | tf_op jit(solution)/shard_map/ppermute | solution.py:188
  68.5 4.9 %collective-permute-start.28 = (f32[32,1152]{1,0:T(8,128)S(1)}, f32[32,1152]{1,0:T(8,128)S(1)}, u32[]{:S(2)}, u32[]{:S(2)}) collective-permute-start(f32[32,1152]{1,0:T(8,128)S(1)} %pad_maximum_fusion), channel_id=1, source_target_pairs={{0,6},{1,7},{2,4},{3,5},{4,2},{5,3},{6,0},{7,1},{8,14},{9,15},{10,... | collective-permute-start | bytes 442376 | tf_op jit(solution)/shard_map/ppermute | solution.py:188
  69.5 5.0 %collective-permute-start.26 = (f32[32,1152]{1,0:T(8,128)S(1)}, f32[32,1152]{1,0:T(8,128)S(1)}, u32[]{:S(2)}, u32[]{:S(2)}) collective-permute-start(f32[32,1152]{1,0:T(8,128)S(1)} %pad_maximum_fusion), channel_id=1, source_target_pairs={{0,2},{1,3},{2,0},{3,1},{4,6},{5,7},{6,4},{7,5},{8,10},{9,11},{10,... | collective-permute-start | bytes 442376 | tf_op jit(solution)/shard_map/ppermute | solution.py:188
  70.1 12.7 %collective-permute-start.32 = (f32[256,128]{1,0:T(8,128)S(1)}, f32[256,128]{1,0:T(8,128)S(1)}, u32[]{:S(2)}, u32[]{:S(2)}) collective-permute-start(f32[256,128]{1,0:T(8,128)S(1)} %fusion), channel_id=1, source_target_pairs={{0,0},{1,1},{2,10},{3,11},{4,20},{5,21},{6,30},{7,31},{8,2},{9,3},... | collective-permute-start | bytes 393224 | tf_op jit(solution)/shard_map/ppermute | solution.py:434
  74.6 12.6 %collective-permute-start.29 = (f32[32,1152]{1,0:T(8,128)S(1)}, f32[32,1152]{1,0:T(8,128)S(1)}, u32[]{:S(2)}, u32[]{:S(2)}) collective-permute-start(f32[32,1152]{1,0:T(8,128)S(1)} %add_add_fusion.refs_0_), channel_id=1, source_target_pairs={{0,1},{1,0},{2,3},{3,2},{4,5},{5,4},{6,7},{7,6},{8,9},{9,8},{10,11... | collective-permute-start | bytes 442376 | tf_op jit(solution)/shard_map/ppermute | solution.py:188
  82.8 4.4 %collective-permute-start.33 = (f32[128,128]{1,0:T(8,128)S(1)}, f32[128,128]{1,0:T(8,128)S(1)}, u32[]{:S(2)}, u32[]{:S(2)}) collective-permute-start(f32[128,128]{1,0:T(8,128)S(1)} %slice.198), channel_id=1, source_target_pairs={{0,1},{1,0},{2,3},{3,2},{4,5},{5,4},{6,7},{7,6},{8,9},{9,8},{10,11... | collective-permute-start | bytes 196616 | tf_op jit(solution)/shard_map/ppermute | solution.py:188
  (15 other events, 61.2 us)
